TPU v7x, 32 devices: a whole 2x2x4 slice. The times are simulated.
32 devices in a mesh: grp: 2 (over x), hist: 16 (over z, y, core).
Axes of the slice: x: 2, y: 2, z: 4, core: 2. Of those that a mesh axis runs over, the one named last changes fastest.
Arguments:
- item_ids: int32 [512], P(('grp', 'hist')), parts along dimension 0, may hold values from 0 to 16383
- item_table: bfloat16 [16384, 1024], P('hist'), may hold values from -6 to 6
- key_cache: bfloat16 [32768, 1024], P(('grp', 'hist')), parts along dimension 0, may hold values from -6 to 6
- value_cache: bfloat16 [32768, 1024], P(('grp', 'hist')), parts along dimension 0, may hold values from -6 to 6
- time_buckets: int32 [32768], P(('grp', 'hist')), parts along dimension 0, may hold values from 0 to 127
- window_start: int32 [2], P('grp'), parts along dimension 0, may hold values from 0 to 16384
- norm_gain: float32 [1024], replicated, may hold values from 0.25 to 1.75
- proj_in: bfloat16 [1024, 2048], replicated, may hold values from -0.1875 to 0.1875
- time_bias: float32 [16, 128], replicated, may hold values from -3 to 3
- pos_bias: float32 [16, 18], replicated, may hold values from -1 to 1
- out_gain: float32 [1024], replicated, may hold values from 0.25 to 1.75
- proj_out: bfloat16 [1024, 1024], replicated, may hold values from -0.1875 to 0.1875
Outputs:
- scored: bfloat16 [512, 1024], P(('grp', 'hist')), parts along dimension 0
There are 2 independent parts, one for each index of `grp`. A program takes and returns all parts, laid end to end along the dimension named above; an argument that names none is the same for every part. Nothing has to cross between parts.
All inputs are finite; a program needn't handle non-finite values.
Results may differ from a plain program's by a relative error of at most 0.0075.
Values may be sent and summed in bfloat16 or wider, within the bound.
No kernel may reach another device: no remote copies, remote signals or barrier semaphores. Data moves between devices by JAX's collectives and lax.ppermute only.
A program may use at most 128 MiB of HBM per device.

v0:
```python
import jax
import jax.numpy as jnp
from jax import lax
from jax.sharding import PartitionSpec as P

GROUP_HEADS = 4


def lookup_rows(indices, table):
    columns = jnp.arange(table.shape[1], dtype=jnp.int32)
    matches = indices[:, None, None] == columns[None, None, :]
    return jnp.sum(jnp.where(matches, table[None, :, :], 0.0), axis=2)


def on_device(
    item_ids,
    item_table,
    key_cache,
    value_cache,
    time_buckets,
    window_start,
    norm_gain,
    proj_in,
    time_bias,
    pos_bias,
    out_gain,
    proj_out,
):
    table_rows = item_table.shape[0]
    table_first = lax.axis_index("hist") * table_rows
    every_id = lax.all_gather(item_ids, "hist", axis=0, tiled=True)
    offsets = every_id - table_first
    owned = (offsets >= 0) & (offsets < table_rows)
    picked = jnp.take(item_table, jnp.clip(offsets, 0, table_rows - 1), axis=0)
    terms = jnp.where(owned[:, None], picked.astype(jnp.float32), 0.0)
    embedded = lax.psum_scatter(terms, "hist", scatter_dimension=0, tiled=True).astype(jnp.bfloat16)
    width = embedded.shape[1]
    heads = time_bias.shape[0]
    head_dim = width // heads
    xfloat = embedded.astype(jnp.float32)
    meansq = jnp.mean(xfloat * xfloat, axis=-1, keepdims=True)
    normed = (xfloat * lax.rsqrt(meansq + 1e-06) * norm_gain).astype(jnp.bfloat16)
    projected = jnp.dot(normed, proj_in, preferred_element_type=jnp.float32)
    queries = jax.nn.silu(projected[:, :width]).astype(jnp.bfloat16)
    gates = jax.nn.silu(projected[:, width:]).astype(jnp.bfloat16)
    events = key_cache.shape[0]
    positions = lax.axis_index("hist") * events + jnp.arange(events, dtype=jnp.int32)
    history = 2 * events * lax.axis_size("hist")
    distance = history - window_start[0] - positions
    npos = pos_bias.shape[1]
    thresholds = jnp.left_shift(
        jnp.ones((npos - 1,), jnp.int32), jnp.arange(1, npos, dtype=jnp.int32)
    )
    buckets = jnp.sum((distance[:, None] >= thresholds[None, :]).astype(jnp.int32), axis=1)
    event_bias = lookup_rows(time_buckets, time_bias) + lookup_rows(buckets, pos_bias)
    groups = heads // GROUP_HEADS
    bias_grouped = event_bias.T.reshape(groups, GROUP_HEADS, events)
    keys_grouped = key_cache.reshape(events, groups, GROUP_HEADS, head_dim).transpose(1, 0, 2, 3)
    values_grouped = value_cache.reshape(events, groups, GROUP_HEADS, head_dim).transpose(
        1, 0, 2, 3
    )
    scale = head_dim ** (-0.5)
    query_rows = lax.all_gather(queries, "hist", axis=0, tiled=True)
    count = query_rows.shape[0]
    query_grouped = query_rows.reshape(count, groups, GROUP_HEADS, head_dim).transpose(1, 0, 2, 3)

    def one_group(operands):
        query_part, key_part, value_part, bias_part = operands
        scores = (
            jnp.einsum("chd,jhd->chj", query_part, key_part, preferred_element_type=jnp.float32)
            * scale
            + bias_part[None]
        )
        weights = jax.nn.silu(scores).astype(jnp.bfloat16)
        return jnp.einsum("chj,jhd->chd", weights, value_part, preferred_element_type=jnp.float32)

    mixed = lax.map(one_group, (query_grouped, keys_grouped, values_grouped, bias_grouped))
    partial_all = mixed.transpose(1, 0, 2, 3).reshape(count, width)
    attended = lax.psum_scatter(partial_all, "hist", scatter_dimension=0, tiled=True)
    centred = attended - jnp.mean(attended, axis=-1, keepdims=True)
    variance = jnp.mean(centred * centred, axis=-1, keepdims=True)
    gated = (centred * lax.rsqrt(variance + 1e-05) * out_gain * gates.astype(jnp.float32)).astype(
        jnp.bfloat16
    )
    return (xfloat + jnp.dot(gated, proj_out, preferred_element_type=jnp.float32)).astype(
        jnp.bfloat16
    )


def solution(mesh):
    placed = (
        P(("grp", "hist")),
        P("hist", None),
        P(("grp", "hist"), None),
        P(("grp", "hist"), None),
        P(("grp", "hist")),
        P("grp"),
        P(),
        P(),
        P(),
        P(),
        P(),
        P(),
    )
    return jax.shard_map(
        on_device, mesh=mesh, in_specs=placed, out_specs=P(("grp", "hist"), None), check_vma=False
    )
```

profile of v0, /device:TPU:0, one launch (start us, length us, event | category | flops | bytes accessed | tf_op | source)
XLA Modules:
  0.0 189.7 jit_solution(7255389539281984132)
XLA Ops:
  6.5 0.0 copy-start
  6.5 0.0 reduce-scatter.3.cloned.1.call-start
  6.5 1.5 dynamic-slice
  8.7 0.9 dynamic-update-slice
  9.6 13.8 %all-reduce = s32[256]{0:T(256)S(1)} all-reduce(s32[256]{0:T(256)S(1)} %dynamic-update-slice), channel_id=1, replica_groups=mesh['grp'=2,'hist'=16] {'hist'}, use_global_device_ids=true, to_apply=%add | all-reduce | flops 256 | bytes 2048
  23.4 0.0 copy-done
  23.4 1.2 gather_fusion
  24.5 0.0 copy-start.2
  24.5 0.0 copy-start.5
  24.6 0.0 copy-start.3
  24.6 1.2 convert_select_fusion
  25.8 0.0 reduce-scatter.3.cloned.1.call-update
  25.8 0.0 reduce-scatter.5.cloned.1.call-start
  26.5 0.0 copy-done.2
  26.5 0.1 copy.35
  26.6 0.1 convert_reduce_fusion
  26.8 0.2 select_reduce_fusion.1
  26.9 0.2 copy.36
  27.1 0.0 copy-done.5
  27.2 0.2 iota_compare_fusion
  27.4 0.0 copy-done.3
  27.4 2.2 %select_reduce_fusion = f32[1024,16]{1,0:T(8,128)S(1)} fusion(f32[16,128]{1,0:T(8,128)S(1)} %copy-done.3, pred[1024,128]{1,0:T(8,128)(4,1)S(1)} %iota_compare_fusion), kind=kLoop, calls=%fused_computation.20 | loop fusion | flops 4177920 | bytes 204800 | tf_op jit(solution)/shard_map/reduce_sum | solution.py:12
  29.6 0.1 add_bitcast_fusion
  29.7 0.2 copy.37
  29.9 4.0 %copy.33 = bf16[1024,1024]{0,1:T(8,128)(2,1)} copy(bf16[1024,1024]{1,0:T(8,128)(2,1)} %param.16) | data formatting | bytes 4194304 | tf_op args[2]
  33.9 0.0 copy-start.6
  33.9 4.0 %copy.32 = bf16[1024,1024]{0,1:T(8,128)(2,1)} copy(bf16[1024,1024]{1,0:T(8,128)(2,1)} %param.17) | data formatting | bytes 4194304 | tf_op args[3]
  37.9 43.3 %reduce-scatter.3.cloned.1.call-done = f32[16,1024]{1,0:T(8,128)} async-done(((f32[256,1024]{1,0:T(8,128)}), f32[16,1024]{1,0:T(8,128)}) %reduce-scatter.3.cloned.1.call-update) | async-done | bytes 65552 | tf_op jit(solution)/shard_map/reduce_scatter | solution.py:36
  81.2 1.0 fusion.22
  82.2 0.0 copy-done.6
  82.2 2.9 %fusion.25 = f32[16,2048]{1,0:T(8,128)S(1)} fusion(bf16[1024,2048]{1,0:T(8,128)(2,1)} %param.21, f32[1024]{0:T(1024)S(1)} %copy-done.6, f32[16]{0:T(128)S(1)} %add_rsqrt_fusion.1, f32[16,1024]{1,0:T(8,128)} %reduce-scatter.3.cloned.1.call-done), kind=kOutput, calls=%fused_computation.38 | convolution fusion | flops 67190784 | bytes 4395072 | tf_op jit(solution)/shard_map/dot_general | solution.py:43
  85.1 20.8 %all_gather.7 = bf16[256,1024]{1,0:T(8,128)(2,1)S(1)} all-gather(bf16[16,1024]{1,0:T(8,128)(2,1)S(1)} %multiply_convert_fusion.2), channel_id=1, replica_groups=mesh['grp'=2,'hist'=16] {'hist'}, dimensions={0}, use_global_device_ids=true | all-gather | bytes 557056 | tf_op jit(solution)/shard_map/all_gather | solution.py:63
  105.9 0.2 copy.34
  106.1 14.5 %while.10 = (s32[]{:T(128)}, f32[4,256,4,64]{1,3,2,0:T(8,128)}, bf16[4,1024,4,64]{1,3,2,0:T(8,128)(2,1)}, bf16[4,1024,4,64]{1,3,2,0:T(8,128)(2,1)}, bf16[4,256,4...) while((s32[]{:T(128)}, f32[4,256,4,64]{1,3,2,0:T(8,128)}, ...), condition=%wide.region_6.7_spmd, body=%wide.region_5.6_spmd.sunk | while | flops 275775488 | bytes 1493073 | solution.py:77
  106.1 3.6 %fusion.44 = f32[4,256,4,64]{1,3,2,0:T(8,128)} fusion(f32[4,256,4,64]{1,3,2,0:T(8,128)} %get-tuple-element.104, s32[]{:T(128)} %get-tuple-element.103, f32[4,1024]{1,0:T(4,128)S(1)} %dynamic-slice_bitcast_fusion.2, bf16[4,1024,4,64]{1,3,2,0:T(8,128)(2,1)} %get-tuple-element.113, bf16[4,1024,4,64]{1,3,2,0:T(8,128)(2,1)} %get-tuple-element.112, ...), kind=kOutput, calls=%fused_computation.9.clone.1 | convolution fusion | flops 275775488 | bytes 1460224 | tf_op jit(solution)/shard_map/while/body/eval_jaxpr/chj,jhd->chd/dot_general | solution.py:75
  109.7 3.6 %fusion.44 = f32[4,256,4,64]{1,3,2,0:T(8,128)} fusion(f32[4,256,4,64]{1,3,2,0:T(8,128)} %get-tuple-element.104, s32[]{:T(128)} %get-tuple-element.103, f32[4,1024]{1,0:T(4,128)S(1)} %dynamic-slice_bitcast_fusion.2, bf16[4,1024,4,64]{1,3,2,0:T(8,128)(2,1)} %get-tuple-element.113, bf16[4,1024,4,64]{1,3,2,0:T(8,128)(2,1)} %get-tuple-element.112, ...), kind=kOutput, calls=%fused_computation.9.clone.1 | convolution fusion | flops 275775488 | bytes 1460224 | tf_op jit(solution)/shard_map/while/body/eval_jaxpr/chj,jhd->chd/dot_general | solution.py:75
  113.3 3.6 %fusion.44 = f32[4,256,4,64]{1,3,2,0:T(8,128)} fusion(f32[4,256,4,64]{1,3,2,0:T(8,128)} %get-tuple-element.104, s32[]{:T(128)} %get-tuple-element.103, f32[4,1024]{1,0:T(4,128)S(1)} %dynamic-slice_bitcast_fusion.2, bf16[4,1024,4,64]{1,3,2,0:T(8,128)(2,1)} %get-tuple-element.113, bf16[4,1024,4,64]{1,3,2,0:T(8,128)(2,1)} %get-tuple-element.112, ...), kind=kOutput, calls=%fused_computation.9.clone.1 | convolution fusion | flops 275775488 | bytes 1460224 | tf_op jit(solution)/shard_map/while/body/eval_jaxpr/chj,jhd->chd/dot_general | solution.py:75
  116.9 3.6 %fusion.44 = f32[4,256,4,64]{1,3,2,0:T(8,128)} fusion(f32[4,256,4,64]{1,3,2,0:T(8,128)} %get-tuple-element.104, s32[]{:T(128)} %get-tuple-element.103, f32[4,1024]{1,0:T(4,128)S(1)} %dynamic-slice_bitcast_fusion.2, bf16[4,1024,4,64]{1,3,2,0:T(8,128)(2,1)} %get-tuple-element.113, bf16[4,1024,4,64]{1,3,2,0:T(8,128)(2,1)} %get-tuple-element.112, ...), kind=kOutput, calls=%fused_computation.9.clone.1 | convolution fusion | flops 275775488 | bytes 1460224 | tf_op jit(solution)/shard_map/while/body/eval_jaxpr/chj,jhd->chd/dot_general | solution.py:75
  120.6 0.0 copy-start.1
  120.6 0.0 copy-start.4
  120.6 2.6 %copy.38 = f32[256,1024]{1,0:T(8,128)} copy(f32[256,1024]{0,1:T(8,128)} %bitcast.70) | data formatting | bytes 2097152 | tf_op jit(solution)/shard_map/reshape | solution.py:78
  123.2 0.0 reduce-scatter.5.cloned.1.call-update
  123.2 55.0 %reduce-scatter.5.cloned.1.call-done = f32[16,1024]{1,0:T(8,128)} async-done(((f32[256,1024]{1,0:T(8,128)}), f32[16,1024]{1,0:T(8,128)}) %reduce-scatter.5.cloned.1.call-update) | async-done | bytes 65552 | tf_op jit(solution)/shard_map/reduce_scatter | solution.py:79
  178.2 1.0 reduce_sum.58
  179.1 1.0 multiply_reduce_fusion
  180.2 0.0 copy-done.1
  180.2 0.0 copy-done.4
  180.2 2.7 %fusion.21 = bf16[16,1024]{1,0:T(8,128)(2,1)} fusion(bf16[1024,1024]{1,0:T(8,128)(2,1)} %param.25, f32[16,1024]{1,0:T(8,128)} %reduce-scatter.5.cloned.1.call-done, f32[16,2048]{1,0:T(8,128)S(1)} %fusion.25, f32[1024]{0:T(1024)S(1)} %copy-done.4, f32[16]{0:T(128)S(1)} %add_rsqrt_fusion, f32[16]{0:T(128)S(1)} %broadcast_multiply_fusion, ...), kind=kOutput, calls=%fused_computation.23 | convolution fusion | flops 33800192 | bytes 2331648 | tf_op jit(solution)/shard_map/dot_general | solution.py:85
  (16 shorter events, 0.1 us)
Async XLA Ops:
  6.5 16.8 %copy-start = (bf16[1024,1024]{1,0:T(8,128)(2,1)S(1)}, bf16[1024,1024]{1,0:T(8,128)(2,1)}, u32[]{:S(2)}) copy-start(bf16[1024,1024]{1,0:T(8,128)(2,1)} %param.15) | copy-start | bytes 6291460
  6.5 74.7 %reduce-scatter.3.cloned.1.call-start = ((), (), s32[]{:S(2)}) async-start(), calls=%async_computation.2 | async-start | bytes 1114112 | tf_op jit(solution)/shard_map/reduce_scatter | solution.py:36
  24.5 2.0 %copy-start.2 = (f32[16,18]{1,0:T(8,128)S(1)}, f32[16,18]{1,0:T(8,128)}, u32[]{:S(2)}) copy-start(f32[16,18]{1,0:T(8,128)} %param.23) | copy-start | bytes 3460
  24.5 2.6 %copy-start.5 = (s32[1024]{0:T(1024)S(1)}, s32[1024]{0:T(1024)}, u32[]{:S(2)}) copy-start(s32[1024]{0:T(1024)} %param.18) | copy-start | bytes 12292
  24.6 2.8 %copy-start.3 = (f32[16,128]{1,0:T(8,128)S(1)}, f32[16,128]{1,0:T(8,128)}, u32[]{:S(2)}) copy-start(f32[16,128]{1,0:T(8,128)} %param.22) | copy-start | bytes 24580
  25.8 152.3 %reduce-scatter.5.cloned.1.call-start = ((), (), s32[]{:S(2)}) async-start(), calls=%async_computation.3 | async-start | bytes 1114112 | tf_op jit(solution)/shard_map/reduce_scatter | solution.py:79
  33.9 48.3 %copy-start.6 = (f32[1024]{0:T(1024)S(1)}, f32[1024]{0:T(1024)}, u32[]{:S(2)}) copy-start(f32[1024]{0:T(1024)} %param.20) | copy-start | bytes 12292
  120.6 59.6 %copy-start.1 = (f32[16,1024]{1,0:T(8,128)S(1)}, f32[16,1024]{1,0:T(8,128)}, u32[]{:S(2)}) copy-start(f32[16,1024]{1,0:T(8,128)} %reduce-scatter.3.cloned.1.call-done) | copy-start | bytes 196612
  120.6 59.6 %copy-start.4 = (f32[1024]{0:T(1024)S(1)}, f32[1024]{0:T(1024)}, u32[]{:S(2)}) copy-start(f32[1024]{0:T(1024)} %param.24) | copy-start | bytes 12292
Sparse Core Ops, SparseCore 0:
  26.0 55.2 reduce-scatter.2
  123.3 54.8 reduce-scatter.4
where the time goes:
time: 190 us
  waiting for transfers between devices  98.4 us (52%)
  blocking collectives  34.5 us (18%)
  matrix products  20 us (11%)
  between operations  14.9 us (8%)
  local copies, waits for them, and re-layouts  14.8 us (8%)
  other arithmetic  7.06 us (4%)
    reduce_scatter x1, waiting for transfers between devices, on_device(): lax.psum_scatter(partial_all, 'hist', scatter_dimension=0, tiled=True)  55 us
    reduce_scatter x1, waiting for transfers between devices, on_device(): lax.psum_scatter(terms, 'hist', scatter_dimension=0, tiled=True)  43.3 us
    all_gather x1, blocking collectives, on_device(): query_rows = lax.all_gather(queries, 'hist', axis=0, tiled=True)  20.8 us
    dot_general x4, matrix products, one_group(): jnp.einsum('chj,jhd->chd', weights, value_part, preferred_element_type=jn...  14.4 us
    unnamed x1, blocking collectives  13.8 us
    unnamed x20, local copies, waits for them, and re-layouts  10.4 us
  transfers between devices with their start and end apart: 2, of which 2 were waited for; matrix products, arithmetic and copies ran while one was open for 6% of the time, Pallas kernels for 0%

commit v1 on v0

v1 whole, which is shorter than its diff:
```python
import functools

import jax
import jax.numpy as jnp
from jax import lax
from jax.experimental import pallas as pl
from jax.experimental.pallas import tpu as pltpu
from jax.sharding import PartitionSpec as P

BF16 = jnp.bfloat16
F32 = jnp.float32
LANES = 128
ROWS_AT_ONCE = 256
EVENTS_AT_ONCE = 512
NT = (((1,), (1,)), ((), ()))
VMEM = pl.BlockSpec(memory_space=pltpu.VMEM)
SMEM = pl.BlockSpec(memory_space=pltpu.SMEM)


def params(mib):
    return pltpu.CompilerParams(vmem_limit_bytes=mib << 20)


def stage_masks(size, joined_tail):
    bits = [1 << k for k in range(size.bit_length() - 1)][::-1]
    near = bits[-2:]
    far = bits[:-2]
    stages = [sorted(far[k : k + 2]) for k in range(0, len(far), 2)]
    return stages + ([near] if joined_tail else [[b] for b in near])


def combos(bits):
    out = [0]
    for b in bits:
        out = out + [m | b for m in out]
    return out


def swap(x, mask, axis, size):
    return lax.ppermute(x, axis, [(i, i ^ mask) for i in range(size)])


def gather_relative(x, dim, axis, size, joined_tail):
    for bits in stage_masks(size, joined_tail):
        x = jnp.concatenate([x] + [swap(x, m, axis, size) for m in combos(bits)[1:]], axis=dim)
    return x


def position_bits(size):
    return [b for stage in stage_masks(size, False) for b in stage]


def rounds_of(ranks, slots):
    return jnp.max(ranks) // slots + 1


def candidates_info(ids_ref, me, size, table_rows):
    count = ids_ref.shape[1]
    each = count // size
    ids = ids_ref[...]
    owner = ids // table_rows
    place = lax.broadcasted_iota(jnp.int32, (1, count), 1)
    block = place // each
    mask = jnp.zeros_like(place)
    for k, b in enumerate(position_bits(size)):
        mask = mask + ((block >> k) & 1) * b
    key = owner * count + (mask ^ me) * each + place % each
    return owner, key, ids - owner * table_rows


def to_column(row):
    count = row.shape[1]
    r = lax.broadcasted_iota(jnp.int32, (count, count), 0)
    c = lax.broadcasted_iota(jnp.int32, (count, count), 1)
    return jnp.sum(jnp.where(r == c, row, 0), axis=1, keepdims=True)


def lookup_kernel(place_ref, ids_ref, table_ref, out_ref, *, size):
    me, turn = place_ref[0], place_ref[1]
    slots = out_ref.shape[0]
    rows = table_ref.shape[0]
    count = ids_ref.shape[1]
    owner, key, offset = candidates_info(ids_ref, me, size, rows)
    key_col = to_column(key)
    before = (key_col < key) & (key_col >= owner * count)
    rank = jnp.sum(before.astype(jnp.int32), axis=0, keepdims=True)
    slot = lax.broadcasted_iota(jnp.int32, (slots, count), 0) + turn * slots
    hit = (owner == me) & (rank == slot)
    want = jnp.sum(jnp.where(hit, offset + 1, 0), axis=1, keepdims=True) - 1
    pick = (want == lax.broadcasted_iota(jnp.int32, (slots, rows), 1)).astype(F32).astype(BF16)
    out_ref[...] = jnp.dot(pick, table_ref[...], preferred_element_type=F32).astype(BF16)


def lookup(place, ids, table, slots, size):
    return pl.pallas_call(
        functools.partial(lookup_kernel, size=size),
        out_shape=jax.ShapeDtypeStruct((slots, table.shape[1]), BF16),
        in_specs=[SMEM, VMEM, VMEM],
        out_specs=VMEM,
        compiler_params=params(24),
        name="lookup",
    )(place, ids, table)


def plan_kernel(place_ref, ids_ref, pick_ref, rounds_ref, *, size, slots, table_rows):
    me, turn = place_ref[0], place_ref[1]
    count = ids_ref.shape[1]
    owner, key, _ = candidates_info(ids_ref, me, size, table_rows)
    key_col = to_column(key)
    owner_col = key_col // count
    before = (key < key_col) & (key >= owner_col * count)
    rank = jnp.sum(before.astype(jnp.int32), axis=1, keepdims=True)
    rounds_ref[0] = rounds_of(rank, slots)
    away = owner_col ^ me
    block = jnp.zeros_like(away)
    for k, b in enumerate(position_bits(size)):
        block = block + jnp.where((away & b) != 0, 1 << k, 0)
    mine = rank - turn * slots
    slot = jnp.where((mine >= 0) & (mine < slots), block * slots + mine, -1)
    pick = slot == lax.broadcasted_iota(jnp.int32, pick_ref.shape, 1)
    pick_ref[...] = pick.astype(F32).astype(BF16)


def plan(place, ids, slots, table_rows, size):
    count = ids.shape[1]
    return pl.pallas_call(
        functools.partial(plan_kernel, size=size, slots=slots, table_rows=table_rows),
        out_shape=(
            jax.ShapeDtypeStruct((count, size * slots), BF16),
            jax.ShapeDtypeStruct((1,), jnp.int32),
        ),
        in_specs=[SMEM, VMEM],
        out_specs=(VMEM, SMEM),
        compiler_params=params(40),
        cost_estimate=pl.CostEstimate(flops=1 << 22, transcendentals=0, bytes_accessed=1 << 20),
        name="plan",
    )(place, ids)


def select_kernel(pick_ref, rows_ref, out_ref):
    out_ref[...] = jnp.dot(pick_ref[...], rows_ref[...], preferred_element_type=F32).astype(BF16)


def select(pick, rows):
    return pl.pallas_call(
        select_kernel,
        out_shape=jax.ShapeDtypeStruct((pick.shape[0], rows.shape[1]), BF16),
        in_specs=[VMEM, VMEM],
        out_specs=VMEM,
        compiler_params=params(32),
        name="select",
    )(pick, rows)


def three_parts(x):
    high = x.astype(BF16)
    rest = x - high.astype(F32)
    middle = rest.astype(BF16)
    return [high, middle, (rest - middle.astype(F32)).astype(BF16)]


def bias_kernel(place_ref, start_ref, times_ref, time_bias_ref, pos_bias_ref, out_ref, *, npos, history):
    events = times_ref.shape[1]
    first = history - start_ref[0] - place_ref[0] * events
    distance = first - lax.broadcasted_iota(jnp.int32, (1, events), 1)
    bucket = jnp.zeros((1, events), jnp.int32)
    for k in range(1, npos):
        bucket = bucket + (distance >= (1 << k)).astype(jnp.int32)
    columns = []
    for table_ref, index in ((time_bias_ref, times_ref[...]), (pos_bias_ref, bucket)):
        table = jnp.concatenate(three_parts(table_ref[...] * 0.5), axis=0)
        kinds = table.shape[1]
        hot = lax.broadcasted_iota(jnp.int32, (kinds, events), 0) == index
        columns.append(
            jnp.dot(table, hot.astype(F32).astype(BF16), preferred_element_type=F32)
        )
    used = sum(c.shape[0] for c in columns)
    columns.append(jnp.zeros((LANES - used, events), F32))
    out_ref[...] = jnp.concatenate(columns, axis=0).T.astype(BF16)


def bias_columns(place, start, times, time_bias, pos_bias, npos, history):
    return pl.pallas_call(
        functools.partial(bias_kernel, npos=npos, history=history),
        out_shape=jax.ShapeDtypeStruct((times.shape[1], LANES), BF16),
        in_specs=[SMEM, SMEM, VMEM, VMEM, VMEM],
        out_specs=VMEM,
        compiler_params=params(16),
        cost_estimate=pl.CostEstimate(flops=1 << 25, transcendentals=0, bytes_accessed=1 << 20),
        name="bias",
    )(place, start, times, time_bias, pos_bias)


def silu(x):
    return x / (1.0 + jnp.exp(-x))


def normalise(embedded, gain):
    x = embedded.astype(F32)
    meansq = jnp.mean(x * x, axis=-1, keepdims=True)
    return (x * lax.rsqrt(meansq + 1e-06) * gain).astype(BF16)


def attend_kernel(
    emb_ref, gain_ref, proj_ref, key_ref, value_ref, bias_ref, keep_ref, send_ref, query_ref, *, heads
):
    count, width = emb_ref.shape
    head_dim = width // heads
    events = key_ref.shape[0]
    half = count // 2
    rows = min(ROWS_AT_ONCE, count)
    per = LANES // head_dim
    step = min(EVENTS_AT_ONCE, events)
    for first in range(0, count, rows):
        normed = normalise(emb_ref[first : first + rows, :], gain_ref[...])
        projected = jnp.dot(normed, proj_ref[:, :width], preferred_element_type=F32)
        query = silu(projected).astype(BF16)
        query_ref[...] = query * jnp.asarray(0.5 * head_dim**-0.5, BF16)
        lane = lax.broadcasted_iota(jnp.int32, (rows, LANES), 1)
        for group in range(heads // per):
            at = slice(group * LANES, (group + 1) * LANES)
            part = query_ref[:, at]
            zero, one = jnp.zeros_like(part), jnp.ones_like(part)
            stacked = []
            for k in range(per):
                own = jnp.where(lane // head_dim == k, part, zero)
                chosen = jnp.where(lane % heads == group * per + k, one, zero)
                stacked.append(jnp.concatenate([own, chosen], axis=1))
            left = jnp.concatenate(stacked, axis=0)
            total = jnp.zeros((per * rows, LANES), F32)
            for j in range(0, events, step):
                right = jnp.concatenate([key_ref[j : j + step, at], bias_ref[j : j + step, :]], axis=1)
                t = lax.dot_general(left, right, NT, preferred_element_type=F32)
                weights = (t + t * jnp.tanh(t)).astype(BF16)
                total = total + jnp.dot(weights, value_ref[j : j + step, at], preferred_element_type=F32)
            out = total[:rows]
            for k in range(1, per):
                out = jnp.where(lane // head_dim == k, total[k * rows : (k + 1) * rows], out)
            if first + rows <= half:
                keep_ref[first : first + rows, at] = out
            elif first >= half:
                send_ref[first - half : first - half + rows, at] = out.astype(BF16)
            else:
                keep_ref[first:half, at] = out[: half - first]
                send_ref[: first + rows - half, at] = out[half - first :].astype(BF16)


def attend(embedded, gain, proj_in, keys, values, bias, heads):
    count, width = embedded.shape
    return pl.pallas_call(
        functools.partial(attend_kernel, heads=heads),
        out_shape=(
            jax.ShapeDtypeStruct((count // 2, width), F32),
            jax.ShapeDtypeStruct((count // 2, width), BF16),
        ),
        in_specs=[VMEM] * 6,
        out_specs=(VMEM, VMEM),
        scratch_shapes=[pltpu.VMEM((min(ROWS_AT_ONCE, count), width), BF16)],
        compiler_params=params(40),
        cost_estimate=pl.CostEstimate(
            flops=8 * count * width * keys.shape[0],
            transcendentals=count * heads * keys.shape[0],
            bytes_accessed=4 * keys.size,
        ),
        name="attend",
    )(embedded, gain, proj_in, keys, values, bias)


def gates_kernel(emb_ref, gain_ref, proj_ref, out_ref):
    width = emb_ref.shape[1]
    normed = normalise(emb_ref[...], gain_ref[...])
    projected = jnp.dot(normed, proj_ref[:, width:], preferred_element_type=F32)
    out_ref[...] = silu(projected).astype(BF16)


def gates_of(embedded, gain, proj_in):
    return pl.pallas_call(
        gates_kernel,
        out_shape=jax.ShapeDtypeStruct(embedded.shape, BF16),
        in_specs=[VMEM] * 3,
        out_specs=VMEM,
        compiler_params=params(16),
        cost_estimate=pl.CostEstimate(flops=1 << 26, transcendentals=1 << 14, bytes_accessed=1 << 22),
        name="gates",
    )(embedded, gain, proj_in)


def finish_kernel(own_ref, *refs):
    *parts, emb_ref, gates_ref, gain_ref, proj_ref, out_ref = refs
    attended = own_ref[...]
    for p in parts:
        attended = attended + p[...].astype(F32)
    centred = attended - jnp.mean(attended, axis=-1, keepdims=True)
    variance = jnp.mean(centred * centred, axis=-1, keepdims=True)
    gated = centred * lax.rsqrt(variance + 1e-05) * gain_ref[...] * gates_ref[...].astype(F32)
    product = jnp.dot(gated.astype(BF16), proj_ref[...], preferred_element_type=F32)
    out_ref[...] = (emb_ref[...].astype(F32) + product).astype(BF16)


def finish(own, parts, embedded, gates, gain, proj_out):
    return pl.pallas_call(
        finish_kernel,
        out_shape=jax.ShapeDtypeStruct(embedded.shape, BF16),
        in_specs=[VMEM] * (len(parts) + 5),
        out_specs=VMEM,
        compiler_params=params(16),
        name="finish",
    )(own, *parts, embedded, gates, gain, proj_out)


def on_device(
    item_ids,
    item_table,
    key_cache,
    value_cache,
    time_buckets,
    window_start,
    norm_gain,
    proj_in,
    time_bias,
    pos_bias,
    out_gain,
    proj_out,
):
    axis = "hist"
    size = lax.axis_size(axis)
    me = lax.axis_index(axis).astype(jnp.int32)
    each = item_ids.shape[0]
    slots = 2 * each
    heads = time_bias.shape[0]
    npos = pos_bias.shape[1]
    events = key_cache.shape[0]
    table_rows = item_table.shape[0]
    gain = norm_gain[None, :]

    def place(turn):
        return jnp.stack([me, jnp.asarray(turn, jnp.int32)])

    here = place(0)
    bias = bias_columns(
        here,
        window_start,
        time_buckets[None, :],
        time_bias,
        jnp.pad(pos_bias, ((0, 0), (0, -npos % 32))),
        npos,
        2 * events * size,
    )
    ids = gather_relative(item_ids[None, :], 1, axis, size, True)

    def fetch(turn):
        return gather_relative(
            lookup(place(turn), ids, item_table, slots, size), 0, axis, size, False
        )

    rows = fetch(0)
    pick, rounds = plan(here, ids, slots, table_rows, size)
    embedded = select(pick, rows)

    def more(state):
        turn, so_far = state
        picked, _ = plan(place(turn), ids, slots, table_rows, size)
        return turn + 1, so_far + select(picked, fetch(turn))

    _, embedded = lax.while_loop(lambda s: s[0] < rounds[0], more, (jnp.int32(1), embedded))

    keep, send = attend(embedded, gain, proj_in, key_cache, value_cache, bias, heads)
    own = embedded[:each]
    gates = gates_of(own, gain, proj_in)

    stages = stage_masks(size, False)[::-1]
    total = keep + swap(send, stages[0][0], axis, size).astype(F32)
    for bits in stages[1:]:
        masks = combos(bits)
        block = total.shape[0] // len(masks)
        parts = [
            swap(total[k * block : (k + 1) * block].astype(BF16), m, axis, size)
            for k, m in enumerate(masks)
            if k
        ]
        if bits is stages[-1]:
            break
        total = sum([p.astype(F32) for p in parts], total[:block])
    return finish(total[:block], parts, own, gates, out_gain[None, :], proj_out)


def solution(mesh):
    placed = (
        P(("grp", "hist")),
        P("hist", None),
        P(("grp", "hist"), None),
        P(("grp", "hist"), None),
        P(("grp", "hist")),
        P("grp"),
        P(),
        P(),
        P(),
        P(),
        P(),
        P(),
    )
    return jax.shard_map(
        on_device, mesh=mesh, in_specs=placed, out_specs=P(("grp", "hist"), None), check_vma=False
    )
```

time: 190 us -> 68.7 us (0.36)
  waiting for transfers between devices: 98.4 us -> 25.8 us
  blocking collectives: 34.5 us -> 0 us
  matrix products: 20 us -> 0 us
  starting transfers between devices: 0.04 us -> 19.2 us
  Pallas kernels: 0 us -> 14.4 us
  between operations: 14.9 us -> 0.88 us
  local copies, waits for them, and re-layouts: 14.8 us -> 6.26 us
  other arithmetic: 7.06 us -> 0.91 us
    reduce_scatter x2 -> x0, waiting for transfers between devices: 98.3 us -> none  [the longest x1 55 us: on_device(): lax.psum_scatter(partial_all, 'hist', scatter_dimension=0, tiled=True)]
    ppermute x0 -> x16, waiting for transfers between devices: none -> 25.8 us  [swap(): return lax.ppermute(x, axis, [(i, i ^ mask) for i in range(size)])]
    all_gather x1 -> x0, blocking collectives: 20.8 us -> none  [on_device(): query_rows = lax.all_gather(queries, 'hist', axis=0, tiled=True)]
    dot_general x6 -> x0, matrix products: 20 us -> none  [the longest x4 14.4 us: one_group(): jnp.einsum('chj,jhd->chd', weights, value_part, preferred_element_type=jn...]
    ppermute x0 -> x16, starting transfers between devices: none -> 19.2 us  [swap(): return lax.ppermute(x, axis, [(i, i ^ mask) for i in range(size)])]
    pallas_call x0 -> x7, Pallas kernels: none -> 14.4 us  [the longest x1 6.78 us: attend(): pl.pallas_call(functools.partial(attend_kernel, heads=heads), out_shape=(...]
    unnamed x1 -> x0, blocking collectives: 13.8 us -> none
    unnamed x20 -> x22, local copies, waits for them, and re-layouts: 10.4 us -> 4.65 us
  transfers between devices with their start and end apart: 2 -> 16, of which waited for: 2 -> 11; matrix products, arithmetic and copies ran while one was open for 6% -> 1% of each run, Pallas kernels for 0% -> 4%
where the time goes in v1:
time: 68.7 us; the launch traced here: 68.3 us
  waiting for transfers between devices  25.8 us (38%)
  starting transfers between devices  19.2 us (28%)
  Pallas kernels  14.4 us (21%)
  local copies, waits for them, and re-layouts  6.26 us (9%)
  other arithmetic  0.91 us (1%)
  between operations  0.88 us (1%)
  loops' own time  0.78 us (1%)
    ppermute x16, waiting for transfers between devices, swap(): return lax.ppermute(x, axis, [(i, i ^ mask) for i in range(size)])  25.8 us
    ppermute x16, starting transfers between devices, swap(): return lax.ppermute(x, axis, [(i, i ^ mask) for i in range(size)])  19.2 us
    pallas_call x1, Pallas kernels, attend(): pl.pallas_call(functools.partial(attend_kernel, heads=heads), out_shape=(...  6.78 us
    unnamed x22, local copies, waits for them, and re-layouts  4.65 us
    pallas_call x1, Pallas kernels, lookup(): pl.pallas_call(functools.partial(lookup_kernel, size=size), out_shape=jax...  2.32 us
    pallas_call x1, Pallas kernels, plan(): pl.pallas_call(functools.partial(plan_kernel, size=size, slots=slots, tab...  1.53 us
  transfers between devices with their start and end apart: 16, of which 11 were waited for; matrix products, arithmetic and copies ran while one was open for 1% of the time, Pallas kernels for 4%

profile of v1, /device:TPU:0, one launch (start us, length us, event | category | flops | bytes accessed | tf_op | source)
XLA Modules:
  0.0 68.3 jit_solution(7926076589183684771)
XLA Ops:
  0.0 3.1 %collective-permute-start.5 = (s32[1,16]{1,0:T(1,128)}, s32[1,16]{1,0:T(1,128)S(1)}, u32[]{:S(2)}, u32[]{:S(2)}) collective-permute-start(s32[1,16]{1,0:T(1,128)} %bitcast.17), channel_id=1, source_target_pairs={{0,4},{1,5},{2,6},{3,7},{4,0},{5,1},{6,2},{7,3},{8,12},{9,13},{10,... | collective-permute-start | bytes 200 | tf_op jit(solution)/shard_map/ppermute | solution.py:40
  3.1 2.6 %collective-permute-start.6 = (s32[1,16]{1,0:T(1,128)}, s32[1,16]{1,0:T(1,128)S(1)}, u32[]{:S(2)}, u32[]{:S(2)}) collective-permute-start(s32[1,16]{1,0:T(1,128)} %bitcast.18), channel_id=1, source_target_pairs={{0,8},{1,9},{2,10},{3,11},{4,12},{5,13},{6,14},{7,15},{8,0},{9,1},... | collective-permute-start | bytes 200 | tf_op jit(solution)/shard_map/ppermute | solution.py:40
  5.6 0.0 collective-permute-start.7
  5.6 0.0 collective-permute-done.5
  5.6 2.0 %collective-permute-done.6 = s32[1,16]{1,0:T(1,128)S(1)} collective-permute-done((s32[1,16]{1,0:T(1,128)}, s32[1,16]{1,0:T(1,128)S(1)}, u32[]{:S(2)}, u32[]{:S(2)}) %collective-permute-start.6) | collective-permute-done | bytes 96 | tf_op jit(solution)/shard_map/ppermute | solution.py:40
  7.7 3.5 %collective-permute-done.7 = s32[1,16]{1,0:T(1,128)S(1)} collective-permute-done((s32[1,16]{1,0:T(1,128)}, s32[1,16]{1,0:T(1,128)S(1)}, u32[]{:S(2)}, u32[]{:S(2)}) %collective-permute-start.7) | collective-permute-done | bytes 96 | tf_op jit(solution)/shard_map/ppermute | solution.py:40
  11.1 0.7 %pad_add_fusion.2 = s32[1,64]{1,0:T(1,128)S(1)} fusion(s32[1,16]{1,0:T(1,128)S(1)} %collective-permute-done.7, s32[1,16]{1,0:T(1,128)S(1)} %collective-permute-done.6, s32[1,16]{1,0:T(1,128)S(1)} %collective-permute-done.5, s32[1,16]{1,0:T(1,128)} %bitcast.20), kind=kLoop, calls=%fused_computation.29 | loop fusion | flops 192 | bytes 512 | tf_op jit(solution)/shard_map/concatenate | solution.py:45
  11.9 0.0 collective-permute-start.10
  11.9 1.6 %collective-permute-start.8 = (s32[1,64]{1,0:T(1,128)S(1)}, s32[1,64]{1,0:T(1,128)S(1)}, u32[]{:S(2)}, u32[]{:S(2)}) collective-permute-start(s32[1,64]{1,0:T(1,128)S(1)} %pad_add_fusion.2), channel_id=1, source_target_pairs={{0,2},{1,3},{2,0},{3,1},{4,6},{5,7},{6,4},{7,5},{8,10},{9,11},{10,... | collective-permute-start | bytes 776 | tf_op jit(solution)/shard_map/ppermute | solution.py:40
  13.5 0.3 collective-permute-start.9
  13.7 0.1 pad_add_fusion.1.place_ref
  13.8 1.1 %collective-permute-done.10 = s32[1,64]{1,0:T(1,128)S(1)} collective-permute-done((s32[1,64]{1,0:T(1,128)S(1)}, s32[1,64]{1,0:T(1,128)S(1)}, u32[]{:S(2)}, u32[]{:S(2)}) %collective-permute-start.10) | collective-permute-done | bytes 288 | tf_op jit(solution)/shard_map/ppermute | solution.py:40
  14.9 0.7 collective-permute-done.8
  15.5 0.0 collective-permute-done.9
  15.5 0.7 %concatenate.30.ids_ref = s32[1,256]{1,0:T(1,128)S(1)} concatenate(s32[1,16]{1,0:T(1,128)} %bitcast.21, s32[1,16]{1,0:T(1,128)S(1)} %collective-permute-done.5, s32[1,16]{1,0:T(1,128)S(1)} %collective-permute-done.6, s32[1,16]{1,0:T(1,128)S(1)} %collective-permute-done.7, s32[1,64]{1,0:T(1,128)S(1)} %collective-permute-done.8, s32[1,64]{1,0:T(1,128)S(1)} %collective-permute-done.9, ...), dimensions={1} | concatenate | bytes 2048 | tf_op jit(solution)/shard_map/concatenate | solution.py:45
  16.3 0.0 copy-start.10
  16.3 0.0 copy-start.5
  16.3 0.0 copy-start.6
  16.3 2.3 %lookup.2 = bf16[32,1024]{1,0:T(8,128)(2,1)S(1)} custom-call(s32[2]{0:T(128)S(1)} %pad_add_fusion.1.place_ref, s32[1,256]{1,0:T(1,128)S(1)} %concatenate.30.ids_ref, bf16[1024,1024]{1,0:T(8,128)(2,1)} %table_ref.1), custom_call_target="tpu_custom_call" | custom-call | tf_op jit(solution)/shard_map/lookup/pallas_call | solution.py:95
  18.6 0.1 collective-permute-start.11
  18.7 0.6 collective-permute-start.12
  19.3 3.8 %collective-permute-start.13 = (bf16[32,1024]{1,0:T(8,128)(2,1)S(1)}, bf16[32,1024]{1,0:T(8,128)(2,1)S(1)}, u32[]{:S(2)}, u32[]{:S(2)}) collective-permute-start(bf16[32,1024]{1,0:T(8,128)(2,1)S(1)} %lookup.2), channel_id=1, source_target_pairs={{0,12},{1,13},{2,14},{3,15},{4,8},{5,9},{6,10},{7,11},{8,4},{9,5},... | collective-permute-start | bytes 196616 | tf_op jit(solution)/shard_map/ppermute | solution.py:40
  23.1 1.0 %collective-permute-done.11 = bf16[32,1024]{1,0:T(8,128)(2,1)S(1)} collective-permute-done((bf16[32,1024]{1,0:T(8,128)(2,1)S(1)}, bf16[32,1024]{1,0:T(8,128)(2,1)S(1)}, u32[]{:S(2)}, u32[]{:S(2)}) %collective-permute-start.11) | collective-permute-done | bytes 65568 | tf_op jit(solution)/shard_map/ppermute | solution.py:40
  24.1 3.3 %collective-permute-done.12 = bf16[32,1024]{1,0:T(8,128)(2,1)S(1)} collective-permute-done((bf16[32,1024]{1,0:T(8,128)(2,1)S(1)}, bf16[32,1024]{1,0:T(8,128)(2,1)S(1)}, u32[]{:S(2)}, u32[]{:S(2)}) %collective-permute-start.12) | collective-permute-done | bytes 65568 | tf_op jit(solution)/shard_map/ppermute | solution.py:40
  27.4 0.0 collective-permute-done.13
  27.5 0.7 %collective-permute-start.14 = (bf16[128,1024]{1,0:T(8,128)(2,1)S(1)}, bf16[128,1024]{1,0:T(8,128)(2,1)S(1)}, u32[]{:S(2)}, u32[]{:S(2)}) collective-permute-start(bf16[128,1024]{1,0:T(8,128)(2,1)S(1)} %pad_maximum_fusion.1), channel_id=1, source_target_pairs={{0,2},{1,3},{2,0},{3,1},{4,6},{5,7},{6,4},{7,5},{8,10},{9,11},{10,... | collective-permute-start | bytes 786440 | tf_op jit(solution)/shard_map/ppermute | solution.py:40
  28.2 5.7 %collective-permute-done.14 = bf16[128,1024]{1,0:T(8,128)(2,1)S(1)} collective-permute-done((bf16[128,1024]{1,0:T(8,128)(2,1)S(1)}, bf16[128,1024]{1,0:T(8,128)(2,1)S(1)}, u32[]{:S(2)}, u32[]{:S(2)}) %collective-permute-start.14) | collective-permute-done | bytes 262176 | tf_op jit(solution)/shard_map/ppermute | solution.py:40
  34.0 0.1 collective-permute-start.15
  34.7 0.0 copy-done.10
  34.7 0.0 copy-done.5
  34.8 0.0 copy-done.6
  34.8 0.9 %bias.1.bias_ref = bf16[1024,128]{1,0:T(8,128)(2,1)S(1)} custom-call(s32[2]{0:T(128)S(1)} %pad_add_fusion.1.place_ref, s32[1]{0:T(128)S(6)} %copy.37.start_ref, s32[1,1024]{1,0:T(1,128)S(1)} %bitcast.15, f32[16,128]{1,0:T(8,128)S(1)} %copy-done.5, f32[16,32]{1,0:T(8,128)S(1)} %pad.4.pos_bias_ref), custom_call_target="tpu_custom_call" | custom-call | flops 33554432 | bytes 1048576 | tf_op jit(solution)/shard_map/bias/pallas_call | solution.py:183
  35.6 1.5 %plan.2 = (bf16[256,512]{1,0:T(8,128)(2,1)S(1)}, s32[1]{0:T(128)}) custom-call(s32[2]{0:T(128)S(1)} %pad_add_fusion.1.place_ref, s32[1,256]{1,0:T(1,128)S(1)} %concatenate.30.ids_ref), custom_call_target="tpu_custom_call" | custom-call | flops 4194304 | bytes 1048576 | tf_op jit(solution)/shard_map/plan/pallas_call | solution.py:126
  37.2 0.0 collective-permute-done.15
  37.2 1.3 %select.3 = bf16[256,1024]{1,0:T(8,128)(2,1)} custom-call(bf16[256,512]{1,0:T(8,128)(2,1)S(1)} %get-tuple-element.43.pick_ref, bf16[512,1024]{1,0:T(8,128)(2,1)S(1)} %constant_dynamic-update-slice_fusion.16.rows_ref), custom_call_target="tpu_custom_call" | custom-call | tf_op jit(solution)/shard_map/select/pallas_call | solution.py:145
  38.5 0.0 copy-start.2
  38.5 0.0 copy-start.4
  38.5 0.8 %while.10 = (s32[]{:T(128)}, bf16[256,1024]{1,0:T(8,128)(2,1)}, s32[1]{0:T(128)}, s32[]{:T(128)}, s32[1,256]{1,0:T(1,128)S(1)}, /*index=5*/bf16[1024,1024]{1,0:T(8,128)(2,1)}, s32[]{:T(128)}) while((s32[]{:T(128)}, bf16[256,1024]{1,0:T(8,128)(2,1)}, s32[1]{0:T(128)}, s32[]{:T(128)}, s32[1,256]{1,0:T(1,128)S(1)}, ...), condition=%wide.region_1.2_spmd, body=%wide.region_0.1_spmd.sunk | while | flops 5505028 | bytes 13893981 | solution.py:365
  39.3 0.8 %copy-done.2 = bf16[1024,1024]{1,0:T(8,128)(2,1)S(1)} copy-done((bf16[1024,1024]{1,0:T(8,128)(2,1)S(1)}, bf16[1024,1024]{1,0:T(8,128)(2,1)}, u32[]{:S(2)}) %copy-start.2) | copy-done | bytes 2097176
  40.1 0.0 copy-done.4
  40.1 0.0 copy-start
  40.1 2.2 %copy-done = bf16[1024,2048]{1,0:T(8,128)(2,1)S(1)} copy-done((bf16[1024,2048]{1,0:T(8,128)(2,1)S(1)}, bf16[1024,2048]{1,0:T(8,128)(2,1)}, u32[]{:S(2)}) %copy-start) | copy-done | bytes 4194328
  42.3 0.0 copy-start.3
  42.3 1.6 %copy-done.3 = bf16[1024,1024]{1,0:T(8,128)(2,1)S(1)} copy-done((bf16[1024,1024]{1,0:T(8,128)(2,1)S(1)}, bf16[1024,1024]{1,0:T(8,128)(2,1)}, u32[]{:S(2)}) %copy-start.3) | copy-done | bytes 2097176
  43.9 6.8 %attend.1 = (f32[128,1024]{1,0:T(8,128)S(1)}, bf16[128,1024]{1,0:T(8,128)(2,1)S(1)}) custom-call(bf16[256,1024]{1,0:T(8,128)(2,1)} %get-tuple-element.45.emb_ref, f32[1,1024]{1,0:T(1,128)S(1)} %bitcast.13, bf16[1024,2048]{1,0:T(8,128)(2,1)S(1)} %copy-done, bf16[1024,1024]{1,0:T(8,128)(2,1)S(1)} %copy-done.2, bf16[1024,1024]{1,0:T(8,128)(2,1)S(1)} %copy-done.3, ...), custom_call_target="tpu_custom_call" | custom-call | flops 2147483648 | bytes 4194304 | tf_op jit(solution)/shard_map/attend/pallas_call | solution.py:250
  50.7 0.6 collective-permute-start.16
  51.2 1.2 %collective-permute-done.16 = bf16[128,1024]{1,0:T(8,128)(2,1)S(1)} collective-permute-done((bf16[128,1024]{1,0:T(8,128)(2,1)S(1)}, bf16[128,1024]{1,0:T(8,128)(2,1)S(1)}, u32[]{:S(2)}, u32[]{:S(2)}) %collective-permute-start.16) | collective-permute-done | bytes 262176 | tf_op jit(solution)/shard_map/ppermute | solution.py:40
  52.4 0.1 convert_add_fusion
  52.5 0.7 collective-permute-start.17
  53.2 5.2 %collective-permute-done.17 = bf16[64,1024]{1,0:T(8,128)(2,1)S(1)} collective-permute-done((bf16[64,1024]{1,0:T(8,128)(2,1)S(1)}, bf16[64,1024]{1,0:T(8,128)(2,1)S(1)}, u32[]{:S(2)}, u32[]{:S(2)}) %collective-permute-start.17) | collective-permute-done | bytes 131104 | tf_op jit(solution)/shard_map/ppermute | solution.py:40
  58.4 2.8 %collective-permute-start.18 = (bf16[16,1024]{1,0:T(8,128)(2,1)S(1)}, bf16[16,1024]{1,0:T(8,128)(2,1)S(1)}, u32[]{:S(2)}, u32[]{:S(2)}) collective-permute-start(bf16[16,1024]{1,0:T(8,128)(2,1)S(1)} %get-tuple-element.76), channel_id=1, source_target_pairs={{0,4},{1,5},{2,6},{3,7},{4,0},{5,1},{6,2},{7,3},{8,12},{9,13},{10,... | collective-permute-start | bytes 98312 | tf_op jit(solution)/shard_map/ppermute | solution.py:40
  61.2 0.2 collective-permute-start.19
  61.4 2.2 %collective-permute-start.20 = (bf16[16,1024]{1,0:T(8,128)(2,1)S(1)}, bf16[16,1024]{1,0:T(8,128)(2,1)S(1)}, u32[]{:S(2)}, u32[]{:S(2)}) collective-permute-start(bf16[16,1024]{1,0:T(8,128)(2,1)S(1)} %get-tuple-element.74), channel_id=1, source_target_pairs={{0,12},{1,13},{2,14},{3,15},{4,8},{5,9},{6,10},{7,11},{8,4},{9,5},... | collective-permute-start | bytes 98312 | tf_op jit(solution)/shard_map/ppermute | solution.py:40
  63.6 0.8 %slice.31.emb_ref.refs_3_ = bf16[16,1024]{1,0:T(8,128)(2,1)S(1)} slice(bf16[256,1024]{1,0:T(8,128)(2,1)} %get-tuple-element.45.emb_ref), slice={[0:16], [0:1024]} | slice | bytes 65536 | tf_op jit(solution)/shard_map/slice | solution.py:368
  64.4 0.0 copy-start.1
  64.4 0.0 copy-start.7
  64.4 0.5 gates.1.refs_4_
  64.9 0.0 collective-permute-done.18.refs_0_
  64.9 1.2 %collective-permute-done.19.refs_1_ = bf16[16,1024]{1,0:T(8,128)(2,1)S(1)} collective-permute-done((bf16[16,1024]{1,0:T(8,128)(2,1)S(1)}, bf16[16,1024]{1,0:T(8,128)(2,1)S(1)}, u32[]{:S(2)}, u32[]{:S(2)}) %collective-permute-start.19) | collective-permute-done | bytes 32800 | tf_op jit(solution)/shard_map/ppermute | solution.py:40
  66.1 1.0 %collective-permute-done.20.refs_2_ = bf16[16,1024]{1,0:T(8,128)(2,1)S(1)} collective-permute-done((bf16[16,1024]{1,0:T(8,128)(2,1)S(1)}, bf16[16,1024]{1,0:T(8,128)(2,1)S(1)}, u32[]{:S(2)}, u32[]{:S(2)}) %collective-permute-start.20) | collective-permute-done | bytes 32800 | tf_op jit(solution)/shard_map/ppermute | solution.py:40
  67.1 0.0 copy-done.1
  67.1 0.0 copy-done.7
  67.1 1.2 %finish.1 = bf16[16,1024]{1,0:T(8,128)(2,1)} custom-call(f32[16,1024]{1,0:T(8,128)S(1)} %slice.34.own_ref, bf16[16,1024]{1,0:T(8,128)(2,1)S(1)} %collective-permute-done.18.refs_0_, bf16[16,1024]{1,0:T(8,128)(2,1)S(1)} %collective-permute-done.19.refs_1_, bf16[16,1024]{1,0:T(8,128)(2,1)S(1)} %collective-permute-done.20.refs_2_, ...), custom_call_target="tpu_custom_call" | custom-call | tf_op jit(solution)/shard_map/finish/pallas_call | solution.py:301
  (12 shorter events, 0.2 us)
Async XLA Ops:
  0.0 5.6 %collective-permute-start.5 = (s32[1,16]{1,0:T(1,128)}, s32[1,16]{1,0:T(1,128)S(1)}, u32[]{:S(2)}, u32[]{:S(2)}) collective-permute-start(s32[1,16]{1,0:T(1,128)} %bitcast.17), channel_id=1, source_target_pairs={{0,4},{1,5},{2,6},{3,7},{4,0},{5,1},{6,2},{7,3},{8,12},{9,13},{10,... | collective-permute-start | bytes 200 | tf_op jit(solution)/shard_map/ppermute | solution.py:40
  3.1 4.6 %collective-permute-start.6 = (s32[1,16]{1,0:T(1,128)}, s32[1,16]{1,0:T(1,128)S(1)}, u32[]{:S(2)}, u32[]{:S(2)}) collective-permute-start(s32[1,16]{1,0:T(1,128)} %bitcast.18), channel_id=1, source_target_pairs={{0,8},{1,9},{2,10},{3,11},{4,12},{5,13},{6,14},{7,15},{8,0},{9,1},... | collective-permute-start | bytes 200 | tf_op jit(solution)/shard_map/ppermute | solution.py:40
  5.6 5.5 %collective-permute-start.7 = (s32[1,16]{1,0:T(1,128)}, s32[1,16]{1,0:T(1,128)S(1)}, u32[]{:S(2)}, u32[]{:S(2)}) collective-permute-start(s32[1,16]{1,0:T(1,128)} %bitcast.19), channel_id=1, source_target_pairs={{0,12},{1,13},{2,14},{3,15},{4,8},{5,9},{6,10},{7,11},{8,4},{9,5},... | collective-permute-start | bytes 200 | tf_op jit(solution)/shard_map/ppermute | solution.py:40
  11.9 3.0 %collective-permute-start.10 = (s32[1,64]{1,0:T(1,128)S(1)}, s32[1,64]{1,0:T(1,128)S(1)}, u32[]{:S(2)}, u32[]{:S(2)}) collective-permute-start(s32[1,64]{1,0:T(1,128)S(1)} %pad_add_fusion.2), channel_id=1, source_target_pairs={{0,3},{1,2},{2,1},{3,0},{4,7},{5,6},{6,5},{7,4},{8,11},{9,10},{10,... | collective-permute-start | bytes 776 | tf_op jit(solution)/shard_map/ppermute | solution.py:40
  11.9 3.6 %collective-permute-start.8 = (s32[1,64]{1,0:T(1,128)S(1)}, s32[1,64]{1,0:T(1,128)S(1)}, u32[]{:S(2)}, u32[]{:S(2)}) collective-permute-start(s32[1,64]{1,0:T(1,128)S(1)} %pad_add_fusion.2), channel_id=1, source_target_pairs={{0,2},{1,3},{2,0},{3,1},{4,6},{5,7},{6,4},{7,5},{8,10},{9,11},{10,... | collective-permute-start | bytes 776 | tf_op jit(solution)/shard_map/ppermute | solution.py:40
  13.5 2.1 %collective-permute-start.9 = (s32[1,64]{1,0:T(1,128)S(1)}, s32[1,64]{1,0:T(1,128)S(1)}, u32[]{:S(2)}, u32[]{:S(2)}) collective-permute-start(s32[1,64]{1,0:T(1,128)S(1)} %pad_add_fusion.2), channel_id=1, source_target_pairs={{0,1},{1,0},{2,3},{3,2},{4,5},{5,4},{6,7},{7,6},{8,9},{9,8},{10,11... | collective-permute-start | bytes 776 | tf_op jit(solution)/shard_map/ppermute | solution.py:40
  16.3 18.4 %copy-start.10 = (f32[16,18]{1,0:T(8,128)S(1)}, f32[16,18]{1,0:T(8,128)}, u32[]{:S(2)}) copy-start(f32[16,18]{1,0:T(8,128)} %param.23) | copy-start | bytes 3460
  16.3 18.5 %copy-start.5 = (f32[16,128]{1,0:T(8,128)S(1)}, f32[16,128]{1,0:T(8,128)}, u32[]{:S(2)}) copy-start(f32[16,128]{1,0:T(8,128)} %time_bias_ref.1) | copy-start | bytes 24580
  16.3 18.5 %copy-start.6 = (s32[1024]{0:T(1024)S(1)}, s32[1024]{0:T(1024)}, u32[]{:S(2)}) copy-start(s32[1024]{0:T(1024)} %param.18) | copy-start | bytes 12292
  18.6 5.5 %collective-permute-start.11 = (bf16[32,1024]{1,0:T(8,128)(2,1)S(1)}, bf16[32,1024]{1,0:T(8,128)(2,1)S(1)}, u32[]{:S(2)}, u32[]{:S(2)}) collective-permute-start(bf16[32,1024]{1,0:T(8,128)(2,1)S(1)} %lookup.2), channel_id=1, source_target_pairs={{0,4},{1,5},{2,6},{3,7},{4,0},{5,1},{6,2},{7,3},{8,12},{9,13},{10,... | collective-permute-start | bytes 196616 | tf_op jit(solution)/shard_map/ppermute | solution.py:40
  18.7 8.7 %collective-permute-start.12 = (bf16[32,1024]{1,0:T(8,128)(2,1)S(1)}, bf16[32,1024]{1,0:T(8,128)(2,1)S(1)}, u32[]{:S(2)}, u32[]{:S(2)}) collective-permute-start(bf16[32,1024]{1,0:T(8,128)(2,1)S(1)} %lookup.2), channel_id=1, source_target_pairs={{0,8},{1,9},{2,10},{3,11},{4,12},{5,13},{6,14},{7,15},{8,0},{9,1},... | collective-permute-start | bytes 196616 | tf_op jit(solution)/shard_map/ppermute | solution.py:40
  19.3 8.2 %collective-permute-start.13 = (bf16[32,1024]{1,0:T(8,128)(2,1)S(1)}, bf16[32,1024]{1,0:T(8,128)(2,1)S(1)}, u32[]{:S(2)}, u32[]{:S(2)}) collective-permute-start(bf16[32,1024]{1,0:T(8,128)(2,1)S(1)} %lookup.2), channel_id=1, source_target_pairs={{0,12},{1,13},{2,14},{3,15},{4,8},{5,9},{6,10},{7,11},{8,4},{9,5},... | collective-permute-start | bytes 196616 | tf_op jit(solution)/shard_map/ppermute | solution.py:40
  27.5 6.5 %collective-permute-start.14 = (bf16[128,1024]{1,0:T(8,128)(2,1)S(1)}, bf16[128,1024]{1,0:T(8,128)(2,1)S(1)}, u32[]{:S(2)}, u32[]{:S(2)}) collective-permute-start(bf16[128,1024]{1,0:T(8,128)(2,1)S(1)} %pad_maximum_fusion.1), channel_id=1, source_target_pairs={{0,2},{1,3},{2,0},{3,1},{4,6},{5,7},{6,4},{7,5},{8,10},{9,11},{10,... | collective-permute-start | bytes 786440 | tf_op jit(solution)/shard_map/ppermute | solution.py:40
  34.0 3.2 %collective-permute-start.15 = (bf16[256,1024]{1,0:T(8,128)(2,1)S(1)}, bf16[256,1024]{1,0:T(8,128)(2,1)S(1)}, u32[]{:S(2)}, u32[]{:S(2)}) collective-permute-start(bf16[256,1024]{1,0:T(8,128)(2,1)S(1)} %get-tuple-element.72), channel_id=1, source_target_pairs={{0,1},{1,0},{2,3},{3,2},{4,5},{5,4},{6,7},{7,6},{8,9},{9,8},{10,11... | collective-permute-start | bytes 1572872 | tf_op jit(solution)/shard_map/ppermute | solution.py:40
  38.5 1.6 %copy-start.2 = (bf16[1024,1024]{1,0:T(8,128)(2,1)S(1)}, bf16[1024,1024]{1,0:T(8,128)(2,1)}, u32[]{:S(2)}) copy-start(bf16[1024,1024]{1,0:T(8,128)(2,1)} %key_ref.1) | copy-start | bytes 6291460
  38.5 1.6 %copy-start.4 = (f32[1024]{0:T(1024)S(1)}, f32[1024]{0:T(1024)}, u32[]{:S(2)}) copy-start(f32[1024]{0:T(1024)} %param.20) | copy-start | bytes 12292
  40.1 2.2 %copy-start = (bf16[1024,2048]{1,0:T(8,128)(2,1)S(1)}, bf16[1024,2048]{1,0:T(8,128)(2,1)}, u32[]{:S(2)}) copy-start(bf16[1024,2048]{1,0:T(8,128)(2,1)} %proj_ref.3) | copy-start | bytes 12582916
  42.3 1.6 %copy-start.3 = (bf16[1024,1024]{1,0:T(8,128)(2,1)S(1)}, bf16[1024,1024]{1,0:T(8,128)(2,1)}, u32[]{:S(2)}) copy-start(bf16[1024,1024]{1,0:T(8,128)(2,1)} %value_ref.1) | copy-start | bytes 6291460
  50.7 1.7 %collective-permute-start.16 = (bf16[128,1024]{1,0:T(8,128)(2,1)S(1)}, bf16[128,1024]{1,0:T(8,128)(2,1)S(1)}, u32[]{:S(2)}, u32[]{:S(2)}) collective-permute-start(bf16[128,1024]{1,0:T(8,128)(2,1)S(1)} %get-tuple-element.47), channel_id=1, source_target_pairs={{0,1},{1,0},{2,3},{3,2},{4,5},{5,4},{6,7},{7,6},{8,9},{9,8},{10,11... | collective-permute-start | bytes 786440 | tf_op jit(solution)/shard_map/ppermute | solution.py:40
  52.5 5.8 %collective-permute-start.17 = (bf16[64,1024]{1,0:T(8,128)(2,1)S(1)}, bf16[64,1024]{1,0:T(8,128)(2,1)S(1)}, u32[]{:S(2)}, u32[]{:S(2)}) collective-permute-start(bf16[64,1024]{1,0:T(8,128)(2,1)S(1)} %slice.40), channel_id=1, source_target_pairs={{0,2},{1,3},{2,0},{3,1},{4,6},{5,7},{6,4},{7,5},{8,10},{9,11},{10,... | collective-permute-start | bytes 393224 | tf_op jit(solution)/shard_map/ppermute | solution.py:40
  58.4 6.5 %collective-permute-start.18 = (bf16[16,1024]{1,0:T(8,128)(2,1)S(1)}, bf16[16,1024]{1,0:T(8,128)(2,1)S(1)}, u32[]{:S(2)}, u32[]{:S(2)}) collective-permute-start(bf16[16,1024]{1,0:T(8,128)(2,1)S(1)} %get-tuple-element.76), channel_id=1, source_target_pairs={{0,4},{1,5},{2,6},{3,7},{4,0},{5,1},{6,2},{7,3},{8,12},{9,13},{10,... | collective-permute-start | bytes 98312 | tf_op jit(solution)/shard_map/ppermute | solution.py:40
  61.2 4.9 %collective-permute-start.19 = (bf16[16,1024]{1,0:T(8,128)(2,1)S(1)}, bf16[16,1024]{1,0:T(8,128)(2,1)S(1)}, u32[]{:S(2)}, u32[]{:S(2)}) collective-permute-start(bf16[16,1024]{1,0:T(8,128)(2,1)S(1)} %get-tuple-element.75), channel_id=1, source_target_pairs={{0,8},{1,9},{2,10},{3,11},{4,12},{5,13},{6,14},{7,15},{8,0},{9,1},... | collective-permute-start | bytes 98312 | tf_op jit(solution)/shard_map/ppermute | solution.py:40
  61.4 5.7 %collective-permute-start.20 = (bf16[16,1024]{1,0:T(8,128)(2,1)S(1)}, bf16[16,1024]{1,0:T(8,128)(2,1)S(1)}, u32[]{:S(2)}, u32[]{:S(2)}) collective-permute-start(bf16[16,1024]{1,0:T(8,128)(2,1)S(1)} %get-tuple-element.74), channel_id=1, source_target_pairs={{0,12},{1,13},{2,14},{3,15},{4,8},{5,9},{6,10},{7,11},{8,4},{9,5},... | collective-permute-start | bytes 98312 | tf_op jit(solution)/shard_map/ppermute | solution.py:40
  64.4 2.7 %copy-start.1 = (bf16[1024,1024]{1,0:T(8,128)(2,1)S(1)}, bf16[1024,1024]{1,0:T(8,128)(2,1)}, u32[]{:S(2)}) copy-start(bf16[1024,1024]{1,0:T(8,128)(2,1)} %refs_6_.1) | copy-start | bytes 6291460
  64.4 2.7 %copy-start.7 = (f32[1024]{0:T(1024)S(1)}, f32[1024]{0:T(1024)}, u32[]{:S(2)}) copy-start(f32[1024]{0:T(1024)} %param.24) | copy-start | bytes 12292

commit v2 on v1

--- a/solution.py
+++ b/solution.py
@@ -6,6 +6,7 @@
 from jax.experimental import pallas as pl
 from jax.experimental.pallas import tpu as pltpu
 from jax.sharding import PartitionSpec as P
+
 
 BF16 = jnp.bfloat16
 F32 = jnp.float32
@@ -15,6 +16,7 @@
 NT = (((1,), (1,)), ((), ()))
 VMEM = pl.BlockSpec(memory_space=pltpu.VMEM)
 SMEM = pl.BlockSpec(memory_space=pltpu.SMEM)
+HBM = pl.BlockSpec(memory_space=pltpu.HBM)
 
 
 def params(mib):
@@ -41,9 +43,12 @@
 
 
 def gather_relative(x, dim, axis, size, joined_tail):
-    for bits in stage_masks(size, joined_tail):
-        x = jnp.concatenate([x] + [swap(x, m, axis, size) for m in combos(bits)[1:]], axis=dim)
-    return x
+    stages = stage_masks(size, joined_tail)
+    for bits in stages:
+        pieces = [x] + [swap(x, m, axis, size) for m in combos(bits)[1:]]
+        if bits is not stages[-1]:
+            x = jnp.concatenate(pieces, axis=dim)
+    return pieces
 
 
 def position_bits(size):
@@ -54,10 +59,10 @@
     return jnp.max(ranks) // slots + 1
 
 
-def candidates_info(ids_ref, me, size, table_rows):
-    count = ids_ref.shape[1]
+def candidates_info(ids_refs, me, size, table_rows):
+    ids = jnp.concatenate([r[...] for r in ids_refs], axis=1)
+    count = ids.shape[1]
     each = count // size
-    ids = ids_ref[...]
     owner = ids // table_rows
     place = lax.broadcasted_iota(jnp.int32, (1, count), 1)
     block = place // each
@@ -75,12 +80,15 @@
     return jnp.sum(jnp.where(r == c, row, 0), axis=1, keepdims=True)
 
 
-def lookup_kernel(place_ref, ids_ref, table_ref, out_ref, *, size):
+def lookup_kernel(place_ref, *refs, size):
+    *ids_refs, table_hbm, out_ref, table_ref, sem = refs
+    copy = pltpu.make_async_copy(table_hbm, table_ref, sem)
+    copy.start()
     me, turn = place_ref[0], place_ref[1]
     slots = out_ref.shape[0]
     rows = table_ref.shape[0]
-    count = ids_ref.shape[1]
-    owner, key, offset = candidates_info(ids_ref, me, size, rows)
+    owner, key, offset = candidates_info(ids_refs, me, size, rows)
+    count = owner.shape[1]
     key_col = to_column(key)
     before = (key_col < key) & (key_col >= owner * count)
     rank = jnp.sum(before.astype(jnp.int32), axis=0, keepdims=True)
@@ -88,6 +96,7 @@
     hit = (owner == me) & (rank == slot)
     want = jnp.sum(jnp.where(hit, offset + 1, 0), axis=1, keepdims=True) - 1
     pick = (want == lax.broadcasted_iota(jnp.int32, (slots, rows), 1)).astype(F32).astype(BF16)
+    copy.wait()
     out_ref[...] = jnp.dot(pick, table_ref[...], preferred_element_type=F32).astype(BF16)
 
 
@@ -95,17 +104,19 @@
     return pl.pallas_call(
         functools.partial(lookup_kernel, size=size),
         out_shape=jax.ShapeDtypeStruct((slots, table.shape[1]), BF16),
-        in_specs=[SMEM, VMEM, VMEM],
+        in_specs=[SMEM] + [VMEM] * len(ids) + [HBM],
         out_specs=VMEM,
+        scratch_shapes=[pltpu.VMEM(table.shape, BF16), pltpu.SemaphoreType.DMA],
         compiler_params=params(24),
         name="lookup",
-    )(place, ids, table)
-
-
-def plan_kernel(place_ref, ids_ref, pick_ref, rounds_ref, *, size, slots, table_rows):
+    )(place, *ids, table)
+
+
+def plan_kernel(place_ref, *refs, size, slots, table_rows):
+    *ids_refs, pick_ref, rounds_ref = refs
     me, turn = place_ref[0], place_ref[1]
-    count = ids_ref.shape[1]
-    owner, key, _ = candidates_info(ids_ref, me, size, table_rows)
+    owner, key, _ = candidates_info(ids_refs, me, size, table_rows)
+    count = owner.shape[1]
     key_col = to_column(key)
     owner_col = key_col // count
     before = (key < key_col) & (key >= owner_col * count)
@@ -122,26 +133,27 @@
 
 
 def plan(place, ids, slots, table_rows, size):
-    count = ids.shape[1]
+    count = sum(i.shape[1] for i in ids)
     return pl.pallas_call(
         functools.partial(plan_kernel, size=size, slots=slots, table_rows=table_rows),
         out_shape=(
             jax.ShapeDtypeStruct((count, size * slots), BF16),
             jax.ShapeDtypeStruct((1,), jnp.int32),
         ),
-        in_specs=[SMEM, VMEM],
+        in_specs=[SMEM] + [VMEM] * len(ids),
         out_specs=(VMEM, SMEM),
         compiler_params=params(40),
         cost_estimate=pl.CostEstimate(flops=1 << 22, transcendentals=0, bytes_accessed=1 << 20),
         name="plan",
-    )(place, ids)
+    )(place, *ids)
 
 
 def select_kernel(pick_ref, rows_ref, out_ref):
     out_ref[...] = jnp.dot(pick_ref[...], rows_ref[...], preferred_element_type=F32).astype(BF16)
 
 
-def select(pick, rows):
+def select(pick, pieces):
+    rows = jnp.concatenate(pieces, axis=0)
     return pl.pallas_call(
         select_kernel,
         out_shape=jax.ShapeDtypeStruct((pick.shape[0], rows.shape[1]), BF16),
@@ -202,24 +214,49 @@
 
 
 def attend_kernel(
-    emb_ref, gain_ref, proj_ref, key_ref, value_ref, bias_ref, keep_ref, send_ref, query_ref, *, heads
+    rounds_ref, pick_ref, near_ref, far_ref, extra_hbm, gain_ref, proj_hbm, key_hbm, value_hbm, bias_ref,
+    own_ref, keep_ref, send_ref, emb_ref, query_ref, proj_ref, key_ref, value_ref, sems, *, heads
 ):
     count, width = emb_ref.shape
+    copies = [
+        pltpu.make_async_copy(proj_hbm.at[:, pl.ds(0, width)], proj_ref, sems.at[0]),
+        pltpu.make_async_copy(key_hbm, key_ref, sems.at[1]),
+        pltpu.make_async_copy(value_hbm, value_ref, sems.at[2]),
+    ]
+    for c in copies:
+        c.start()
+    split = near_ref.shape[0]
+    picked = jnp.dot(pick_ref[:, :split], near_ref[...], preferred_element_type=F32)
+    picked = picked + jnp.dot(pick_ref[:, split:], far_ref[...], preferred_element_type=F32)
+    emb_ref[...] = picked.astype(BF16)
+
+    @pl.when(rounds_ref[0] > 1)
+    def _():
+        extra = pltpu.make_async_copy(extra_hbm, query_ref, sems.at[3])
+        extra.start()
+        extra.wait()
+        emb_ref[...] = emb_ref[...] + query_ref[...]
+
+    own_ref[...] = emb_ref[: own_ref.shape[0], :]
     head_dim = width // heads
     events = key_ref.shape[0]
     half = count // 2
     rows = min(ROWS_AT_ONCE, count)
     per = LANES // head_dim
     step = min(EVENTS_AT_ONCE, events)
+    copies[0].wait()
     for first in range(0, count, rows):
         normed = normalise(emb_ref[first : first + rows, :], gain_ref[...])
-        projected = jnp.dot(normed, proj_ref[:, :width], preferred_element_type=F32)
+        projected = jnp.dot(normed, proj_ref[...], preferred_element_type=F32)
         query = silu(projected).astype(BF16)
-        query_ref[...] = query * jnp.asarray(0.5 * head_dim**-0.5, BF16)
+        query_ref[first : first + rows, :] = query * jnp.asarray(0.5 * head_dim**-0.5, BF16)
+        if first == 0:
+            copies[1].wait()
+            copies[2].wait()
         lane = lax.broadcasted_iota(jnp.int32, (rows, LANES), 1)
         for group in range(heads // per):
             at = slice(group * LANES, (group + 1) * LANES)
-            part = query_ref[:, at]
+            part = query_ref[first : first + rows, at]
             zero, one = jnp.zeros_like(part), jnp.ones_like(part)
             stacked = []
             for k in range(per):
@@ -245,31 +282,38 @@
                 send_ref[: first + rows - half, at] = out[half - first :].astype(BF16)
 
 
-def attend(embedded, gain, proj_in, keys, values, bias, heads):
-    count, width = embedded.shape
+def attend(rounds, pick, near, far, extra, gain, proj_in, keys, values, bias, heads, each):
+    count, width = extra.shape
     return pl.pallas_call(
         functools.partial(attend_kernel, heads=heads),
         out_shape=(
+            jax.ShapeDtypeStruct((each, width), BF16),
             jax.ShapeDtypeStruct((count // 2, width), F32),
             jax.ShapeDtypeStruct((count // 2, width), BF16),
         ),
-        in_specs=[VMEM] * 6,
-        out_specs=(VMEM, VMEM),
-        scratch_shapes=[pltpu.VMEM((min(ROWS_AT_ONCE, count), width), BF16)],
-        compiler_params=params(40),
+        in_specs=[SMEM, VMEM, VMEM, VMEM, HBM, VMEM, HBM, HBM, HBM, VMEM],
+        out_specs=(VMEM, VMEM, VMEM),
+        scratch_shapes=[
+            pltpu.VMEM((count, width), BF16),
+            pltpu.VMEM((count, width), BF16),
+            pltpu.VMEM((width, width), BF16),
+            pltpu.VMEM(keys.shape, BF16),
+            pltpu.VMEM(values.shape, BF16),
+            pltpu.SemaphoreType.DMA((4,)),
+        ],
+        compiler_params=params(48),
         cost_estimate=pl.CostEstimate(
             flops=8 * count * width * keys.shape[0],
             transcendentals=count * heads * keys.shape[0],
             bytes_accessed=4 * keys.size,
         ),
         name="attend",
-    )(embedded, gain, proj_in, keys, values, bias)
+    )(rounds, pick, near, far, extra, gain, proj_in, keys, values, bias)
 
 
 def gates_kernel(emb_ref, gain_ref, proj_ref, out_ref):
-    width = emb_ref.shape[1]
     normed = normalise(emb_ref[...], gain_ref[...])
-    projected = jnp.dot(normed, proj_ref[:, width:], preferred_element_type=F32)
+    projected = jnp.dot(normed, proj_ref[...], preferred_element_type=F32)
     out_ref[...] = silu(projected).astype(BF16)
 
 
@@ -277,7 +321,8 @@
     return pl.pallas_call(
         gates_kernel,
         out_shape=jax.ShapeDtypeStruct(embedded.shape, BF16),
-        in_specs=[VMEM] * 3,
+        grid=(1,),
+        in_specs=[VMEM, VMEM, pl.BlockSpec(proj_in.shape[:1] * 2, lambda i: (0, 1))],
         out_specs=VMEM,
         compiler_params=params(16),
         cost_estimate=pl.CostEstimate(flops=1 << 26, transcendentals=1 << 14, bytes_accessed=1 << 22),
@@ -349,23 +394,23 @@
     ids = gather_relative(item_ids[None, :], 1, axis, size, True)
 
     def fetch(turn):
-        return gather_relative(
-            lookup(place(turn), ids, item_table, slots, size), 0, axis, size, False
-        )
-
-    rows = fetch(0)
+        found = lookup(place(turn), ids, item_table, slots, size)
+        return gather_relative(found, 0, axis, size, False)
+
+    near, far = fetch(0)
     pick, rounds = plan(here, ids, slots, table_rows, size)
-    embedded = select(pick, rows)
 
     def more(state):
         turn, so_far = state
         picked, _ = plan(place(turn), ids, slots, table_rows, size)
         return turn + 1, so_far + select(picked, fetch(turn))
 
-    _, embedded = lax.while_loop(lambda s: s[0] < rounds[0], more, (jnp.int32(1), embedded))
-
-    keep, send = attend(embedded, gain, proj_in, key_cache, value_cache, bias, heads)
-    own = embedded[:each]
+    none = jnp.zeros((each * size, item_table.shape[1]), BF16)
+    _, extra = lax.while_loop(lambda s: s[0] < rounds[0], more, (jnp.int32(1), none))
+
+    own, keep, send = attend(
+        rounds, pick, near, far, extra, gain, proj_in, key_cache, value_cache, bias, heads, each
+    )
     gates = gates_of(own, gain, proj_in)
 
     stages = stage_masks(size, False)[::-1]
@@ -399,6 +444,5 @@
         P(),
         P(),
     )
-    return jax.shard_map(
-        on_device, mesh=mesh, in_specs=placed, out_specs=P(("grp", "hist"), None), check_vma=False
-    )
+
+    return jax.shard_map(on_device, mesh=mesh, in_specs=placed, out_specs=P(("grp", "hist"), None), check_vma=False)

time: 68.7 us -> 65.5 us (0.953)
  waiting for transfers between devices: 25.8 us -> 18.9 us
  Pallas kernels: 14.4 us -> 16.4 us
  local copies, waits for them, and re-layouts: 6.26 us -> 7.43 us
  starting transfers between devices: 19.2 us -> 19.9 us
    ppermute x16, waiting for transfers between devices: 25.8 us -> 18.9 us  [swap(): return lax.ppermute(x, axis, [(i, i ^ mask) for i in range(size)])]
    pallas_call x1, Pallas kernels: 6.78 us -> 9.68 us  [attend(): pl.pallas_call(functools.partial(attend_kernel, heads=heads), out_shape=(...]
    pallas_call x1 -> x0, Pallas kernels: 1.28 us -> none  [select(): pl.pallas_call(select_kernel, out_shape=jax.ShapeDtypeStruct((pick.shape[...]
    broadcast_in_dim x0 -> x1, local copies, waits for them, and re-layouts: none -> 0.86 us  [on_device(): none = jnp.zeros((each * size, item_table.shape[1]), BF16)]
    slice x1 -> x0, local copies, waits for them, and re-layouts: 0.76 us -> none  [on_device(): own = embedded[:each]]
    ppermute x16, starting transfers between devices: 19.2 us -> 19.9 us  [swap(): return lax.ppermute(x, axis, [(i, i ^ mask) for i in range(size)])]
    pad x1, local copies, waits for them, and re-layouts: 0.01 us -> 0.7 us  [on_device(): jnp.pad(pos_bias, ((0, 0), (0, -npos % 32)))]
  transfers between devices with their start and end apart: 16 -> 16, of which waited for: 11 -> 9; matrix products, arithmetic and copies ran while one was open for 1% -> 6% of each run, Pallas kernels for 4% -> 4%
where the time goes in v2:
time: 65.5 us; the launch traced here: 65.2 us
  starting transfers between devices  19.9 us (30%)
  waiting for transfers between devices  18.9 us (29%)
  Pallas kernels  16.4 us (25%)
  local copies, waits for them, and re-layouts  7.43 us (11%)
  other arithmetic  0.91 us (1%)
  between operations  0.83 us (1%)
  loops' own time  0.78 us (1%)
    ppermute x16, starting transfers between devices, swap(): return lax.ppermute(x, axis, [(i, i ^ mask) for i in range(size)])  19.9 us
    ppermute x16, waiting for transfers between devices, swap(): return lax.ppermute(x, axis, [(i, i ^ mask) for i in range(size)])  18.9 us
    pallas_call x1, Pallas kernels, attend(): pl.pallas_call(functools.partial(attend_kernel, heads=heads), out_shape=(...  9.68 us
    unnamed x22, local copies, waits for them, and re-layouts  5.11 us
    pallas_call x1, Pallas kernels, lookup(): pl.pallas_call(functools.partial(lookup_kernel, size=size), out_shape=jax...  2.61 us
    pallas_call x1, Pallas kernels, plan(): pl.pallas_call(functools.partial(plan_kernel, size=size, slots=slots, tab...  1.59 us
  transfers between devices with their start and end apart: 16, of which 9 were waited for; matrix products, arithmetic and copies ran while one was open for 6% of the time, Pallas kernels for 4%

profile of v2, /device:TPU:0, one launch (start us, length us, event | category | flops | bytes accessed | tf_op | source)
XLA Modules:
  0.0 65.2 jit_solution(15589480561722210522)
XLA Ops:
  0.0 3.1 %collective-permute-start.5 = (s32[1,16]{1,0:T(1,128)}, s32[1,16]{1,0:T(1,128)S(1)}, u32[]{:S(2)}, u32[]{:S(2)}) collective-permute-start(s32[1,16]{1,0:T(1,128)} %bitcast.17), channel_id=1, source_target_pairs={{0,4},{1,5},{2,6},{3,7},{4,0},{5,1},{6,2},{7,3},{8,12},{9,13},{10,... | collective-permute-start | bytes 200 | tf_op jit(solution)/shard_map/ppermute | solution.py:42
  3.1 2.6 %collective-permute-start.6 = (s32[1,16]{1,0:T(1,128)}, s32[1,16]{1,0:T(1,128)S(1)}, u32[]{:S(2)}, u32[]{:S(2)}) collective-permute-start(s32[1,16]{1,0:T(1,128)} %bitcast.18), channel_id=1, source_target_pairs={{0,8},{1,9},{2,10},{3,11},{4,12},{5,13},{6,14},{7,15},{8,0},{9,1},... | collective-permute-start | bytes 200 | tf_op jit(solution)/shard_map/ppermute | solution.py:42
  5.6 0.0 collective-permute-start.7
  6.3 0.1 pad_add_fusion.1.place_ref
  6.4 0.7 %pad.4.pos_bias_ref = f32[16,32]{1,0:T(8,128)S(1)} pad(f32[16,18]{1,0:T(8,128)} %param.23, f32[]{:T(128)} %constant.14.clone.1), padding=0_0x0_14 | pad | bytes 3204 | tf_op jit(solution)/shard_map/jit(_pad)/pad | solution.py:390
  7.1 0.0 collective-permute-done.5
  7.1 0.6 collective-permute-done.6
  7.7 3.5 %collective-permute-done.7 = s32[1,16]{1,0:T(1,128)S(1)} collective-permute-done((s32[1,16]{1,0:T(1,128)}, s32[1,16]{1,0:T(1,128)S(1)}, u32[]{:S(2)}, u32[]{:S(2)}) %collective-permute-start.7) | collective-permute-done | bytes 96 | tf_op jit(solution)/shard_map/ppermute | solution.py:42
  11.1 0.7 %pad_add_fusion.2.refs_0_ = s32[1,64]{1,0:T(1,128)S(1)} fusion(s32[1,16]{1,0:T(1,128)S(1)} %collective-permute-done.7, s32[1,16]{1,0:T(1,128)S(1)} %collective-permute-done.6, s32[1,16]{1,0:T(1,128)S(1)} %collective-permute-done.5, s32[1,16]{1,0:T(1,128)} %bitcast.20), kind=kLoop, calls=%fused_computation.23 | loop fusion | flops 192 | bytes 512 | tf_op jit(solution)/shard_map/concatenate | solution.py:50
  11.9 0.0 collective-permute-start.10
  11.9 1.6 %collective-permute-start.8 = (s32[1,64]{1,0:T(1,128)S(1)}, s32[1,64]{1,0:T(1,128)S(1)}, u32[]{:S(2)}, u32[]{:S(2)}) collective-permute-start(s32[1,64]{1,0:T(1,128)S(1)} %pad_add_fusion.2.refs_0_), channel_id=1, source_target_pairs={{0,2},{1,3},{2,0},{3,1},{4,6},{5,7},{6,4},{7,5},{8,10},{9,11},{10,... | collective-permute-start | bytes 776 | tf_op jit(solution)/shard_map/ppermute | solution.py:42
  13.5 0.3 collective-permute-start.9
  13.7 0.0 copy-start.6
  13.7 0.7 %copy-done.6 = f32[16,128]{1,0:T(8,128)S(1)} copy-done((f32[16,128]{1,0:T(8,128)S(1)}, f32[16,128]{1,0:T(8,128)}, u32[]{:S(2)}) %copy-start.6) | copy-done | bytes 8216
  14.4 0.0 copy-start.7
  14.4 0.7 %copy-done.7 = s32[1024]{0:T(1024)S(1)} copy-done((s32[1024]{0:T(1024)S(1)}, s32[1024]{0:T(1024)}, u32[]{:S(2)}) %copy-start.7) | copy-done | bytes 4120
  15.1 0.9 %bias.1.bias_ref = bf16[1024,128]{1,0:T(8,128)(2,1)S(1)} custom-call(s32[2]{0:T(128)S(1)} %pad_add_fusion.1.place_ref, s32[1]{0:T(128)S(6)} %copy.32.start_ref, s32[1,1024]{1,0:T(1,128)S(1)} %bitcast.15, f32[16,128]{1,0:T(8,128)S(1)} %copy-done.6, f32[16,32]{1,0:T(8,128)S(1)} %pad.4.pos_bias_ref), custom_call_target="tpu_custom_call" | custom-call | flops 33554432 | bytes 1048576 | tf_op jit(solution)/shard_map/bias/pallas_call | solution.py:195
  16.0 0.0 collective-permute-done.10.refs_3_
  16.0 0.0 collective-permute-done.8.refs_1_
  16.0 0.0 collective-permute-done.9.refs_2_
  16.0 2.6 %lookup.2 = bf16[32,1024]{1,0:T(8,128)(2,1)S(1)} custom-call(s32[2]{0:T(128)S(1)} %pad_add_fusion.1.place_ref, s32[1,64]{1,0:T(1,128)S(1)} %pad_add_fusion.2.refs_0_, s32[1,64]{1,0:T(1,128)S(1)} %collective-permute-done.8.refs_1_, s32[1,64]{1,0:T(1,128)S(1)} %collective-permute-done.9.refs_2_, s32[1,64]{1,0:T(1,128)S(1)} %collective-permute-done.10.refs_3_, ...), custom_call_target="tpu_custom_call" | custom-call | tf_op jit(solution)/shard_map/lookup/pallas_call | solution.py:104
  18.7 0.1 collective-permute-start.11
  18.7 0.6 collective-permute-start.12
  19.3 3.8 %collective-permute-start.13 = (bf16[32,1024]{1,0:T(8,128)(2,1)S(1)}, bf16[32,1024]{1,0:T(8,128)(2,1)S(1)}, u32[]{:S(2)}, u32[]{:S(2)}) collective-permute-start(bf16[32,1024]{1,0:T(8,128)(2,1)S(1)} %lookup.2), channel_id=1, source_target_pairs={{0,12},{1,13},{2,14},{3,15},{4,8},{5,9},{6,10},{7,11},{8,4},{9,5},... | collective-permute-start | bytes 196616 | tf_op jit(solution)/shard_map/ppermute | solution.py:42
  23.1 1.6 %plan.2 = (bf16[256,512]{1,0:T(8,128)(2,1)S(1)}, s32[1]{0:T(128)}) custom-call(s32[2]{0:T(128)S(1)} %pad_add_fusion.1.place_ref, s32[1,64]{1,0:T(1,128)S(1)} %pad_add_fusion.2.refs_0_, s32[1,64]{1,0:T(1,128)S(1)} %collective-permute-done.8.refs_1_, s32[1,64]{1,0:T(1,128)S(1)} %collective-permute-done.9.refs_2_, s32[1,64]{1,0:T(1,128)S(1)} %collective-permute-done.10.refs_3_), custom_call_target="tpu_custom_call" | custom-call | flops 4194304 | bytes 1048576 | tf_op jit(solution)/shard_map/plan/pallas_call | solution.py:137
  24.7 0.0 copy-start.3
  24.7 0.7 %constant_dynamic-update-slice_fusion.15 = bf16[256,1024]{1,0:T(8,128)(2,1)} fusion(bf16[32,1024]{1,0:T(8,128)(2,1)S(1)} %lookup.2), kind=kLoop, calls=%fused_computation.21 | loop fusion | bytes 131072
  25.4 0.0 collective-permute-done.11
  25.4 2.1 %collective-permute-done.12 = bf16[32,1024]{1,0:T(8,128)(2,1)S(1)} collective-permute-done((bf16[32,1024]{1,0:T(8,128)(2,1)S(1)}, bf16[32,1024]{1,0:T(8,128)(2,1)S(1)}, u32[]{:S(2)}, u32[]{:S(2)}) %collective-permute-start.12) | collective-permute-done | bytes 65568 | tf_op jit(solution)/shard_map/ppermute | solution.py:42
  27.5 0.0 collective-permute-done.13
  27.5 1.3 %collective-permute-start.14 = (bf16[128,1024]{1,0:T(8,128)(2,1)S(1)}, bf16[128,1024]{1,0:T(8,128)(2,1)S(1)}, u32[]{:S(2)}, u32[]{:S(2)}) collective-permute-start(bf16[128,1024]{1,0:T(8,128)(2,1)S(1)} %pad_maximum_fusion.1), channel_id=1, source_target_pairs={{0,2},{1,3},{2,0},{3,1},{4,6},{5,7},{6,4},{7,5},{8,10},{9,11},{10,... | collective-permute-start | bytes 786440 | tf_op jit(solution)/shard_map/ppermute | solution.py:42
  28.8 0.6 constant_dynamic-update-slice_fusion.14
  29.5 0.6 constant_dynamic-update-slice_fusion.13
  30.1 0.6 constant_dynamic-update-slice_fusion.12
  30.7 3.2 %collective-permute-done.14 = bf16[128,1024]{1,0:T(8,128)(2,1)S(1)} collective-permute-done((bf16[128,1024]{1,0:T(8,128)(2,1)S(1)}, bf16[128,1024]{1,0:T(8,128)(2,1)S(1)}, u32[]{:S(2)}, u32[]{:S(2)}) %collective-permute-start.14) | collective-permute-done | bytes 262176 | tf_op jit(solution)/shard_map/ppermute | solution.py:42
  33.9 0.7 %constant_dynamic-update-slice_fusion.11.near_ref = bf16[256,1024]{1,0:T(8,128)(2,1)} fusion(bf16[256,1024]{1,0:T(8,128)(2,1)} %constant_dynamic-update-slice_fusion.12, bf16[128,1024]{1,0:T(8,128)(2,1)S(1)} %collective-permute-done.14), kind=kLoop, calls=%fused_computation.17 | loop fusion | bytes 524288 | tf_op jit(solution)/shard_map/concatenate | solution.py:50
  34.6 0.0 collective-permute-start.15
  34.7 0.9 %broadcast_in_dim.16 = bf16[256,1024]{1,0:T(8,128)(2,1)} broadcast(bf16[]{:T(256)} %constant.6.clone.1), dimensions={} | broadcast | bytes 524290 | tf_op jit(solution)/shard_map/broadcast_in_dim | solution.py:408
  35.5 0.0 copy-done.3
  35.5 0.0 copy-start.1
  35.5 0.8 %while.10 = (s32[]{:T(128)}, bf16[256,1024]{1,0:T(8,128)(2,1)}, s32[1]{0:T(128)}, s32[]{:T(128)}, s32[1,64]{1,0:T(1,128)S(1)}, /*index=5*/s32[1,64]{1,0:T(1,128)...) while((s32[]{:T(128)}, bf16[256,1024]{1,0:T(8,128)(2,1)}, ...), condition=%wide.region_1.2_spmd, body=%wide.region_0.1_spmd.sunk | while | flops 5505028 | bytes 13894005 | solution.py:409
  36.3 0.6 collective-permute-done.15.far_ref
  36.9 0.2 copy-done.1
  37.1 0.0 copy-done.5
  37.1 0.0 copy-start.4
  37.1 0.9 %copy-done.4 = bf16[256,512]{1,0:T(8,128)(2,1)S(1)} copy-done((bf16[256,512]{1,0:T(8,128)(2,1)S(1)}, bf16[256,512]{1,0:T(8,128)(2,1)}, u32[]{:S(2)}) %copy-start.4) | copy-done | bytes 262168
  38.1 0.0 copy-start
  38.1 9.7 %attend.1 = (bf16[16,1024]{1,0:T(8,128)(2,1)S(1)}, f32[128,1024]{1,0:T(8,128)S(1)}, bf16[128,1024]{1,0:T(8,128)(2,1)S(1)}) custom-call(s32[1]{0:T(128)} %get-tuple-element.178.rounds_ref, bf16[256,512]{1,0:T(8,128)(2,1)S(1)} %copy-done.4, bf16[256,1024]{1,0:T(8,128)(2,1)} %constant_dynamic-update-slice_fusion.11.near_ref, ...), custom_call_target="tpu_custom_call" | custom-call | flops 2147483648 | bytes 4194304 | tf_op jit(solution)/shard_map/attend/pallas_call | solution.py:287
  47.8 0.6 collective-permute-start.16
  48.3 1.2 %collective-permute-done.16 = bf16[128,1024]{1,0:T(8,128)(2,1)S(1)} collective-permute-done((bf16[128,1024]{1,0:T(8,128)(2,1)S(1)}, bf16[128,1024]{1,0:T(8,128)(2,1)S(1)}, u32[]{:S(2)}, u32[]{:S(2)}) %collective-permute-start.16) | collective-permute-done | bytes 262176 | tf_op jit(solution)/shard_map/ppermute | solution.py:42
  49.5 0.1 convert_add_fusion
  49.6 1.3 %collective-permute-start.17 = (bf16[64,1024]{1,0:T(8,128)(2,1)S(1)}, bf16[64,1024]{1,0:T(8,128)(2,1)S(1)}, u32[]{:S(2)}, u32[]{:S(2)}) collective-permute-start(bf16[64,1024]{1,0:T(8,128)(2,1)S(1)} %slice.36), channel_id=1, source_target_pairs={{0,2},{1,3},{2,0},{3,1},{4,6},{5,7},{6,4},{7,5},{8,10},{9,11},{10,... | collective-permute-start | bytes 393224 | tf_op jit(solution)/shard_map/ppermute | solution.py:42
  50.9 4.5 %collective-permute-done.17 = bf16[64,1024]{1,0:T(8,128)(2,1)S(1)} collective-permute-done((bf16[64,1024]{1,0:T(8,128)(2,1)S(1)}, bf16[64,1024]{1,0:T(8,128)(2,1)S(1)}, u32[]{:S(2)}, u32[]{:S(2)}) %collective-permute-start.17) | collective-permute-done | bytes 131104 | tf_op jit(solution)/shard_map/ppermute | solution.py:42
  55.5 2.3 %collective-permute-start.18 = (bf16[16,1024]{1,0:T(8,128)(2,1)S(1)}, bf16[16,1024]{1,0:T(8,128)(2,1)S(1)}, u32[]{:S(2)}, u32[]{:S(2)}) collective-permute-start(bf16[16,1024]{1,0:T(8,128)(2,1)S(1)} %get-tuple-element.97), channel_id=1, source_target_pairs={{0,4},{1,5},{2,6},{3,7},{4,0},{5,1},{6,2},{7,3},{8,12},{9,13},{10,... | collective-permute-start | bytes 98312 | tf_op jit(solution)/shard_map/ppermute | solution.py:42
  57.7 0.6 collective-permute-start.19
  58.3 1.9 %collective-permute-start.20 = (bf16[16,1024]{1,0:T(8,128)(2,1)S(1)}, bf16[16,1024]{1,0:T(8,128)(2,1)S(1)}, u32[]{:S(2)}, u32[]{:S(2)}) collective-permute-start(bf16[16,1024]{1,0:T(8,128)(2,1)S(1)} %get-tuple-element.95), channel_id=1, source_target_pairs={{0,12},{1,13},{2,14},{3,15},{4,8},{5,9},{6,10},{7,11},{8,4},{9,5},... | collective-permute-start | bytes 98312 | tf_op jit(solution)/shard_map/ppermute | solution.py:42
  60.2 0.0 copy-done
  60.2 0.5 gates.1.refs_4_
  60.7 0.0 collective-permute-done.18.refs_0_
  60.7 2.0 %collective-permute-done.19.refs_1_ = bf16[16,1024]{1,0:T(8,128)(2,1)S(1)} collective-permute-done((bf16[16,1024]{1,0:T(8,128)(2,1)S(1)}, bf16[16,1024]{1,0:T(8,128)(2,1)S(1)}, u32[]{:S(2)}, u32[]{:S(2)}) %collective-permute-start.19) | collective-permute-done | bytes 32800 | tf_op jit(solution)/shard_map/ppermute | solution.py:42
  62.7 1.3 %collective-permute-done.20.refs_2_ = bf16[16,1024]{1,0:T(8,128)(2,1)S(1)} collective-permute-done((bf16[16,1024]{1,0:T(8,128)(2,1)S(1)}, bf16[16,1024]{1,0:T(8,128)(2,1)S(1)}, u32[]{:S(2)}, u32[]{:S(2)}) %collective-permute-start.20) | collective-permute-done | bytes 32800 | tf_op jit(solution)/shard_map/ppermute | solution.py:42
  64.0 0.0 copy-done.2
  64.0 0.0 copy-done.8
  64.0 1.2 %finish.1 = bf16[16,1024]{1,0:T(8,128)(2,1)} custom-call(f32[16,1024]{1,0:T(8,128)S(1)} %slice.30.own_ref, bf16[16,1024]{1,0:T(8,128)(2,1)S(1)} %collective-permute-done.18.refs_0_, bf16[16,1024]{1,0:T(8,128)(2,1)S(1)} %collective-permute-done.19.refs_1_, bf16[16,1024]{1,0:T(8,128)(2,1)S(1)} %collective-permute-done.20.refs_2_, ...), custom_call_target="tpu_custom_call" | custom-call | tf_op jit(solution)/shard_map/finish/pallas_call | solution.py:346
  (8 shorter events, 0.1 us)
Async XLA Ops:
  0.0 7.1 %collective-permute-start.5 = (s32[1,16]{1,0:T(1,128)}, s32[1,16]{1,0:T(1,128)S(1)}, u32[]{:S(2)}, u32[]{:S(2)}) collective-permute-start(s32[1,16]{1,0:T(1,128)} %bitcast.17), channel_id=1, source_target_pairs={{0,4},{1,5},{2,6},{3,7},{4,0},{5,1},{6,2},{7,3},{8,12},{9,13},{10,... | collective-permute-start | bytes 200 | tf_op jit(solution)/shard_map/ppermute | solution.py:42
  3.1 4.6 %collective-permute-start.6 = (s32[1,16]{1,0:T(1,128)}, s32[1,16]{1,0:T(1,128)S(1)}, u32[]{:S(2)}, u32[]{:S(2)}) collective-permute-start(s32[1,16]{1,0:T(1,128)} %bitcast.18), channel_id=1, source_target_pairs={{0,8},{1,9},{2,10},{3,11},{4,12},{5,13},{6,14},{7,15},{8,0},{9,1},... | collective-permute-start | bytes 200 | tf_op jit(solution)/shard_map/ppermute | solution.py:42
  5.6 5.5 %collective-permute-start.7 = (s32[1,16]{1,0:T(1,128)}, s32[1,16]{1,0:T(1,128)S(1)}, u32[]{:S(2)}, u32[]{:S(2)}) collective-permute-start(s32[1,16]{1,0:T(1,128)} %bitcast.19), channel_id=1, source_target_pairs={{0,12},{1,13},{2,14},{3,15},{4,8},{5,9},{6,10},{7,11},{8,4},{9,5},... | collective-permute-start | bytes 200 | tf_op jit(solution)/shard_map/ppermute | solution.py:42
  11.9 4.1 %collective-permute-start.10 = (s32[1,64]{1,0:T(1,128)S(1)}, s32[1,64]{1,0:T(1,128)S(1)}, u32[]{:S(2)}, u32[]{:S(2)}) collective-permute-start(s32[1,64]{1,0:T(1,128)S(1)} %pad_add_fusion.2.refs_0_), channel_id=1, source_target_pairs={{0,3},{1,2},{2,1},{3,0},{4,7},{5,6},{6,5},{7,4},{8,11},{9,10},{10,... | collective-permute-start | bytes 776 | tf_op jit(solution)/shard_map/ppermute | solution.py:42
  11.9 4.1 %collective-permute-start.8 = (s32[1,64]{1,0:T(1,128)S(1)}, s32[1,64]{1,0:T(1,128)S(1)}, u32[]{:S(2)}, u32[]{:S(2)}) collective-permute-start(s32[1,64]{1,0:T(1,128)S(1)} %pad_add_fusion.2.refs_0_), channel_id=1, source_target_pairs={{0,2},{1,3},{2,0},{3,1},{4,6},{5,7},{6,4},{7,5},{8,10},{9,11},{10,... | collective-permute-start | bytes 776 | tf_op jit(solution)/shard_map/ppermute | solution.py:42
  13.5 2.6 %collective-permute-start.9 = (s32[1,64]{1,0:T(1,128)S(1)}, s32[1,64]{1,0:T(1,128)S(1)}, u32[]{:S(2)}, u32[]{:S(2)}) collective-permute-start(s32[1,64]{1,0:T(1,128)S(1)} %pad_add_fusion.2.refs_0_), channel_id=1, source_target_pairs={{0,1},{1,0},{2,3},{3,2},{4,5},{5,4},{6,7},{7,6},{8,9},{9,8},{10,11... | collective-permute-start | bytes 776 | tf_op jit(solution)/shard_map/ppermute | solution.py:42
  13.7 0.7 %copy-start.6 = (f32[16,128]{1,0:T(8,128)S(1)}, f32[16,128]{1,0:T(8,128)}, u32[]{:S(2)}) copy-start(f32[16,128]{1,0:T(8,128)} %time_bias_ref.1) | copy-start | bytes 24580
  14.4 0.7 %copy-start.7 = (s32[1024]{0:T(1024)S(1)}, s32[1024]{0:T(1024)}, u32[]{:S(2)}) copy-start(s32[1024]{0:T(1024)} %param.18) | copy-start | bytes 12292
  18.7 6.7 %collective-permute-start.11 = (bf16[32,1024]{1,0:T(8,128)(2,1)S(1)}, bf16[32,1024]{1,0:T(8,128)(2,1)S(1)}, u32[]{:S(2)}, u32[]{:S(2)}) collective-permute-start(bf16[32,1024]{1,0:T(8,128)(2,1)S(1)} %lookup.2), channel_id=1, source_target_pairs={{0,4},{1,5},{2,6},{3,7},{4,0},{5,1},{6,2},{7,3},{8,12},{9,13},{10,... | collective-permute-start | bytes 196616 | tf_op jit(solution)/shard_map/ppermute | solution.py:42
  18.7 8.7 %collective-permute-start.12 = (bf16[32,1024]{1,0:T(8,128)(2,1)S(1)}, bf16[32,1024]{1,0:T(8,128)(2,1)S(1)}, u32[]{:S(2)}, u32[]{:S(2)}) collective-permute-start(bf16[32,1024]{1,0:T(8,128)(2,1)S(1)} %lookup.2), channel_id=1, source_target_pairs={{0,8},{1,9},{2,10},{3,11},{4,12},{5,13},{6,14},{7,15},{8,0},{9,1},... | collective-permute-start | bytes 196616 | tf_op jit(solution)/shard_map/ppermute | solution.py:42
  19.3 8.1 %collective-permute-start.13 = (bf16[32,1024]{1,0:T(8,128)(2,1)S(1)}, bf16[32,1024]{1,0:T(8,128)(2,1)S(1)}, u32[]{:S(2)}, u32[]{:S(2)}) collective-permute-start(bf16[32,1024]{1,0:T(8,128)(2,1)S(1)} %lookup.2), channel_id=1, source_target_pairs={{0,12},{1,13},{2,14},{3,15},{4,8},{5,9},{6,10},{7,11},{8,4},{9,5},... | collective-permute-start | bytes 196616 | tf_op jit(solution)/shard_map/ppermute | solution.py:42
  24.7 10.8 %copy-start.3 = (bf16[256,512]{1,0:T(8,128)(2,1)}, bf16[256,512]{1,0:T(8,128)(2,1)S(1)}, u32[]{:S(2)}) copy-start(bf16[256,512]{1,0:T(8,128)(2,1)S(1)} %get-tuple-element.60.pick_ref) | copy-start | bytes 786436
  27.5 6.4 %collective-permute-start.14 = (bf16[128,1024]{1,0:T(8,128)(2,1)S(1)}, bf16[128,1024]{1,0:T(8,128)(2,1)S(1)}, u32[]{:S(2)}, u32[]{:S(2)}) collective-permute-start(bf16[128,1024]{1,0:T(8,128)(2,1)S(1)} %pad_maximum_fusion.1), channel_id=1, source_target_pairs={{0,2},{1,3},{2,0},{3,1},{4,6},{5,7},{6,4},{7,5},{8,10},{9,11},{10,... | collective-permute-start | bytes 786440 | tf_op jit(solution)/shard_map/ppermute | solution.py:42
  34.6 2.3 %collective-permute-start.15 = (bf16[256,1024]{1,0:T(8,128)(2,1)}, bf16[256,1024]{1,0:T(8,128)(2,1)}, u32[]{:S(2)}, u32[]{:S(2)}) collective-permute-start(bf16[256,1024]{1,0:T(8,128)(2,1)} %constant_dynamic-update-slice_fusion.11.near_ref), channel_id=1, source_target_pairs={{0,1},{1,0},{2,3},{3,2},{4,5},{5,4},{6,7},{7,6},{8,9},{9,8},{10,11... | collective-permute-start | bytes 1572872 | tf_op jit(solution)/shard_map/ppermute | solution.py:42
  35.5 1.6 %copy-start.1 = (bf16[1024,1024]{1,0:T(8,128)(2,1)S(1)}, bf16[1024,1024]{1,0:T(8,128)(2,1)}, u32[]{:S(2)}) copy-start(bf16[1024,1024]{1,0:T(8,128)(2,1)} %key_hbm.1) | copy-start | bytes 6291460
  35.5 1.6 %copy-start.5 = (f32[1024]{0:T(1024)S(1)}, f32[1024]{0:T(1024)}, u32[]{:S(2)}) copy-start(f32[1024]{0:T(1024)} %param.20) | copy-start | bytes 12292
  37.1 1.0 %copy-start.4 = (bf16[256,512]{1,0:T(8,128)(2,1)S(1)}, bf16[256,512]{1,0:T(8,128)(2,1)}, u32[]{:S(2)}) copy-start(bf16[256,512]{1,0:T(8,128)(2,1)} %copy-done.3) | copy-start | bytes 786436
  38.1 22.1 %copy-start = (bf16[1024,2048]{1,0:T(8,128)(2,1)S(1)}, bf16[1024,2048]{1,0:T(8,128)(2,1)}, u32[]{:S(2)}) copy-start(bf16[1024,2048]{1,0:T(8,128)(2,1)} %proj_ref.1) | copy-start | bytes 12582916
  47.8 1.7 %collective-permute-start.16 = (bf16[128,1024]{1,0:T(8,128)(2,1)S(1)}, bf16[128,1024]{1,0:T(8,128)(2,1)S(1)}, u32[]{:S(2)}, u32[]{:S(2)}) collective-permute-start(bf16[128,1024]{1,0:T(8,128)(2,1)S(1)} %get-tuple-element.63), channel_id=1, source_target_pairs={{0,1},{1,0},{2,3},{3,2},{4,5},{5,4},{6,7},{7,6},{8,9},{9,8},{10,11... | collective-permute-start | bytes 786440 | tf_op jit(solution)/shard_map/ppermute | solution.py:42
  49.6 5.8 %collective-permute-start.17 = (bf16[64,1024]{1,0:T(8,128)(2,1)S(1)}, bf16[64,1024]{1,0:T(8,128)(2,1)S(1)}, u32[]{:S(2)}, u32[]{:S(2)}) collective-permute-start(bf16[64,1024]{1,0:T(8,128)(2,1)S(1)} %slice.36), channel_id=1, source_target_pairs={{0,2},{1,3},{2,0},{3,1},{4,6},{5,7},{6,4},{7,5},{8,10},{9,11},{10,... | collective-permute-start | bytes 393224 | tf_op jit(solution)/shard_map/ppermute | solution.py:42
  55.5 5.2 %collective-permute-start.18 = (bf16[16,1024]{1,0:T(8,128)(2,1)S(1)}, bf16[16,1024]{1,0:T(8,128)(2,1)S(1)}, u32[]{:S(2)}, u32[]{:S(2)}) collective-permute-start(bf16[16,1024]{1,0:T(8,128)(2,1)S(1)} %get-tuple-element.97), channel_id=1, source_target_pairs={{0,4},{1,5},{2,6},{3,7},{4,0},{5,1},{6,2},{7,3},{8,12},{9,13},{10,... | collective-permute-start | bytes 98312 | tf_op jit(solution)/shard_map/ppermute | solution.py:42
  57.7 5.0 %collective-permute-start.19 = (bf16[16,1024]{1,0:T(8,128)(2,1)S(1)}, bf16[16,1024]{1,0:T(8,128)(2,1)S(1)}, u32[]{:S(2)}, u32[]{:S(2)}) collective-permute-start(bf16[16,1024]{1,0:T(8,128)(2,1)S(1)} %get-tuple-element.96), channel_id=1, source_target_pairs={{0,8},{1,9},{2,10},{3,11},{4,12},{5,13},{6,14},{7,15},{8,0},{9,1},... | collective-permute-start | bytes 98312 | tf_op jit(solution)/shard_map/ppermute | solution.py:42
  58.3 5.7 %collective-permute-start.20 = (bf16[16,1024]{1,0:T(8,128)(2,1)S(1)}, bf16[16,1024]{1,0:T(8,128)(2,1)S(1)}, u32[]{:S(2)}, u32[]{:S(2)}) collective-permute-start(bf16[16,1024]{1,0:T(8,128)(2,1)S(1)} %get-tuple-element.95), channel_id=1, source_target_pairs={{0,12},{1,13},{2,14},{3,15},{4,8},{5,9},{6,10},{7,11},{8,4},{9,5},... | collective-permute-start | bytes 98312 | tf_op jit(solution)/shard_map/ppermute | solution.py:42
  60.2 3.8 %copy-start.2 = (bf16[1024,1024]{1,0:T(8,128)(2,1)S(1)}, bf16[1024,1024]{1,0:T(8,128)(2,1)}, u32[]{:S(2)}) copy-start(bf16[1024,1024]{1,0:T(8,128)(2,1)} %refs_6_.1) | copy-start | bytes 6291460
  60.2 3.8 %copy-start.8 = (f32[1024]{0:T(1024)S(1)}, f32[1024]{0:T(1024)}, u32[]{:S(2)}) copy-start(f32[1024]{0:T(1024)} %param.24) | copy-start | bytes 12292

commit v3 on v2

--- a/solution.py
+++ b/solution.py
@@ -23,12 +23,10 @@
     return pltpu.CompilerParams(vmem_limit_bytes=mib << 20)
 
 
-def stage_masks(size, joined_tail):
+def stage_masks(size):
     bits = [1 << k for k in range(size.bit_length() - 1)][::-1]
-    near = bits[-2:]
     far = bits[:-2]
-    stages = [sorted(far[k : k + 2]) for k in range(0, len(far), 2)]
-    return stages + ([near] if joined_tail else [[b] for b in near])
+    return [sorted(far[k : k + 2]) for k in range(0, len(far), 2)] + [[2], [1]]
 
 
 def combos(bits):
@@ -42,21 +40,23 @@
     return lax.ppermute(x, axis, [(i, i ^ mask) for i in range(size)])
 
 
-def gather_relative(x, dim, axis, size, joined_tail):
-    stages = stage_masks(size, joined_tail)
-    for bits in stages:
-        pieces = [x] + [swap(x, m, axis, size) for m in combos(bits)[1:]]
-        if bits is not stages[-1]:
-            x = jnp.concatenate(pieces, axis=dim)
-    return pieces
+def gather_far(x, dim, axis, size):
+    for bits in stage_masks(size)[:-2]:
+        x = jnp.concatenate([x] + [swap(x, m, axis, size) for m in combos(bits)[1:]], axis=dim)
+    return x
+
+
+def gather_relative(x, dim, axis, size, direct):
+    x = gather_far(x, dim, axis, size)
+    beside = swap(x, 2, axis, size)
+    other = swap(x, 1, axis, size)
+    if direct:
+        return [x, beside, other, swap(x, 3, axis, size)]
+    return [x, beside, other, swap(beside, 1, axis, size)]
 
 
 def position_bits(size):
-    return [b for stage in stage_masks(size, False) for b in stage]
-
-
-def rounds_of(ranks, slots):
-    return jnp.max(ranks) // slots + 1
+    return [b for stage in stage_masks(size) for b in stage]
 
 
 def candidates_info(ids_refs, me, size, table_rows):
@@ -81,9 +81,7 @@
 
 
 def lookup_kernel(place_ref, *refs, size):
-    *ids_refs, table_hbm, out_ref, table_ref, sem = refs
-    copy = pltpu.make_async_copy(table_hbm, table_ref, sem)
-    copy.start()
+    *ids_refs, table_ref, out_ref, rounds_ref = refs
     me, turn = place_ref[0], place_ref[1]
     slots = out_ref.shape[0]
     rows = table_ref.shape[0]
@@ -96,24 +94,27 @@
     hit = (owner == me) & (rank == slot)
     want = jnp.sum(jnp.where(hit, offset + 1, 0), axis=1, keepdims=True) - 1
     pick = (want == lax.broadcasted_iota(jnp.int32, (slots, rows), 1)).astype(F32).astype(BF16)
-    copy.wait()
+    rounds_ref[0] = jnp.max(rank) // slots + 1
     out_ref[...] = jnp.dot(pick, table_ref[...], preferred_element_type=F32).astype(BF16)
 
 
 def lookup(place, ids, table, slots, size):
     return pl.pallas_call(
         functools.partial(lookup_kernel, size=size),
-        out_shape=jax.ShapeDtypeStruct((slots, table.shape[1]), BF16),
-        in_specs=[SMEM] + [VMEM] * len(ids) + [HBM],
-        out_specs=VMEM,
-        scratch_shapes=[pltpu.VMEM(table.shape, BF16), pltpu.SemaphoreType.DMA],
+        out_shape=(
+            jax.ShapeDtypeStruct((slots, table.shape[1]), BF16),
+            jax.ShapeDtypeStruct((1,), jnp.int32),
+        ),
+        in_specs=[SMEM] + [VMEM] * (len(ids) + 1),
+        out_specs=(VMEM, SMEM),
         compiler_params=params(24),
+        cost_estimate=pl.CostEstimate(flops=1 << 26, transcendentals=0, bytes_accessed=2 * table.size),
         name="lookup",
     )(place, *ids, table)
 
 
 def plan_kernel(place_ref, *refs, size, slots, table_rows):
-    *ids_refs, pick_ref, rounds_ref = refs
+    *ids_refs, pick_ref = refs
     me, turn = place_ref[0], place_ref[1]
     owner, key, _ = candidates_info(ids_refs, me, size, table_rows)
     count = owner.shape[1]
@@ -121,7 +122,6 @@
     owner_col = key_col // count
     before = (key < key_col) & (key >= owner_col * count)
     rank = jnp.sum(before.astype(jnp.int32), axis=1, keepdims=True)
-    rounds_ref[0] = rounds_of(rank, slots)
     away = owner_col ^ me
     block = jnp.zeros_like(away)
     for k, b in enumerate(position_bits(size)):
@@ -136,12 +136,9 @@
     count = sum(i.shape[1] for i in ids)
     return pl.pallas_call(
         functools.partial(plan_kernel, size=size, slots=slots, table_rows=table_rows),
-        out_shape=(
-            jax.ShapeDtypeStruct((count, size * slots), BF16),
-            jax.ShapeDtypeStruct((1,), jnp.int32),
-        ),
+        out_shape=jax.ShapeDtypeStruct((count, size * slots), BF16),
         in_specs=[SMEM] + [VMEM] * len(ids),
-        out_specs=(VMEM, SMEM),
+        out_specs=VMEM,
         compiler_params=params(40),
         cost_estimate=pl.CostEstimate(flops=1 << 22, transcendentals=0, bytes_accessed=1 << 20),
         name="plan",
@@ -214,25 +211,17 @@
 
 
 def attend_kernel(
-    rounds_ref, pick_ref, near_ref, far_ref, extra_hbm, gain_ref, proj_hbm, key_hbm, value_hbm, bias_ref,
-    own_ref, keep_ref, send_ref, emb_ref, query_ref, proj_ref, key_ref, value_ref, sems, *, heads
+    rounds_ref, pick_ref, *refs, heads
 ):
+    *row_refs, extra_hbm, gain_ref, proj_ref, key_ref, value_ref, bias_ref = refs[:-6]
+    own_ref, keep_ref, send_ref, emb_ref, query_ref, sem = refs[-6:]
     count, width = emb_ref.shape
-    copies = [
-        pltpu.make_async_copy(proj_hbm.at[:, pl.ds(0, width)], proj_ref, sems.at[0]),
-        pltpu.make_async_copy(key_hbm, key_ref, sems.at[1]),
-        pltpu.make_async_copy(value_hbm, value_ref, sems.at[2]),
-    ]
-    for c in copies:
-        c.start()
-    split = near_ref.shape[0]
-    picked = jnp.dot(pick_ref[:, :split], near_ref[...], preferred_element_type=F32)
-    picked = picked + jnp.dot(pick_ref[:, split:], far_ref[...], preferred_element_type=F32)
-    emb_ref[...] = picked.astype(BF16)
+    rows = jnp.concatenate([r[...] for r in row_refs], axis=0)
+    emb_ref[...] = jnp.dot(pick_ref[...], rows, preferred_element_type=F32).astype(BF16)
 
     @pl.when(rounds_ref[0] > 1)
     def _():
-        extra = pltpu.make_async_copy(extra_hbm, query_ref, sems.at[3])
+        extra = pltpu.make_async_copy(extra_hbm, query_ref, sem)
         extra.start()
         extra.wait()
         emb_ref[...] = emb_ref[...] + query_ref[...]
@@ -244,15 +233,11 @@
     rows = min(ROWS_AT_ONCE, count)
     per = LANES // head_dim
     step = min(EVENTS_AT_ONCE, events)
-    copies[0].wait()
     for first in range(0, count, rows):
         normed = normalise(emb_ref[first : first + rows, :], gain_ref[...])
-        projected = jnp.dot(normed, proj_ref[...], preferred_element_type=F32)
+        projected = jnp.dot(normed, proj_ref[:, :width], preferred_element_type=F32)
         query = silu(projected).astype(BF16)
         query_ref[first : first + rows, :] = query * jnp.asarray(0.5 * head_dim**-0.5, BF16)
-        if first == 0:
-            copies[1].wait()
-            copies[2].wait()
         lane = lax.broadcasted_iota(jnp.int32, (rows, LANES), 1)
         for group in range(heads // per):
             at = slice(group * LANES, (group + 1) * LANES)
@@ -282,7 +267,7 @@
                 send_ref[: first + rows - half, at] = out[half - first :].astype(BF16)
 
 
-def attend(rounds, pick, near, far, extra, gain, proj_in, keys, values, bias, heads, each):
+def attend(rounds, pick, pieces, extra, gain, proj_in, keys, values, bias, heads, each):
     count, width = extra.shape
     return pl.pallas_call(
         functools.partial(attend_kernel, heads=heads),
@@ -291,24 +276,21 @@
             jax.ShapeDtypeStruct((count // 2, width), F32),
             jax.ShapeDtypeStruct((count // 2, width), BF16),
         ),
-        in_specs=[SMEM, VMEM, VMEM, VMEM, HBM, VMEM, HBM, HBM, HBM, VMEM],
+        in_specs=[SMEM, VMEM] + [VMEM] * len(pieces) + [HBM] + [VMEM] * 5,
         out_specs=(VMEM, VMEM, VMEM),
         scratch_shapes=[
             pltpu.VMEM((count, width), BF16),
             pltpu.VMEM((count, width), BF16),
-            pltpu.VMEM((width, width), BF16),
-            pltpu.VMEM(keys.shape, BF16),
-            pltpu.VMEM(values.shape, BF16),
-            pltpu.SemaphoreType.DMA((4,)),
+            pltpu.SemaphoreType.DMA,
         ],
-        compiler_params=params(48),
+        compiler_params=params(40),
         cost_estimate=pl.CostEstimate(
             flops=8 * count * width * keys.shape[0],
             transcendentals=count * heads * keys.shape[0],
             bytes_accessed=4 * keys.size,
         ),
         name="attend",
-    )(rounds, pick, near, far, extra, gain, proj_in, keys, values, bias)
+    )(rounds, pick, *pieces, extra, gain, proj_in, keys, values, bias)
 
 
 def gates_kernel(emb_ref, gain_ref, proj_ref, out_ref):
@@ -394,27 +376,27 @@
     ids = gather_relative(item_ids[None, :], 1, axis, size, True)
 
     def fetch(turn):
-        found = lookup(place(turn), ids, item_table, slots, size)
-        return gather_relative(found, 0, axis, size, False)
-
-    near, far = fetch(0)
-    pick, rounds = plan(here, ids, slots, table_rows, size)
+        found, rounds = lookup(place(turn), ids, item_table, slots, size)
+        return gather_relative(found, 0, axis, size, False), rounds
+
+    pieces, rounds = fetch(0)
+    pick = plan(here, ids, slots, table_rows, size)
 
     def more(state):
         turn, so_far = state
-        picked, _ = plan(place(turn), ids, slots, table_rows, size)
-        return turn + 1, so_far + select(picked, fetch(turn))
+        picked = plan(place(turn), ids, slots, table_rows, size)
+        return turn + 1, so_far + select(picked, fetch(turn)[0])
 
     none = jnp.zeros((each * size, item_table.shape[1]), BF16)
     _, extra = lax.while_loop(lambda s: s[0] < rounds[0], more, (jnp.int32(1), none))
 
     own, keep, send = attend(
-        rounds, pick, near, far, extra, gain, proj_in, key_cache, value_cache, bias, heads, each
+        rounds, pick, pieces, extra, gain, proj_in, key_cache, value_cache, bias, heads, each
     )
     gates = gates_of(own, gain, proj_in)
 
-    stages = stage_masks(size, False)[::-1]
-    total = keep + swap(send, stages[0][0], axis, size).astype(F32)
+    stages = stage_masks(size)[::-1]
+    total = keep + swap(send, 1, axis, size).astype(F32)
     for bits in stages[1:]:
         masks = combos(bits)
         block = total.shape[0] // len(masks)

time: 65.5 us -> 68.3 us (1.043)
  waiting for transfers between devices: 18.9 us -> 22.2 us
  Pallas kernels: 16.4 us -> 14.1 us
  local copies, waits for them, and re-layouts: 7.43 us -> 8.72 us
    ppermute x16 -> x17, waiting for transfers between devices: 18.9 us -> 22.2 us  [swap(): return lax.ppermute(x, axis, [(i, i ^ mask) for i in range(size)])]
    unnamed x22 -> x25, local copies, waits for them, and re-layouts: 5.11 us -> 7.21 us
    pallas_call x1, Pallas kernels: 9.68 us -> 7.95 us  [attend(): pl.pallas_call(functools.partial(attend_kernel, heads=heads), out_shape=(...]
    pad x1, local copies, waits for them, and re-layouts: 0.7 us -> 0.01 us  [on_device(): jnp.pad(pos_bias, ((0, 0), (0, -npos % 32)))]
    ppermute x16 -> x17, starting transfers between devices: 19.9 us -> 20.5 us  [swap(): return lax.ppermute(x, axis, [(i, i ^ mask) for i in range(size)])]
  transfers between devices with their start and end apart: 16 -> 17, of which waited for: 9 -> 12; matrix products, arithmetic and copies ran while one was open for 6% -> 4% of each run, Pallas kernels for 4% -> 3%
where the time goes in v3:
time: 68.3 us; the launch traced here: 68 us
  waiting for transfers between devices  22.2 us (33%)
  starting transfers between devices  20.5 us (30%)
  Pallas kernels  14.1 us (21%)
  local copies, waits for them, and re-layouts  8.72 us (13%)
  other arithmetic  0.89 us (1%)
  between operations  0.84 us (1%)
  loops' own time  0.73 us (1%)
    ppermute x17, waiting for transfers between devices, swap(): return lax.ppermute(x, axis, [(i, i ^ mask) for i in range(size)])  22.2 us
    ppermute x17, starting transfers between devices, swap(): return lax.ppermute(x, axis, [(i, i ^ mask) for i in range(size)])  20.5 us
    pallas_call x1, Pallas kernels, attend(): pl.pallas_call(functools.partial(attend_kernel, heads=heads), out_shape=(...  7.95 us
    unnamed x25, local copies, waits for them, and re-layouts  7.21 us
    pallas_call x1, Pallas kernels, lookup(): pl.pallas_call(functools.partial(lookup_kernel, size=size), out_shape=(ja...  2.6 us
  transfers between devices with their start and end apart: 17, of which 12 were waited for; matrix products, arithmetic and copies ran while one was open for 4% of the time, Pallas kernels for 3%

profile of v3, /device:TPU:0, one launch (start us, length us, event | category | flops | bytes accessed | tf_op | source)
XLA Modules:
  0.0 68.0 jit_solution(18021545322224590817)
XLA Ops:
  0.0 0.0 copy-start.12
  0.0 0.0 copy-start.8
  0.0 0.0 copy-start.7
  0.0 3.1 %collective-permute-start.6 = (s32[1,16]{1,0:T(1,128)}, s32[1,16]{1,0:T(1,128)S(1)}, u32[]{:S(2)}, u32[]{:S(2)}) collective-permute-start(s32[1,16]{1,0:T(1,128)} %bitcast.17), channel_id=1, source_target_pairs={{0,4},{1,5},{2,6},{3,7},{4,0},{5,1},{6,2},{7,3},{8,12},{9,13},{10,... | collective-permute-start | bytes 200 | tf_op jit(solution)/shard_map/ppermute | solution.py:40
  3.1 2.6 %collective-permute-start.7 = (s32[1,16]{1,0:T(1,128)}, s32[1,16]{1,0:T(1,128)S(1)}, u32[]{:S(2)}, u32[]{:S(2)}) collective-permute-start(s32[1,16]{1,0:T(1,128)} %bitcast.18), channel_id=1, source_target_pairs={{0,8},{1,9},{2,10},{3,11},{4,12},{5,13},{6,14},{7,15},{8,0},{9,1},... | collective-permute-start | bytes 200 | tf_op jit(solution)/shard_map/ppermute | solution.py:40
  5.7 0.0 collective-permute-start.8
  5.7 0.0 collective-permute-done.6
  5.7 2.0 %collective-permute-done.7 = s32[1,16]{1,0:T(1,128)S(1)} collective-permute-done((s32[1,16]{1,0:T(1,128)}, s32[1,16]{1,0:T(1,128)S(1)}, u32[]{:S(2)}, u32[]{:S(2)}) %collective-permute-start.7) | collective-permute-done | bytes 96 | tf_op jit(solution)/shard_map/ppermute | solution.py:40
  7.7 3.5 %collective-permute-done.8 = s32[1,16]{1,0:T(1,128)S(1)} collective-permute-done((s32[1,16]{1,0:T(1,128)}, s32[1,16]{1,0:T(1,128)S(1)}, u32[]{:S(2)}, u32[]{:S(2)}) %collective-permute-start.8) | collective-permute-done | bytes 96 | tf_op jit(solution)/shard_map/ppermute | solution.py:40
  11.2 0.7 %pad_add_fusion.2.refs_0_ = s32[1,64]{1,0:T(1,128)S(1)} fusion(s32[1,16]{1,0:T(1,128)S(1)} %collective-permute-done.8, s32[1,16]{1,0:T(1,128)S(1)} %collective-permute-done.7, s32[1,16]{1,0:T(1,128)S(1)} %collective-permute-done.6, s32[1,16]{1,0:T(1,128)} %bitcast.20), kind=kLoop, calls=%fused_computation.20 | loop fusion | flops 192 | bytes 512 | tf_op jit(solution)/shard_map/concatenate | solution.py:45
  11.9 0.0 collective-permute-start.10
  12.0 1.6 %collective-permute-start.11 = (s32[1,64]{1,0:T(1,128)S(1)}, s32[1,64]{1,0:T(1,128)S(1)}, u32[]{:S(2)}, u32[]{:S(2)}) collective-permute-start(s32[1,64]{1,0:T(1,128)S(1)} %pad_add_fusion.2.refs_0_), channel_id=1, source_target_pairs={{0,3},{1,2},{2,1},{3,0},{4,7},{5,6},{6,5},{7,4},{8,11},{9,10},{10,... | collective-permute-start | bytes 776 | tf_op jit(solution)/shard_map/ppermute | solution.py:40
  13.6 0.5 collective-permute-start.9
  14.1 0.1 pad_add_fusion.1.place_ref
  14.2 0.0 collective-permute-done.10.refs_2_
  14.2 0.9 %collective-permute-done.11.refs_3_ = s32[1,64]{1,0:T(1,128)S(1)} collective-permute-done((s32[1,64]{1,0:T(1,128)S(1)}, s32[1,64]{1,0:T(1,128)S(1)}, u32[]{:S(2)}, u32[]{:S(2)}) %collective-permute-start.11) | collective-permute-done | bytes 288 | tf_op jit(solution)/shard_map/ppermute | solution.py:40
  15.0 2.1 %collective-permute-done.9.refs_1_ = s32[1,64]{1,0:T(1,128)S(1)} collective-permute-done((s32[1,64]{1,0:T(1,128)S(1)}, s32[1,64]{1,0:T(1,128)S(1)}, u32[]{:S(2)}, u32[]{:S(2)}) %collective-permute-start.9) | collective-permute-done | bytes 288 | tf_op jit(solution)/shard_map/ppermute | solution.py:40
  17.2 2.6 %lookup.2 = (bf16[32,1024]{1,0:T(8,128)(2,1)S(1)}, s32[1]{0:T(128)}) custom-call(s32[2]{0:T(128)S(1)} %pad_add_fusion.1.place_ref, s32[1,64]{1,0:T(1,128)S(1)} %pad_add_fusion.2.refs_0_, s32[1,64]{1,0:T(1,128)S(1)} %collective-permute-done.9.refs_1_, s32[1,64]{1,0:T(1,128)S(1)} %collective-permute-done.10.refs_2_, ...), custom_call_target="tpu_custom_call" | custom-call | flops 67108864 | bytes 2097152 | tf_op jit(solution)/shard_map/lookup/pallas_call | solution.py:102
  19.8 0.1 collective-permute-start.12
  19.8 0.8 %collective-permute-start.13 = (bf16[32,1024]{1,0:T(8,128)(2,1)S(1)}, bf16[32,1024]{1,0:T(8,128)(2,1)S(1)}, u32[]{:S(2)}, u32[]{:S(2)}) collective-permute-start(bf16[32,1024]{1,0:T(8,128)(2,1)S(1)} %get-tuple-element.60), channel_id=1, source_target_pairs={{0,8},{1,9},{2,10},{3,11},{4,12},{5,13},{6,14},{7,15},{8,0},{9,1},... | collective-permute-start | bytes 196616 | tf_op jit(solution)/shard_map/ppermute | solution.py:40
  20.6 3.6 %collective-permute-start.14 = (bf16[32,1024]{1,0:T(8,128)(2,1)S(1)}, bf16[32,1024]{1,0:T(8,128)(2,1)S(1)}, u32[]{:S(2)}, u32[]{:S(2)}) collective-permute-start(bf16[32,1024]{1,0:T(8,128)(2,1)S(1)} %get-tuple-element.60), channel_id=1, source_target_pairs={{0,12},{1,13},{2,14},{3,15},{4,8},{5,9},{6,10},{7,11},{8,4},{9,5},... | collective-permute-start | bytes 196616 | tf_op jit(solution)/shard_map/ppermute | solution.py:40
  24.2 0.6 constant_dynamic-update-slice_fusion.14
  24.8 0.0 collective-permute-done.12
  24.8 0.6 constant_dynamic-update-slice_fusion.13
  25.5 0.4 collective-permute-done.13
  25.8 0.6 constant_dynamic-update-slice_fusion.12
  26.5 0.8 %collective-permute-done.14 = bf16[32,1024]{1,0:T(8,128)(2,1)S(1)} collective-permute-done((bf16[32,1024]{1,0:T(8,128)(2,1)S(1)}, bf16[32,1024]{1,0:T(8,128)(2,1)S(1)}, u32[]{:S(2)}, u32[]{:S(2)}) %collective-permute-start.14) | collective-permute-done | bytes 65568 | tf_op jit(solution)/shard_map/ppermute | solution.py:40
  27.3 0.6 constant_dynamic-update-slice_fusion.11.refs_0_
  27.9 1.5 %collective-permute-start.15 = (bf16[128,1024]{1,0:T(8,128)(2,1)}, bf16[128,1024]{1,0:T(8,128)(2,1)}, u32[]{:S(2)}, u32[]{:S(2)}) collective-permute-start(bf16[128,1024]{1,0:T(8,128)(2,1)} %constant_dynamic-update-slice_fusion.11.refs_0_), channel_id=1, source_target_pairs={{0,2},{1,3},{2,0},{3,1},{4,6},{5,7},{6,4},{7,5},{8,10},{9,11},{10,... | collective-permute-start | bytes 786440 | tf_op jit(solution)/shard_map/ppermute | solution.py:40
  30.0 0.0 copy-done.12
  30.1 0.0 copy-done.8
  30.1 0.0 copy-done.7
  30.1 0.9 %bias.1.refs_9_ = bf16[1024,128]{1,0:T(8,128)(2,1)S(1)} custom-call(s32[2]{0:T(128)S(1)} %pad_add_fusion.1.place_ref, s32[1]{0:T(128)S(6)} %copy.31.start_ref, s32[1,1024]{1,0:T(1,128)S(1)} %bitcast.15, f32[16,128]{1,0:T(8,128)S(1)} %copy-done.7, f32[16,32]{1,0:T(8,128)S(1)} %pad.4.pos_bias_ref), custom_call_target="tpu_custom_call" | custom-call | flops 33554432 | bytes 1048576 | tf_op jit(solution)/shard_map/bias/pallas_call | solution.py:192
  31.0 1.0 %plan.2.pick_ref = bf16[256,512]{1,0:T(8,128)(2,1)S(1)} custom-call(s32[2]{0:T(128)S(1)} %pad_add_fusion.1.place_ref, s32[1,64]{1,0:T(1,128)S(1)} %pad_add_fusion.2.refs_0_, s32[1,64]{1,0:T(1,128)S(1)} %collective-permute-done.9.refs_1_, s32[1,64]{1,0:T(1,128)S(1)} %collective-permute-done.10.refs_2_, s32[1,64]{1,0:T(1,128)S(1)} %collective-permute-done.11.refs_3_), custom_call_target="tpu_custom_call" | custom-call | flops 4194304 | bytes 1048576 | tf_op jit(solution)/shard_map/plan/pallas_call | solution.py:137
  32.0 0.0 copy-start.4
  32.0 0.1 collective-permute-start.16
  32.1 2.5 %collective-permute-done.15.refs_1_ = bf16[128,1024]{1,0:T(8,128)(2,1)} collective-permute-done((bf16[128,1024]{1,0:T(8,128)(2,1)}, bf16[128,1024]{1,0:T(8,128)(2,1)}, u32[]{:S(2)}, u32[]{:S(2)}) %collective-permute-start.15) | collective-permute-done | bytes 262176 | tf_op jit(solution)/shard_map/ppermute | solution.py:40
  34.6 0.0 collective-permute-start.17
  34.6 0.9 %broadcast_in_dim.16 = bf16[256,1024]{1,0:T(8,128)(2,1)} broadcast(bf16[]{:T(256)} %constant.6.clone.1), dimensions={} | broadcast | bytes 524290 | tf_op jit(solution)/shard_map/broadcast_in_dim | solution.py:390
  35.4 0.0 copy-done.4
  35.4 0.7 %while.10 = (s32[]{:T(128)}, bf16[256,1024]{1,0:T(8,128)(2,1)}, s32[1]{0:T(128)}, s32[]{:T(128)}, s32[1,64]{1,0:T(1,128)S(1)}, /*index=5*/s32[1,64]{1,0:T(1,128)...) while((s32[]{:T(128)}, bf16[256,1024]{1,0:T(8,128)(2,1)}, ...), condition=%wide.region_1.2_spmd, body=%wide.region_0.1_spmd.sunk | while | flops 71565312 | bytes 15204765 | solution.py:391
  36.2 0.0 collective-permute-done.16.refs_2_
  36.2 0.3 collective-permute-done.17.refs_3_
  36.4 0.6 copy-done.1
  37.0 0.0 copy-done.6
  37.0 2.2 %copy-done = bf16[1024,2048]{1,0:T(8,128)(2,1)S(1)} copy-done((bf16[1024,2048]{1,0:T(8,128)(2,1)S(1)}, bf16[1024,2048]{1,0:T(8,128)(2,1)}, u32[]{:S(2)}) %copy-start) | copy-done | bytes 4194328
  39.2 1.6 %copy-done.2 = bf16[1024,1024]{1,0:T(8,128)(2,1)S(1)} copy-done((bf16[1024,1024]{1,0:T(8,128)(2,1)S(1)}, bf16[1024,1024]{1,0:T(8,128)(2,1)}, u32[]{:S(2)}) %copy-start.2) | copy-done | bytes 2097176
  40.8 0.9 %copy-done.5 = bf16[256,512]{1,0:T(8,128)(2,1)S(1)} copy-done((bf16[256,512]{1,0:T(8,128)(2,1)S(1)}, bf16[256,512]{1,0:T(8,128)(2,1)}, u32[]{:S(2)}) %copy-start.5) | copy-done | bytes 262168
  41.8 8.0 %attend.1 = (bf16[16,1024]{1,0:T(8,128)(2,1)S(1)}, f32[128,1024]{1,0:T(8,128)S(1)}, bf16[128,1024]{1,0:T(8,128)(2,1)S(1)}) custom-call(s32[1]{0:T(128)} %get-tuple-element.172.rounds_ref, bf16[256,512]{1,0:T(8,128)(2,1)S(1)} %copy-done.5, bf16[128,1024]{1,0:T(8,128)(2,1)} %constant_dynamic-update-slice_fusion.11.refs_0_, ...), custom_call_target="tpu_custom_call" | custom-call | flops 2147483648 | bytes 4194304 | tf_op jit(solution)/shard_map/attend/pallas_call | solution.py:272
  49.7 0.6 collective-permute-start.18
  50.3 1.2 %collective-permute-done.18 = bf16[128,1024]{1,0:T(8,128)(2,1)S(1)} collective-permute-done((bf16[128,1024]{1,0:T(8,128)(2,1)S(1)}, bf16[128,1024]{1,0:T(8,128)(2,1)S(1)}, u32[]{:S(2)}, u32[]{:S(2)}) %collective-permute-start.18) | collective-permute-done | bytes 262176 | tf_op jit(solution)/shard_map/ppermute | solution.py:40
  51.5 0.1 convert_add_fusion
  51.5 1.6 %collective-permute-start.19 = (bf16[64,1024]{1,0:T(8,128)(2,1)S(1)}, bf16[64,1024]{1,0:T(8,128)(2,1)S(1)}, u32[]{:S(2)}, u32[]{:S(2)}) collective-permute-start(bf16[64,1024]{1,0:T(8,128)(2,1)S(1)} %slice.36), channel_id=1, source_target_pairs={{0,2},{1,3},{2,0},{3,1},{4,6},{5,7},{6,4},{7,5},{8,10},{9,11},{10,... | collective-permute-start | bytes 393224 | tf_op jit(solution)/shard_map/ppermute | solution.py:40
  53.1 4.3 %collective-permute-done.19 = bf16[64,1024]{1,0:T(8,128)(2,1)S(1)} collective-permute-done((bf16[64,1024]{1,0:T(8,128)(2,1)S(1)}, bf16[64,1024]{1,0:T(8,128)(2,1)S(1)}, u32[]{:S(2)}, u32[]{:S(2)}) %collective-permute-start.19) | collective-permute-done | bytes 131104 | tf_op jit(solution)/shard_map/ppermute | solution.py:40
  57.4 1.3 %collective-permute-start.20 = (bf16[16,1024]{1,0:T(8,128)(2,1)S(1)}, bf16[16,1024]{1,0:T(8,128)(2,1)S(1)}, u32[]{:S(2)}, u32[]{:S(2)}) collective-permute-start(bf16[16,1024]{1,0:T(8,128)(2,1)S(1)} %get-tuple-element.95), channel_id=1, source_target_pairs={{0,4},{1,5},{2,6},{3,7},{4,0},{5,1},{6,2},{7,3},{8,12},{9,13},{10,... | collective-permute-start | bytes 98312 | tf_op jit(solution)/shard_map/ppermute | solution.py:40
  58.7 2.3 %collective-permute-start.21 = (bf16[16,1024]{1,0:T(8,128)(2,1)S(1)}, bf16[16,1024]{1,0:T(8,128)(2,1)S(1)}, u32[]{:S(2)}, u32[]{:S(2)}) collective-permute-start(bf16[16,1024]{1,0:T(8,128)(2,1)S(1)} %get-tuple-element.94), channel_id=1, source_target_pairs={{0,8},{1,9},{2,10},{3,11},{4,12},{5,13},{6,14},{7,15},{8,0},{9,1},... | collective-permute-start | bytes 98312 | tf_op jit(solution)/shard_map/ppermute | solution.py:40
  61.1 0.8 %collective-permute-start.22 = (bf16[16,1024]{1,0:T(8,128)(2,1)S(1)}, bf16[16,1024]{1,0:T(8,128)(2,1)S(1)}, u32[]{:S(2)}, u32[]{:S(2)}) collective-permute-start(bf16[16,1024]{1,0:T(8,128)(2,1)S(1)} %get-tuple-element.93), channel_id=1, source_target_pairs={{0,12},{1,13},{2,14},{3,15},{4,8},{5,9},{6,10},{7,11},{8,4},{9,5},... | collective-permute-start | bytes 98312 | tf_op jit(solution)/shard_map/ppermute | solution.py:40
  61.9 0.5 gates.1.refs_4_
  62.4 0.0 collective-permute-done.20.refs_0_
  62.4 1.5 %collective-permute-done.21.refs_1_ = bf16[16,1024]{1,0:T(8,128)(2,1)S(1)} collective-permute-done((bf16[16,1024]{1,0:T(8,128)(2,1)S(1)}, bf16[16,1024]{1,0:T(8,128)(2,1)S(1)}, u32[]{:S(2)}, u32[]{:S(2)}) %collective-permute-start.21) | collective-permute-done | bytes 32800 | tf_op jit(solution)/shard_map/ppermute | solution.py:40
  63.9 2.9 %collective-permute-done.22.refs_2_ = bf16[16,1024]{1,0:T(8,128)(2,1)S(1)} collective-permute-done((bf16[16,1024]{1,0:T(8,128)(2,1)S(1)}, bf16[16,1024]{1,0:T(8,128)(2,1)S(1)}, u32[]{:S(2)}, u32[]{:S(2)}) %collective-permute-start.22) | collective-permute-done | bytes 32800 | tf_op jit(solution)/shard_map/ppermute | solution.py:40
  66.8 0.0 copy-done.3
  66.8 0.0 copy-done.9
  66.8 1.2 %finish.1 = bf16[16,1024]{1,0:T(8,128)(2,1)} custom-call(f32[16,1024]{1,0:T(8,128)S(1)} %slice.30.own_ref, bf16[16,1024]{1,0:T(8,128)(2,1)S(1)} %collective-permute-done.20.refs_0_, bf16[16,1024]{1,0:T(8,128)(2,1)S(1)} %collective-permute-done.21.refs_1_, bf16[16,1024]{1,0:T(8,128)(2,1)S(1)} %collective-permute-done.22.refs_2_, ...), custom_call_target="tpu_custom_call" | custom-call | tf_op jit(solution)/shard_map/finish/pallas_call | solution.py:328
  (12 shorter events, 0.1 us)
Async XLA Ops:
  0.0 30.0 %copy-start.12 = (f32[16,18]{1,0:T(8,128)S(1)}, f32[16,18]{1,0:T(8,128)}, u32[]{:S(2)}) copy-start(f32[16,18]{1,0:T(8,128)} %param.23) | copy-start | bytes 3460
  0.0 30.1 %copy-start.8 = (s32[1024]{0:T(1024)S(1)}, s32[1024]{0:T(1024)}, u32[]{:S(2)}) copy-start(s32[1024]{0:T(1024)} %param.18) | copy-start | bytes 12292
  0.0 30.1 %copy-start.7 = (f32[16,128]{1,0:T(8,128)S(1)}, f32[16,128]{1,0:T(8,128)}, u32[]{:S(2)}) copy-start(f32[16,128]{1,0:T(8,128)} %time_bias_ref.1) | copy-start | bytes 24580
  0.0 5.7 %collective-permute-start.6 = (s32[1,16]{1,0:T(1,128)}, s32[1,16]{1,0:T(1,128)S(1)}, u32[]{:S(2)}, u32[]{:S(2)}) collective-permute-start(s32[1,16]{1,0:T(1,128)} %bitcast.17), channel_id=1, source_target_pairs={{0,4},{1,5},{2,6},{3,7},{4,0},{5,1},{6,2},{7,3},{8,12},{9,13},{10,... | collective-permute-start | bytes 200 | tf_op jit(solution)/shard_map/ppermute | solution.py:40
  3.1 4.6 %collective-permute-start.7 = (s32[1,16]{1,0:T(1,128)}, s32[1,16]{1,0:T(1,128)S(1)}, u32[]{:S(2)}, u32[]{:S(2)}) collective-permute-start(s32[1,16]{1,0:T(1,128)} %bitcast.18), channel_id=1, source_target_pairs={{0,8},{1,9},{2,10},{3,11},{4,12},{5,13},{6,14},{7,15},{8,0},{9,1},... | collective-permute-start | bytes 200 | tf_op jit(solution)/shard_map/ppermute | solution.py:40
  5.7 5.5 %collective-permute-start.8 = (s32[1,16]{1,0:T(1,128)}, s32[1,16]{1,0:T(1,128)S(1)}, u32[]{:S(2)}, u32[]{:S(2)}) collective-permute-start(s32[1,16]{1,0:T(1,128)} %bitcast.19), channel_id=1, source_target_pairs={{0,12},{1,13},{2,14},{3,15},{4,8},{5,9},{6,10},{7,11},{8,4},{9,5},... | collective-permute-start | bytes 200 | tf_op jit(solution)/shard_map/ppermute | solution.py:40
  11.9 2.2 %collective-permute-start.10 = (s32[1,64]{1,0:T(1,128)S(1)}, s32[1,64]{1,0:T(1,128)S(1)}, u32[]{:S(2)}, u32[]{:S(2)}) collective-permute-start(s32[1,64]{1,0:T(1,128)S(1)} %pad_add_fusion.2.refs_0_), channel_id=1, source_target_pairs={{0,1},{1,0},{2,3},{3,2},{4,5},{5,4},{6,7},{7,6},{8,9},{9,8},{10,11... | collective-permute-start | bytes 776 | tf_op jit(solution)/shard_map/ppermute | solution.py:40
  12.0 3.1 %collective-permute-start.11 = (s32[1,64]{1,0:T(1,128)S(1)}, s32[1,64]{1,0:T(1,128)S(1)}, u32[]{:S(2)}, u32[]{:S(2)}) collective-permute-start(s32[1,64]{1,0:T(1,128)S(1)} %pad_add_fusion.2.refs_0_), channel_id=1, source_target_pairs={{0,3},{1,2},{2,1},{3,0},{4,7},{5,6},{6,5},{7,4},{8,11},{9,10},{10,... | collective-permute-start | bytes 776 | tf_op jit(solution)/shard_map/ppermute | solution.py:40
  13.6 3.6 %collective-permute-start.9 = (s32[1,64]{1,0:T(1,128)S(1)}, s32[1,64]{1,0:T(1,128)S(1)}, u32[]{:S(2)}, u32[]{:S(2)}) collective-permute-start(s32[1,64]{1,0:T(1,128)S(1)} %pad_add_fusion.2.refs_0_), channel_id=1, source_target_pairs={{0,2},{1,3},{2,0},{3,1},{4,6},{5,7},{6,4},{7,5},{8,10},{9,11},{10,... | collective-permute-start | bytes 776 | tf_op jit(solution)/shard_map/ppermute | solution.py:40
  19.8 5.1 %collective-permute-start.12 = (bf16[32,1024]{1,0:T(8,128)(2,1)S(1)}, bf16[32,1024]{1,0:T(8,128)(2,1)S(1)}, u32[]{:S(2)}, u32[]{:S(2)}) collective-permute-start(bf16[32,1024]{1,0:T(8,128)(2,1)S(1)} %get-tuple-element.60), channel_id=1, source_target_pairs={{0,4},{1,5},{2,6},{3,7},{4,0},{5,1},{6,2},{7,3},{8,12},{9,13},{10,... | collective-permute-start | bytes 196616 | tf_op jit(solution)/shard_map/ppermute | solution.py:40
  19.8 6.0 %collective-permute-start.13 = (bf16[32,1024]{1,0:T(8,128)(2,1)S(1)}, bf16[32,1024]{1,0:T(8,128)(2,1)S(1)}, u32[]{:S(2)}, u32[]{:S(2)}) collective-permute-start(bf16[32,1024]{1,0:T(8,128)(2,1)S(1)} %get-tuple-element.60), channel_id=1, source_target_pairs={{0,8},{1,9},{2,10},{3,11},{4,12},{5,13},{6,14},{7,15},{8,0},{9,1},... | collective-permute-start | bytes 196616 | tf_op jit(solution)/shard_map/ppermute | solution.py:40
  20.6 6.6 %collective-permute-start.14 = (bf16[32,1024]{1,0:T(8,128)(2,1)S(1)}, bf16[32,1024]{1,0:T(8,128)(2,1)S(1)}, u32[]{:S(2)}, u32[]{:S(2)}) collective-permute-start(bf16[32,1024]{1,0:T(8,128)(2,1)S(1)} %get-tuple-element.60), channel_id=1, source_target_pairs={{0,12},{1,13},{2,14},{3,15},{4,8},{5,9},{6,10},{7,11},{8,4},{9,5},... | collective-permute-start | bytes 196616 | tf_op jit(solution)/shard_map/ppermute | solution.py:40
  27.9 6.7 %collective-permute-start.15 = (bf16[128,1024]{1,0:T(8,128)(2,1)}, bf16[128,1024]{1,0:T(8,128)(2,1)}, u32[]{:S(2)}, u32[]{:S(2)}) collective-permute-start(bf16[128,1024]{1,0:T(8,128)(2,1)} %constant_dynamic-update-slice_fusion.11.refs_0_), channel_id=1, source_target_pairs={{0,2},{1,3},{2,0},{3,1},{4,6},{5,7},{6,4},{7,5},{8,10},{9,11},{10,... | collective-permute-start | bytes 786440 | tf_op jit(solution)/shard_map/ppermute | solution.py:40
  32.0 3.4 %copy-start.4 = (bf16[256,512]{1,0:T(8,128)(2,1)}, bf16[256,512]{1,0:T(8,128)(2,1)S(1)}, u32[]{:S(2)}) copy-start(bf16[256,512]{1,0:T(8,128)(2,1)S(1)} %plan.2.pick_ref) | copy-start | bytes 786436
  32.0 4.2 %collective-permute-start.16 = (bf16[128,1024]{1,0:T(8,128)(2,1)}, bf16[128,1024]{1,0:T(8,128)(2,1)}, u32[]{:S(2)}, u32[]{:S(2)}) collective-permute-start(bf16[128,1024]{1,0:T(8,128)(2,1)} %constant_dynamic-update-slice_fusion.11.refs_0_), channel_id=1, source_target_pairs={{0,1},{1,0},{2,3},{3,2},{4,5},{5,4},{6,7},{7,6},{8,9},{9,8},{10,11... | collective-permute-start | bytes 786440 | tf_op jit(solution)/shard_map/ppermute | solution.py:40
  34.6 1.9 %collective-permute-start.17 = (bf16[128,1024]{1,0:T(8,128)(2,1)}, bf16[128,1024]{1,0:T(8,128)(2,1)}, u32[]{:S(2)}, u32[]{:S(2)}) collective-permute-start(bf16[128,1024]{1,0:T(8,128)(2,1)} %collective-permute-done.15.refs_1_), channel_id=1, source_target_pairs={{0,1},{1,0},{2,3},{3,2},{4,5},{5,4},{6,7},{7,6},{8,9},{9,8},{10,11... | collective-permute-start | bytes 786440 | tf_op jit(solution)/shard_map/ppermute | solution.py:40
  35.4 1.6 %copy-start.1 = (bf16[1024,1024]{1,0:T(8,128)(2,1)S(1)}, bf16[1024,1024]{1,0:T(8,128)(2,1)}, u32[]{:S(2)}) copy-start(bf16[1024,1024]{1,0:T(8,128)(2,1)} %refs_7_.1) | copy-start | bytes 6291460
  35.4 1.6 %copy-start.6 = (f32[1024]{0:T(1024)S(1)}, f32[1024]{0:T(1024)}, u32[]{:S(2)}) copy-start(f32[1024]{0:T(1024)} %param.20) | copy-start | bytes 12292
  37.0 2.2 %copy-start = (bf16[1024,2048]{1,0:T(8,128)(2,1)S(1)}, bf16[1024,2048]{1,0:T(8,128)(2,1)}, u32[]{:S(2)}) copy-start(bf16[1024,2048]{1,0:T(8,128)(2,1)} %proj_ref.1) | copy-start | bytes 12582916
  39.2 1.6 %copy-start.2 = (bf16[1024,1024]{1,0:T(8,128)(2,1)S(1)}, bf16[1024,1024]{1,0:T(8,128)(2,1)}, u32[]{:S(2)}) copy-start(bf16[1024,1024]{1,0:T(8,128)(2,1)} %refs_8_.1) | copy-start | bytes 6291460
  40.8 0.9 %copy-start.5 = (bf16[256,512]{1,0:T(8,128)(2,1)S(1)}, bf16[256,512]{1,0:T(8,128)(2,1)}, u32[]{:S(2)}) copy-start(bf16[256,512]{1,0:T(8,128)(2,1)} %copy-done.4) | copy-start | bytes 786436
  49.7 1.7 %collective-permute-start.18 = (bf16[128,1024]{1,0:T(8,128)(2,1)S(1)}, bf16[128,1024]{1,0:T(8,128)(2,1)S(1)}, u32[]{:S(2)}, u32[]{:S(2)}) collective-permute-start(bf16[128,1024]{1,0:T(8,128)(2,1)S(1)} %get-tuple-element.63), channel_id=1, source_target_pairs={{0,1},{1,0},{2,3},{3,2},{4,5},{5,4},{6,7},{7,6},{8,9},{9,8},{10,11... | collective-permute-start | bytes 786440 | tf_op jit(solution)/shard_map/ppermute | solution.py:40
  51.5 5.8 %collective-permute-start.19 = (bf16[64,1024]{1,0:T(8,128)(2,1)S(1)}, bf16[64,1024]{1,0:T(8,128)(2,1)S(1)}, u32[]{:S(2)}, u32[]{:S(2)}) collective-permute-start(bf16[64,1024]{1,0:T(8,128)(2,1)S(1)} %slice.36), channel_id=1, source_target_pairs={{0,2},{1,3},{2,0},{3,1},{4,6},{5,7},{6,4},{7,5},{8,10},{9,11},{10,... | collective-permute-start | bytes 393224 | tf_op jit(solution)/shard_map/ppermute | solution.py:40
  57.4 4.9 %collective-permute-start.20 = (bf16[16,1024]{1,0:T(8,128)(2,1)S(1)}, bf16[16,1024]{1,0:T(8,128)(2,1)S(1)}, u32[]{:S(2)}, u32[]{:S(2)}) collective-permute-start(bf16[16,1024]{1,0:T(8,128)(2,1)S(1)} %get-tuple-element.95), channel_id=1, source_target_pairs={{0,4},{1,5},{2,6},{3,7},{4,0},{5,1},{6,2},{7,3},{8,12},{9,13},{10,... | collective-permute-start | bytes 98312 | tf_op jit(solution)/shard_map/ppermute | solution.py:40
  58.7 5.2 %collective-permute-start.21 = (bf16[16,1024]{1,0:T(8,128)(2,1)S(1)}, bf16[16,1024]{1,0:T(8,128)(2,1)S(1)}, u32[]{:S(2)}, u32[]{:S(2)}) collective-permute-start(bf16[16,1024]{1,0:T(8,128)(2,1)S(1)} %get-tuple-element.94), channel_id=1, source_target_pairs={{0,8},{1,9},{2,10},{3,11},{4,12},{5,13},{6,14},{7,15},{8,0},{9,1},... | collective-permute-start | bytes 98312 | tf_op jit(solution)/shard_map/ppermute | solution.py:40
  61.1 5.7 %collective-permute-start.22 = (bf16[16,1024]{1,0:T(8,128)(2,1)S(1)}, bf16[16,1024]{1,0:T(8,128)(2,1)S(1)}, u32[]{:S(2)}, u32[]{:S(2)}) collective-permute-start(bf16[16,1024]{1,0:T(8,128)(2,1)S(1)} %get-tuple-element.93), channel_id=1, source_target_pairs={{0,12},{1,13},{2,14},{3,15},{4,8},{5,9},{6,10},{7,11},{8,4},{9,5},... | collective-permute-start | bytes 98312 | tf_op jit(solution)/shard_map/ppermute | solution.py:40
  61.9 4.9 %copy-start.3 = (bf16[1024,1024]{1,0:T(8,128)(2,1)S(1)}, bf16[1024,1024]{1,0:T(8,128)(2,1)}, u32[]{:S(2)}) copy-start(bf16[1024,1024]{1,0:T(8,128)(2,1)} %refs_6_.3) | copy-start | bytes 6291460
  61.9 4.9 %copy-start.9 = (f32[1024]{0:T(1024)S(1)}, f32[1024]{0:T(1024)}, u32[]{:S(2)}) copy-start(f32[1024]{0:T(1024)} %param.24) | copy-start | bytes 12292

commit v4 on v3

--- a/solution.py
+++ b/solution.py
@@ -40,9 +40,30 @@
     return lax.ppermute(x, axis, [(i, i ^ mask) for i in range(size)])
 
 
+def join_kernel(*refs):
+    *parts, out_ref = refs
+    rows = parts[0].shape[0]
+    for k, p in enumerate(parts):
+        out_ref[k * rows : (k + 1) * rows, :] = p[...]
+
+
+def join(pieces, dim):
+    if dim:
+        return jnp.concatenate(pieces, axis=dim)
+    rows, width = pieces[0].shape
+    return pl.pallas_call(
+        join_kernel,
+        out_shape=jax.ShapeDtypeStruct((len(pieces) * rows, width), BF16),
+        in_specs=[VMEM] * len(pieces),
+        out_specs=VMEM,
+        compiler_params=params(16),
+        name="join",
+    )(*pieces)
+
+
 def gather_far(x, dim, axis, size):
     for bits in stage_masks(size)[:-2]:
-        x = jnp.concatenate([x] + [swap(x, m, axis, size) for m in combos(bits)[1:]], axis=dim)
+        x = join([x] + [swap(x, m, axis, size) for m in combos(bits)[1:]], dim)
     return x
 
 
@@ -293,6 +314,35 @@
     )(rounds, pick, *pieces, extra, gain, proj_in, keys, values, bias)
 
 
+def stage_kernel(proj_hbm, key_hbm, value_hbm, proj_ref, key_ref, value_ref, sems):
+    copies = [
+        pltpu.make_async_copy(proj_hbm.at[:, pl.ds(0, proj_ref.shape[1])], proj_ref, sems.at[0]),
+        pltpu.make_async_copy(key_hbm, key_ref, sems.at[1]),
+        pltpu.make_async_copy(value_hbm, value_ref, sems.at[2]),
+    ]
+    for c in copies:
+        c.start()
+    for c in copies:
+        c.wait()
+
+
+def stage(proj_in, keys, values):
+    width = keys.shape[1]
+    return pl.pallas_call(
+        stage_kernel,
+        out_shape=(
+            jax.ShapeDtypeStruct((width, width), BF16),
+            jax.ShapeDtypeStruct(keys.shape, BF16),
+            jax.ShapeDtypeStruct(values.shape, BF16),
+        ),
+        in_specs=[HBM] * 3,
+        out_specs=(VMEM,) * 3,
+        scratch_shapes=[pltpu.SemaphoreType.DMA((3,))],
+        compiler_params=params(16),
+        name="stage",
+    )(*(pltpu.with_memory_space_constraint(a, pltpu.HBM) for a in (proj_in, keys, values)))
+
+
 def gates_kernel(emb_ref, gain_ref, proj_ref, out_ref):
     normed = normalise(emb_ref[...], gain_ref[...])
     projected = jnp.dot(normed, proj_ref[...], preferred_element_type=F32)
@@ -390,9 +440,8 @@
     none = jnp.zeros((each * size, item_table.shape[1]), BF16)
     _, extra = lax.while_loop(lambda s: s[0] < rounds[0], more, (jnp.int32(1), none))
 
-    own, keep, send = attend(
-        rounds, pick, pieces, extra, gain, proj_in, key_cache, value_cache, bias, heads, each
-    )
+    staged = stage(proj_in, key_cache, value_cache)
+    own, keep, send = attend(rounds, pick, pieces, extra, gain, *staged, bias, heads, each)
     gates = gates_of(own, gain, proj_in)
 
     stages = stage_masks(size)[::-1]
@@ -427,4 +476,6 @@
         P(),
     )
 
-    return jax.shard_map(on_device, mesh=mesh, in_specs=placed, out_specs=P(("grp", "hist"), None), check_vma=False)
+    return jax.shard_map(
+        on_device, mesh=mesh, in_specs=placed, out_specs=P(("grp", "hist"), None), check_vma=False
+    )

time: 68.3 us -> 64.5 us (0.944)
  waiting for transfers between devices: 22.2 us -> 18.1 us
  Pallas kernels: 14.1 us -> 17.3 us
  local copies, waits for them, and re-layouts: 8.72 us -> 6.79 us
  starting transfers between devices: 20.5 us -> 19.6 us
    ppermute x17, waiting for transfers between devices: 22.2 us -> 18.1 us  [swap(): return lax.ppermute(x, axis, [(i, i ^ mask) for i in range(size)])]
    pallas_call x0 -> x2, Pallas kernels: none -> 2.91 us  [the longest x1 2.89 us: stage(): pl.pallas_call(stage_kernel, out_shape=(jax.ShapeDtypeStruct((width, widt...]
    unnamed x25 -> x22, local copies, waits for them, and re-layouts: 7.21 us -> 5.89 us
    ppermute x17, starting transfers between devices: 20.5 us -> 19.6 us  [swap(): return lax.ppermute(x, axis, [(i, i ^ mask) for i in range(size)])]
  transfers between devices with their start and end apart: 17 -> 17, of which waited for: 12 -> 10; matrix products, arithmetic and copies ran while one was open for 4% -> 1% of each run, Pallas kernels for 3% -> 8%
where the time goes in v4:
time: 64.5 us; the launch traced here: 64.3 us
  starting transfers between devices  19.6 us (30%)
  waiting for transfers between devices  18.1 us (28%)
  Pallas kernels  17.3 us (27%)
  local copies, waits for them, and re-layouts  6.79 us (11%)
  other arithmetic  0.89 us (1%)
  between operations  0.87 us (1%)
  loops' own time  0.71 us (1%)
    ppermute x17, starting transfers between devices, swap(): return lax.ppermute(x, axis, [(i, i ^ mask) for i in range(size)])  19.6 us
    ppermute x17, waiting for transfers between devices, swap(): return lax.ppermute(x, axis, [(i, i ^ mask) for i in range(size)])  18.1 us
    pallas_call x1, Pallas kernels, attend(): pl.pallas_call(functools.partial(attend_kernel, heads=heads), out_shape=(...  8.26 us
    unnamed x22, local copies, waits for them, and re-layouts  5.89 us
    pallas_call x1, Pallas kernels, stage(): pl.pallas_call(stage_kernel, out_shape=(jax.ShapeDtypeStruct((width, widt...  2.89 us
    pallas_call x1, Pallas kernels, lookup(): pl.pallas_call(functools.partial(lookup_kernel, size=size), out_shape=(ja...  2.6 us
  transfers between devices with their start and end apart: 17, of which 10 were waited for; matrix products, arithmetic and copies ran while one was open for 1% of the time, Pallas kernels for 8%

profile of v4, /device:TPU:0, one launch (start us, length us, event | category | flops | bytes accessed | tf_op | source)
XLA Modules:
  0.0 64.3 jit_solution(4867119566611448858)
XLA Ops:
  0.0 0.0 copy-start.12
  0.0 5.1 %collective-permute-start.8 = (s32[1,16]{1,0:T(1,128)}, s32[1,16]{1,0:T(1,128)S(1)}, u32[]{:S(2)}, u32[]{:S(2)}) collective-permute-start(s32[1,16]{1,0:T(1,128)} %bitcast.17), channel_id=1, source_target_pairs={{0,12},{1,13},{2,14},{3,15},{4,8},{5,9},{6,10},{7,11},{8,4},{9,5},... | collective-permute-start | bytes 200 | tf_op jit(solution)/shard_map/ppermute | solution.py:40
  5.1 0.0 collective-permute-start.7
  5.1 0.6 collective-permute-start.6
  5.7 1.1 %collective-permute-done.8 = s32[1,16]{1,0:T(1,128)S(1)} collective-permute-done((s32[1,16]{1,0:T(1,128)}, s32[1,16]{1,0:T(1,128)S(1)}, u32[]{:S(2)}, u32[]{:S(2)}) %collective-permute-start.8) | collective-permute-done | bytes 96 | tf_op jit(solution)/shard_map/ppermute | solution.py:40
  6.8 2.9 %collective-permute-done.7 = s32[1,16]{1,0:T(1,128)S(1)} collective-permute-done((s32[1,16]{1,0:T(1,128)}, s32[1,16]{1,0:T(1,128)S(1)}, u32[]{:S(2)}, u32[]{:S(2)}) %collective-permute-start.7) | collective-permute-done | bytes 96 | tf_op jit(solution)/shard_map/ppermute | solution.py:40
  9.7 0.0 collective-permute-done.6
  9.7 0.7 %pad_add_fusion.2.refs_0_ = s32[1,64]{1,0:T(1,128)S(1)} fusion(s32[1,16]{1,0:T(1,128)S(1)} %collective-permute-done.8, s32[1,16]{1,0:T(1,128)S(1)} %collective-permute-done.7, s32[1,16]{1,0:T(1,128)S(1)} %collective-permute-done.6, s32[1,16]{1,0:T(1,128)} %bitcast.20), kind=kLoop, calls=%fused_computation.6 | loop fusion | flops 192 | bytes 512 | tf_op jit(solution)/shard_map/concatenate | solution.py:52
  10.4 0.0 collective-permute-start.11
  10.4 1.6 %collective-permute-start.10 = (s32[1,64]{1,0:T(1,128)S(1)}, s32[1,64]{1,0:T(1,128)S(1)}, u32[]{:S(2)}, u32[]{:S(2)}) collective-permute-start(s32[1,64]{1,0:T(1,128)S(1)} %pad_add_fusion.2.refs_0_), channel_id=1, source_target_pairs={{0,1},{1,0},{2,3},{3,2},{4,5},{5,4},{6,7},{7,6},{8,9},{9,8},{10,11... | collective-permute-start | bytes 776 | tf_op jit(solution)/shard_map/ppermute | solution.py:40
  12.1 0.5 collective-permute-start.9
  12.6 0.1 pad_add_fusion.1.place_ref
  12.6 0.8 %collective-permute-done.11.refs_3_ = s32[1,64]{1,0:T(1,128)S(1)} collective-permute-done((s32[1,64]{1,0:T(1,128)S(1)}, s32[1,64]{1,0:T(1,128)S(1)}, u32[]{:S(2)}, u32[]{:S(2)}) %collective-permute-start.11) | collective-permute-done | bytes 288 | tf_op jit(solution)/shard_map/ppermute | solution.py:40
  13.4 0.0 collective-permute-done.10.refs_2_
  13.4 2.2 %collective-permute-done.9.refs_1_ = s32[1,64]{1,0:T(1,128)S(1)} collective-permute-done((s32[1,64]{1,0:T(1,128)S(1)}, s32[1,64]{1,0:T(1,128)S(1)}, u32[]{:S(2)}, u32[]{:S(2)}) %collective-permute-start.9) | collective-permute-done | bytes 288 | tf_op jit(solution)/shard_map/ppermute | solution.py:40
  15.6 2.6 %lookup.2 = (bf16[32,1024]{1,0:T(8,128)(2,1)S(1)}, s32[1]{0:T(128)}) custom-call(s32[2]{0:T(128)S(1)} %pad_add_fusion.1.place_ref, s32[1,64]{1,0:T(1,128)S(1)} %pad_add_fusion.2.refs_0_, s32[1,64]{1,0:T(1,128)S(1)} %collective-permute-done.9.refs_1_, s32[1,64]{1,0:T(1,128)S(1)} %collective-permute-done.10.refs_2_, ...), custom_call_target="tpu_custom_call" | custom-call | flops 67108864 | bytes 2097152 | tf_op jit(solution)/shard_map/lookup/pallas_call | solution.py:123
  18.2 1.6 %collective-permute-start.14 = (bf16[32,1024]{1,0:T(8,128)(2,1)S(1)}, bf16[32,1024]{1,0:T(8,128)(2,1)S(1)}, u32[]{:S(2)}, u32[]{:S(2)}) collective-permute-start(bf16[32,1024]{1,0:T(8,128)(2,1)S(1)} %get-tuple-element.63.refs_0_), channel_id=1, source_target_pairs={{0,12},{1,13},{2,14},{3,15},{4,8},{5,9},{6,10},{7,11},{8,4},{9,5},... | collective-permute-start | bytes 196616 | tf_op jit(solution)/shard_map/ppermute | solution.py:40
  19.8 0.6 collective-permute-start.13
  20.4 2.3 %collective-permute-start.12 = (bf16[32,1024]{1,0:T(8,128)(2,1)S(1)}, bf16[32,1024]{1,0:T(8,128)(2,1)S(1)}, u32[]{:S(2)}, u32[]{:S(2)}) collective-permute-start(bf16[32,1024]{1,0:T(8,128)(2,1)S(1)} %get-tuple-element.63.refs_0_), channel_id=1, source_target_pairs={{0,4},{1,5},{2,6},{3,7},{4,0},{5,1},{6,2},{7,3},{8,12},{9,13},{10,... | collective-permute-start | bytes 196616 | tf_op jit(solution)/shard_map/ppermute | solution.py:40
  22.7 1.9 %collective-permute-done.14.refs_3_ = bf16[32,1024]{1,0:T(8,128)(2,1)S(1)} collective-permute-done((bf16[32,1024]{1,0:T(8,128)(2,1)S(1)}, bf16[32,1024]{1,0:T(8,128)(2,1)S(1)}, u32[]{:S(2)}, u32[]{:S(2)}) %collective-permute-start.14) | collective-permute-done | bytes 65568 | tf_op jit(solution)/shard_map/ppermute | solution.py:40
  24.6 1.8 %collective-permute-done.13.refs_2_ = bf16[32,1024]{1,0:T(8,128)(2,1)S(1)} collective-permute-done((bf16[32,1024]{1,0:T(8,128)(2,1)S(1)}, bf16[32,1024]{1,0:T(8,128)(2,1)S(1)}, u32[]{:S(2)}, u32[]{:S(2)}) %collective-permute-start.13) | collective-permute-done | bytes 65568 | tf_op jit(solution)/shard_map/ppermute | solution.py:40
  26.5 0.0 collective-permute-done.12.refs_1_
  26.5 0.6 collective-permute-start.15
  27.7 0.0 copy-done.12
  27.7 0.0 copy-start.7
  27.7 0.0 copy-start.8
  27.8 2.9 %stage.1 = (bf16[1024,1024]{1,0:T(8,128)(2,1)S(1)}, bf16[1024,1024]{1,0:T(8,128)(2,1)S(1)}, bf16[1024,1024]{1,0:T(8,128)(2,1)S(1)}) custom-call(bf16[1024,2048]{1,0:T(8,128)(2,1)} %proj_ref.1, bf16[1024,1024]{1,0:T(8,128)(2,1)} %key_hbm.1, bf16[1024,1024]{1,0:T(8,128)(2,1)} %value_hbm.1), custom_call_target="tpu_custom_call" | custom-call | tf_op jit(solution)/shard_map/stage/pallas_call | solution.py:331
  30.7 0.0 copy-start.2
  30.7 1.4 %copy-done.2 = bf16[1024,1024]{1,0:T(8,128)(2,1)} copy-done((bf16[1024,1024]{1,0:T(8,128)(2,1)}, bf16[1024,1024]{1,0:T(8,128)(2,1)S(1)}, u32[]{:S(2)}) %copy-start.2) | copy-done | bytes 2097176
  32.0 0.0 copy-start.4
  32.0 1.3 %copy-done.4 = bf16[1024,1024]{1,0:T(8,128)(2,1)} copy-done((bf16[1024,1024]{1,0:T(8,128)(2,1)}, bf16[1024,1024]{1,0:T(8,128)(2,1)S(1)}, u32[]{:S(2)}) %copy-start.4) | copy-done | bytes 2097176
  33.4 0.0 copy-done.7
  33.4 0.0 copy-done.8
  33.4 0.9 %bias.1.refs_9_ = bf16[1024,128]{1,0:T(8,128)(2,1)S(1)} custom-call(s32[2]{0:T(128)S(1)} %pad_add_fusion.1.place_ref, s32[1]{0:T(128)S(6)} %copy.19.start_ref, s32[1,1024]{1,0:T(1,128)S(1)} %bitcast.15, f32[16,128]{1,0:T(8,128)S(1)} %copy-done.7, f32[16,32]{1,0:T(8,128)S(1)} %pad.4.pos_bias_ref), custom_call_target="tpu_custom_call" | custom-call | flops 33554432 | bytes 1048576 | tf_op jit(solution)/shard_map/bias/pallas_call | solution.py:213
  34.2 1.0 %plan.2.pick_ref = bf16[256,512]{1,0:T(8,128)(2,1)S(1)} custom-call(s32[2]{0:T(128)S(1)} %pad_add_fusion.1.place_ref, s32[1,64]{1,0:T(1,128)S(1)} %pad_add_fusion.2.refs_0_, s32[1,64]{1,0:T(1,128)S(1)} %collective-permute-done.9.refs_1_, s32[1,64]{1,0:T(1,128)S(1)} %collective-permute-done.10.refs_2_, s32[1,64]{1,0:T(1,128)S(1)} %collective-permute-done.11.refs_3_), custom_call_target="tpu_custom_call" | custom-call | flops 4194304 | bytes 1048576 | tf_op jit(solution)/shard_map/plan/pallas_call | solution.py:158
  35.3 0.1 collective-permute-start.16
  35.3 0.0 collective-permute-done.15.refs_1_
  35.4 0.5 collective-permute-start.17
  35.8 0.9 %broadcast_in_dim.16 = bf16[256,1024]{1,0:T(8,128)(2,1)} broadcast(bf16[]{:T(256)} %constant.6.clone.1), dimensions={} | broadcast | bytes 524290 | tf_op jit(solution)/shard_map/broadcast_in_dim | solution.py:440
  36.7 0.0 copy-start.6
  36.7 0.7 %while.10 = (s32[]{:T(128)}, bf16[256,1024]{1,0:T(8,128)(2,1)}, s32[1]{0:T(128)}, s32[]{:T(128)}, s32[1,64]{1,0:T(1,128)S(1)}, /*index=5*/s32[1,64]{1,0:T(1,128)...) while((s32[]{:T(128)}, bf16[256,1024]{1,0:T(8,128)(2,1)}, ...), condition=%wide.region_1.2_spmd, body=%wide.region_0.1_spmd.sunk | while | flops 75759616 | bytes 14942621 | solution.py:441
  37.4 0.0 collective-permute-done.16.refs_2_
  37.4 0.0 collective-permute-done.17.refs_3_
  37.4 0.0 copy-done.6
  37.5 0.0 copy-start.3
  37.5 1.6 %copy-done.3 = bf16[1024,1024]{1,0:T(8,128)(2,1)S(1)} copy-done((bf16[1024,1024]{1,0:T(8,128)(2,1)S(1)}, bf16[1024,1024]{1,0:T(8,128)(2,1)}, u32[]{:S(2)}) %copy-start.3) | copy-done | bytes 2097176
  39.0 1.6 %copy-done.5 = bf16[1024,1024]{1,0:T(8,128)(2,1)S(1)} copy-done((bf16[1024,1024]{1,0:T(8,128)(2,1)S(1)}, bf16[1024,1024]{1,0:T(8,128)(2,1)}, u32[]{:S(2)}) %copy-start.5) | copy-done | bytes 2097176
  40.6 8.3 %attend.1 = (bf16[16,1024]{1,0:T(8,128)(2,1)S(1)}, f32[128,1024]{1,0:T(8,128)S(1)}, bf16[128,1024]{1,0:T(8,128)(2,1)S(1)}) custom-call(s32[1]{0:T(128)} %get-tuple-element.154.rounds_ref, bf16[256,512]{1,0:T(8,128)(2,1)S(1)} %plan.2.pick_ref, bf16[128,1024]{1,0:T(8,128)(2,1)S(1)} %join.2.refs_0_, bf16[128,1024]{1,0:T(8,128)(2,1)S(1)} %collective-permute-done.15.refs_1_, ...), custom_call_target="tpu_custom_call" | custom-call | flops 2147483648 | bytes 4194304 | tf_op jit(solution)/shard_map/attend/pallas_call | solution.py:293
  48.9 0.1 collective-permute-start.18
  49.1 1.5 %collective-permute-done.18 = bf16[128,1024]{1,0:T(8,128)(2,1)S(1)} collective-permute-done((bf16[128,1024]{1,0:T(8,128)(2,1)S(1)}, bf16[128,1024]{1,0:T(8,128)(2,1)S(1)}, u32[]{:S(2)}, u32[]{:S(2)}) %collective-permute-start.18) | collective-permute-done | bytes 262176 | tf_op jit(solution)/shard_map/ppermute | solution.py:40
  50.5 0.1 convert_add_fusion
  50.6 1.6 %collective-permute-start.19 = (bf16[64,1024]{1,0:T(8,128)(2,1)S(1)}, bf16[64,1024]{1,0:T(8,128)(2,1)S(1)}, u32[]{:S(2)}, u32[]{:S(2)}) collective-permute-start(bf16[64,1024]{1,0:T(8,128)(2,1)S(1)} %slice.36), channel_id=1, source_target_pairs={{0,2},{1,3},{2,0},{3,1},{4,6},{5,7},{6,4},{7,5},{8,10},{9,11},{10,... | collective-permute-start | bytes 393224 | tf_op jit(solution)/shard_map/ppermute | solution.py:40
  52.2 4.0 %collective-permute-done.19 = bf16[64,1024]{1,0:T(8,128)(2,1)S(1)} collective-permute-done((bf16[64,1024]{1,0:T(8,128)(2,1)S(1)}, bf16[64,1024]{1,0:T(8,128)(2,1)S(1)}, u32[]{:S(2)}, u32[]{:S(2)}) %collective-permute-start.19) | collective-permute-done | bytes 131104 | tf_op jit(solution)/shard_map/ppermute | solution.py:40
  56.3 2.0 %collective-permute-start.22 = (bf16[16,1024]{1,0:T(8,128)(2,1)S(1)}, bf16[16,1024]{1,0:T(8,128)(2,1)S(1)}, u32[]{:S(2)}, u32[]{:S(2)}) collective-permute-start(bf16[16,1024]{1,0:T(8,128)(2,1)S(1)} %get-tuple-element.91), channel_id=1, source_target_pairs={{0,12},{1,13},{2,14},{3,15},{4,8},{5,9},{6,10},{7,11},{8,4},{9,5},... | collective-permute-start | bytes 98312 | tf_op jit(solution)/shard_map/ppermute | solution.py:40
  58.2 0.0 collective-permute-start.21
  58.3 2.4 %collective-permute-start.20 = (bf16[16,1024]{1,0:T(8,128)(2,1)S(1)}, bf16[16,1024]{1,0:T(8,128)(2,1)S(1)}, u32[]{:S(2)}, u32[]{:S(2)}) collective-permute-start(bf16[16,1024]{1,0:T(8,128)(2,1)S(1)} %get-tuple-element.93), channel_id=1, source_target_pairs={{0,4},{1,5},{2,6},{3,7},{4,0},{5,1},{6,2},{7,3},{8,12},{9,13},{10,... | collective-permute-start | bytes 98312 | tf_op jit(solution)/shard_map/ppermute | solution.py:40
  60.7 0.0 copy-done
  60.7 0.5 gates.1.refs_4_
  61.2 0.9 %collective-permute-done.22.refs_2_ = bf16[16,1024]{1,0:T(8,128)(2,1)S(1)} collective-permute-done((bf16[16,1024]{1,0:T(8,128)(2,1)S(1)}, bf16[16,1024]{1,0:T(8,128)(2,1)S(1)}, u32[]{:S(2)}, u32[]{:S(2)}) %collective-permute-start.22) | collective-permute-done | bytes 32800 | tf_op jit(solution)/shard_map/ppermute | solution.py:40
  62.1 0.9 %collective-permute-done.21.refs_1_ = bf16[16,1024]{1,0:T(8,128)(2,1)S(1)} collective-permute-done((bf16[16,1024]{1,0:T(8,128)(2,1)S(1)}, bf16[16,1024]{1,0:T(8,128)(2,1)S(1)}, u32[]{:S(2)}, u32[]{:S(2)}) %collective-permute-start.21) | collective-permute-done | bytes 32800 | tf_op jit(solution)/shard_map/ppermute | solution.py:40
  63.1 0.0 collective-permute-done.20.refs_0_
  63.1 0.0 copy-done.1
  63.1 0.0 copy-done.9
  63.1 1.2 %finish.1 = bf16[16,1024]{1,0:T(8,128)(2,1)} custom-call(f32[16,1024]{1,0:T(8,128)S(1)} %slice.30.own_ref, bf16[16,1024]{1,0:T(8,128)(2,1)S(1)} %collective-permute-done.20.refs_0_, bf16[16,1024]{1,0:T(8,128)(2,1)S(1)} %collective-permute-done.21.refs_1_, bf16[16,1024]{1,0:T(8,128)(2,1)S(1)} %collective-permute-done.22.refs_2_, ...), custom_call_target="tpu_custom_call" | custom-call | tf_op jit(solution)/shard_map/finish/pallas_call | solution.py:378
  (10 shorter events, 0.1 us)
Async XLA Ops:
  0.0 27.7 %copy-start.12 = (f32[16,18]{1,0:T(8,128)S(1)}, f32[16,18]{1,0:T(8,128)}, u32[]{:S(2)}) copy-start(f32[16,18]{1,0:T(8,128)} %param.23) | copy-start | bytes 3460
  0.0 6.8 %collective-permute-start.8 = (s32[1,16]{1,0:T(1,128)}, s32[1,16]{1,0:T(1,128)S(1)}, u32[]{:S(2)}, u32[]{:S(2)}) collective-permute-start(s32[1,16]{1,0:T(1,128)} %bitcast.17), channel_id=1, source_target_pairs={{0,12},{1,13},{2,14},{3,15},{4,8},{5,9},{6,10},{7,11},{8,4},{9,5},... | collective-permute-start | bytes 200 | tf_op jit(solution)/shard_map/ppermute | solution.py:40
  5.1 4.6 %collective-permute-start.7 = (s32[1,16]{1,0:T(1,128)}, s32[1,16]{1,0:T(1,128)S(1)}, u32[]{:S(2)}, u32[]{:S(2)}) collective-permute-start(s32[1,16]{1,0:T(1,128)} %bitcast.18), channel_id=1, source_target_pairs={{0,8},{1,9},{2,10},{3,11},{4,12},{5,13},{6,14},{7,15},{8,0},{9,1},... | collective-permute-start | bytes 200 | tf_op jit(solution)/shard_map/ppermute | solution.py:40
  5.1 4.6 %collective-permute-start.6 = (s32[1,16]{1,0:T(1,128)}, s32[1,16]{1,0:T(1,128)S(1)}, u32[]{:S(2)}, u32[]{:S(2)}) collective-permute-start(s32[1,16]{1,0:T(1,128)} %bitcast.19), channel_id=1, source_target_pairs={{0,4},{1,5},{2,6},{3,7},{4,0},{5,1},{6,2},{7,3},{8,12},{9,13},{10,... | collective-permute-start | bytes 200 | tf_op jit(solution)/shard_map/ppermute | solution.py:40
  10.4 3.0 %collective-permute-start.11 = (s32[1,64]{1,0:T(1,128)S(1)}, s32[1,64]{1,0:T(1,128)S(1)}, u32[]{:S(2)}, u32[]{:S(2)}) collective-permute-start(s32[1,64]{1,0:T(1,128)S(1)} %pad_add_fusion.2.refs_0_), channel_id=1, source_target_pairs={{0,3},{1,2},{2,1},{3,0},{4,7},{5,6},{6,5},{7,4},{8,11},{9,10},{10,... | collective-permute-start | bytes 776 | tf_op jit(solution)/shard_map/ppermute | solution.py:40
  10.4 3.0 %collective-permute-start.10 = (s32[1,64]{1,0:T(1,128)S(1)}, s32[1,64]{1,0:T(1,128)S(1)}, u32[]{:S(2)}, u32[]{:S(2)}) collective-permute-start(s32[1,64]{1,0:T(1,128)S(1)} %pad_add_fusion.2.refs_0_), channel_id=1, source_target_pairs={{0,1},{1,0},{2,3},{3,2},{4,5},{5,4},{6,7},{7,6},{8,9},{9,8},{10,11... | collective-permute-start | bytes 776 | tf_op jit(solution)/shard_map/ppermute | solution.py:40
  12.1 3.6 %collective-permute-start.9 = (s32[1,64]{1,0:T(1,128)S(1)}, s32[1,64]{1,0:T(1,128)S(1)}, u32[]{:S(2)}, u32[]{:S(2)}) collective-permute-start(s32[1,64]{1,0:T(1,128)S(1)} %pad_add_fusion.2.refs_0_), channel_id=1, source_target_pairs={{0,2},{1,3},{2,0},{3,1},{4,6},{5,7},{6,4},{7,5},{8,10},{9,11},{10,... | collective-permute-start | bytes 776 | tf_op jit(solution)/shard_map/ppermute | solution.py:40
  18.2 6.4 %collective-permute-start.14 = (bf16[32,1024]{1,0:T(8,128)(2,1)S(1)}, bf16[32,1024]{1,0:T(8,128)(2,1)S(1)}, u32[]{:S(2)}, u32[]{:S(2)}) collective-permute-start(bf16[32,1024]{1,0:T(8,128)(2,1)S(1)} %get-tuple-element.63.refs_0_), channel_id=1, source_target_pairs={{0,12},{1,13},{2,14},{3,15},{4,8},{5,9},{6,10},{7,11},{8,4},{9,5},... | collective-permute-start | bytes 196616 | tf_op jit(solution)/shard_map/ppermute | solution.py:40
  19.8 6.7 %collective-permute-start.13 = (bf16[32,1024]{1,0:T(8,128)(2,1)S(1)}, bf16[32,1024]{1,0:T(8,128)(2,1)S(1)}, u32[]{:S(2)}, u32[]{:S(2)}) collective-permute-start(bf16[32,1024]{1,0:T(8,128)(2,1)S(1)} %get-tuple-element.63.refs_0_), channel_id=1, source_target_pairs={{0,8},{1,9},{2,10},{3,11},{4,12},{5,13},{6,14},{7,15},{8,0},{9,1},... | collective-permute-start | bytes 196616 | tf_op jit(solution)/shard_map/ppermute | solution.py:40
  20.4 6.1 %collective-permute-start.12 = (bf16[32,1024]{1,0:T(8,128)(2,1)S(1)}, bf16[32,1024]{1,0:T(8,128)(2,1)S(1)}, u32[]{:S(2)}, u32[]{:S(2)}) collective-permute-start(bf16[32,1024]{1,0:T(8,128)(2,1)S(1)} %get-tuple-element.63.refs_0_), channel_id=1, source_target_pairs={{0,4},{1,5},{2,6},{3,7},{4,0},{5,1},{6,2},{7,3},{8,12},{9,13},{10,... | collective-permute-start | bytes 196616 | tf_op jit(solution)/shard_map/ppermute | solution.py:40
  26.5 8.9 %collective-permute-start.15 = (bf16[128,1024]{1,0:T(8,128)(2,1)S(1)}, bf16[128,1024]{1,0:T(8,128)(2,1)S(1)}, u32[]{:S(2)}, u32[]{:S(2)}) collective-permute-start(bf16[128,1024]{1,0:T(8,128)(2,1)S(1)} %join.2.refs_0_), channel_id=1, source_target_pairs={{0,2},{1,3},{2,0},{3,1},{4,6},{5,7},{6,4},{7,5},{8,10},{9,11},{10,... | collective-permute-start | bytes 786440 | tf_op jit(solution)/shard_map/ppermute | solution.py:40
  27.7 5.6 %copy-start.7 = (f32[16,128]{1,0:T(8,128)S(1)}, f32[16,128]{1,0:T(8,128)}, u32[]{:S(2)}) copy-start(f32[16,128]{1,0:T(8,128)} %time_bias_ref.1) | copy-start | bytes 24580
  27.7 5.6 %copy-start.8 = (s32[1024]{0:T(1024)S(1)}, s32[1024]{0:T(1024)}, u32[]{:S(2)}) copy-start(s32[1024]{0:T(1024)} %param.18) | copy-start | bytes 12292
  30.7 1.4 %copy-start.2 = (bf16[1024,1024]{1,0:T(8,128)(2,1)}, bf16[1024,1024]{1,0:T(8,128)(2,1)S(1)}, u32[]{:S(2)}) copy-start(bf16[1024,1024]{1,0:T(8,128)(2,1)S(1)} %get-tuple-element.66.refs_7_) | copy-start | bytes 6291460
  32.0 1.3 %copy-start.4 = (bf16[1024,1024]{1,0:T(8,128)(2,1)}, bf16[1024,1024]{1,0:T(8,128)(2,1)S(1)}, u32[]{:S(2)}) copy-start(bf16[1024,1024]{1,0:T(8,128)(2,1)S(1)} %get-tuple-element.67.refs_8_) | copy-start | bytes 6291460
  35.3 2.2 %collective-permute-start.16 = (bf16[128,1024]{1,0:T(8,128)(2,1)S(1)}, bf16[128,1024]{1,0:T(8,128)(2,1)}, u32[]{:S(2)}, u32[]{:S(2)}) collective-permute-start(bf16[128,1024]{1,0:T(8,128)(2,1)S(1)} %join.2.refs_0_), channel_id=1, source_target_pairs={{0,1},{1,0},{2,3},{3,2},{4,5},{5,4},{6,7},{7,6},{8,9},{9,8},{10,11... | collective-permute-start | bytes 786440 | tf_op jit(solution)/shard_map/ppermute | solution.py:40
  35.4 2.1 %collective-permute-start.17 = (bf16[128,1024]{1,0:T(8,128)(2,1)S(1)}, bf16[128,1024]{1,0:T(8,128)(2,1)}, u32[]{:S(2)}, u32[]{:S(2)}) collective-permute-start(bf16[128,1024]{1,0:T(8,128)(2,1)S(1)} %collective-permute-done.15.refs_1_), channel_id=1, source_target_pairs={{0,1},{1,0},{2,3},{3,2},{4,5},{5,4},{6,7},{7,6},{8,9},{9,8},{10,11... | collective-permute-start | bytes 786440 | tf_op jit(solution)/shard_map/ppermute | solution.py:40
  36.7 0.7 %copy-start.6 = (f32[1024]{0:T(1024)S(1)}, f32[1024]{0:T(1024)}, u32[]{:S(2)}) copy-start(f32[1024]{0:T(1024)} %param.20) | copy-start | bytes 12292
  37.5 1.6 %copy-start.3 = (bf16[1024,1024]{1,0:T(8,128)(2,1)S(1)}, bf16[1024,1024]{1,0:T(8,128)(2,1)}, u32[]{:S(2)}) copy-start(bf16[1024,1024]{1,0:T(8,128)(2,1)} %copy-done.2) | copy-start | bytes 6291460
  39.0 1.6 %copy-start.5 = (bf16[1024,1024]{1,0:T(8,128)(2,1)S(1)}, bf16[1024,1024]{1,0:T(8,128)(2,1)}, u32[]{:S(2)}) copy-start(bf16[1024,1024]{1,0:T(8,128)(2,1)} %copy-done.4) | copy-start | bytes 6291460
  40.6 20.1 %copy-start = (bf16[1024,2048]{1,0:T(8,128)(2,1)S(1)}, bf16[1024,2048]{1,0:T(8,128)(2,1)}, u32[]{:S(2)}) copy-start(bf16[1024,2048]{1,0:T(8,128)(2,1)} %proj_ref.1) | copy-start | bytes 12582916
  48.9 1.6 %collective-permute-start.18 = (bf16[128,1024]{1,0:T(8,128)(2,1)S(1)}, bf16[128,1024]{1,0:T(8,128)(2,1)S(1)}, u32[]{:S(2)}, u32[]{:S(2)}) collective-permute-start(bf16[128,1024]{1,0:T(8,128)(2,1)S(1)} %get-tuple-element.69), channel_id=1, source_target_pairs={{0,1},{1,0},{2,3},{3,2},{4,5},{5,4},{6,7},{7,6},{8,9},{9,8},{10,11... | collective-permute-start | bytes 786440 | tf_op jit(solution)/shard_map/ppermute | solution.py:40
  50.6 5.6 %collective-permute-start.19 = (bf16[64,1024]{1,0:T(8,128)(2,1)S(1)}, bf16[64,1024]{1,0:T(8,128)(2,1)S(1)}, u32[]{:S(2)}, u32[]{:S(2)}) collective-permute-start(bf16[64,1024]{1,0:T(8,128)(2,1)S(1)} %slice.36), channel_id=1, source_target_pairs={{0,2},{1,3},{2,0},{3,1},{4,6},{5,7},{6,4},{7,5},{8,10},{9,11},{10,... | collective-permute-start | bytes 393224 | tf_op jit(solution)/shard_map/ppermute | solution.py:40
  56.3 5.9 %collective-permute-start.22 = (bf16[16,1024]{1,0:T(8,128)(2,1)S(1)}, bf16[16,1024]{1,0:T(8,128)(2,1)S(1)}, u32[]{:S(2)}, u32[]{:S(2)}) collective-permute-start(bf16[16,1024]{1,0:T(8,128)(2,1)S(1)} %get-tuple-element.91), channel_id=1, source_target_pairs={{0,12},{1,13},{2,14},{3,15},{4,8},{5,9},{6,10},{7,11},{8,4},{9,5},... | collective-permute-start | bytes 98312 | tf_op jit(solution)/shard_map/ppermute | solution.py:40
  58.2 4.9 %collective-permute-start.21 = (bf16[16,1024]{1,0:T(8,128)(2,1)S(1)}, bf16[16,1024]{1,0:T(8,128)(2,1)S(1)}, u32[]{:S(2)}, u32[]{:S(2)}) collective-permute-start(bf16[16,1024]{1,0:T(8,128)(2,1)S(1)} %get-tuple-element.92), channel_id=1, source_target_pairs={{0,8},{1,9},{2,10},{3,11},{4,12},{5,13},{6,14},{7,15},{8,0},{9,1},... | collective-permute-start | bytes 98312 | tf_op jit(solution)/shard_map/ppermute | solution.py:40
  58.3 4.8 %collective-permute-start.20 = (bf16[16,1024]{1,0:T(8,128)(2,1)S(1)}, bf16[16,1024]{1,0:T(8,128)(2,1)S(1)}, u32[]{:S(2)}, u32[]{:S(2)}) collective-permute-start(bf16[16,1024]{1,0:T(8,128)(2,1)S(1)} %get-tuple-element.93), channel_id=1, source_target_pairs={{0,4},{1,5},{2,6},{3,7},{4,0},{5,1},{6,2},{7,3},{8,12},{9,13},{10,... | collective-permute-start | bytes 98312 | tf_op jit(solution)/shard_map/ppermute | solution.py:40
  60.7 2.4 %copy-start.1 = (bf16[1024,1024]{1,0:T(8,128)(2,1)S(1)}, bf16[1024,1024]{1,0:T(8,128)(2,1)}, u32[]{:S(2)}) copy-start(bf16[1024,1024]{1,0:T(8,128)(2,1)} %refs_6_.1) | copy-start | bytes 6291460
  60.7 2.4 %copy-start.9 = (f32[1024]{0:T(1024)S(1)}, f32[1024]{0:T(1024)}, u32[]{:S(2)}) copy-start(f32[1024]{0:T(1024)} %param.24) | copy-start | bytes 12292

commit v5 on v4

v5 whole, which is shorter than its diff:
```python
import functools

import jax
import jax.numpy as jnp
from jax import lax
from jax.experimental import pallas as pl
from jax.experimental.pallas import tpu as pltpu
from jax.sharding import PartitionSpec as P


BF16 = jnp.bfloat16
F32 = jnp.float32
LANES = 128
ROWS_AT_ONCE = 256
EVENTS_AT_ONCE = 1024
NT = (((1,), (1,)), ((), ()))
VMEM = pl.BlockSpec(memory_space=pltpu.VMEM)
SMEM = pl.BlockSpec(memory_space=pltpu.SMEM)
HBM = pl.BlockSpec(memory_space=pltpu.HBM)


def params(mib):
    return pltpu.CompilerParams(vmem_limit_bytes=mib << 20)


PARTNER = 1


def stage_masks(size):
    bits = [1 << k for k in range(1, size.bit_length() - 1)][::-1]
    far = bits[:-1]
    return [sorted(far[k : k + 2]) for k in range(0, len(far), 2)] + [bits[-1:]]


def combos(bits):
    out = [0]
    for b in bits:
        out = out + [m | b for m in out]
    return out


def swap(x, mask, axis, size):
    return lax.ppermute(x, axis, [(i, i ^ mask) for i in range(size)])


def join_kernel(*refs):
    *parts, out_ref = refs
    rows = parts[0].shape[0]
    for k, p in enumerate(parts):
        out_ref[k * rows : (k + 1) * rows, :] = p[...]


def join(pieces, dim):
    if dim:
        return jnp.concatenate(pieces, axis=dim)
    rows, width = pieces[0].shape
    return pl.pallas_call(
        join_kernel,
        out_shape=jax.ShapeDtypeStruct((len(pieces) * rows, width), BF16),
        in_specs=[VMEM] * len(pieces),
        out_specs=VMEM,
        compiler_params=params(16),
        name="join",
    )(*pieces)


def gather_relative(x, dim, axis, size):
    *far, near = stage_masks(size)
    for bits in far:
        x = join([x] + [swap(x, m, axis, size) for m in combos(bits)[1:]], dim)
    return [x, swap(x, near[0], axis, size)]


def position_bits(size):
    return [b for stage in stage_masks(size) for b in stage]


def candidates_info(ids_refs, me, size, table_rows):
    ids = jnp.concatenate([r[...] for r in ids_refs], axis=1)
    count = ids.shape[1]
    each = count // (size // 2)
    owner = ids // table_rows
    place = lax.broadcasted_iota(jnp.int32, (1, count), 1)
    block = place // each
    mask = jnp.zeros_like(place)
    for k, b in enumerate(position_bits(size)):
        mask = mask + ((block >> k) & 1) * b
    pair = owner >> 1
    key = pair * count + ((mask ^ me) >> 1) * each + place % each
    return pair, key, ids - owner * table_rows + ((owner ^ me) & 1) * table_rows


def to_column(row):
    count = row.shape[1]
    r = lax.broadcasted_iota(jnp.int32, (count, count), 0)
    c = lax.broadcasted_iota(jnp.int32, (count, count), 1)
    return jnp.sum(jnp.where(r == c, row, 0), axis=1, keepdims=True)


def lookup_kernel(place_ref, *refs, size, resident):
    if resident:
        *ids_refs, own_ref, other_ref, out_ref, rounds_ref = refs
        copies = []
    else:
        *ids_refs, own_hbm, other_hbm, out_ref, rounds_ref, own_ref, other_ref, sems = refs
        copies = [
            pltpu.make_async_copy(own_hbm, own_ref, sems.at[0]),
            pltpu.make_async_copy(other_hbm, other_ref, sems.at[1]),
        ]
    for c in copies:
        c.start()
    me, turn = place_ref[0], place_ref[1]
    slots = out_ref.shape[0]
    rows = own_ref.shape[0]
    pair, key, offset = candidates_info(ids_refs, me, size, rows)
    count = pair.shape[1]
    key_col = to_column(key)
    before = (key_col < key) & (key_col >= pair * count)
    rank = jnp.sum(before.astype(jnp.int32), axis=0, keepdims=True)
    slot = lax.broadcasted_iota(jnp.int32, (slots, count), 0) + turn * slots
    hit = (pair == (me >> 1)) & (rank == slot)
    want = jnp.sum(jnp.where(hit, offset + 1, 0), axis=1, keepdims=True) - 1
    row = lax.broadcasted_iota(jnp.int32, (slots, rows), 1)
    rounds_ref[0] = jnp.max(rank) // slots + 1
    for c in copies:
        c.wait()
    found = jnp.dot((want == row).astype(F32).astype(BF16), own_ref[...], preferred_element_type=F32)
    other = (want == row + rows).astype(F32).astype(BF16)
    out_ref[...] = (found + jnp.dot(other, other_ref[...], preferred_element_type=F32)).astype(BF16)


def lookup(place, ids, tables, slots, size, resident):
    if not resident:
        tables = [pltpu.with_memory_space_constraint(t, pltpu.HBM) for t in tables]
    rows, width = tables[0].shape
    return pl.pallas_call(
        functools.partial(lookup_kernel, size=size, resident=resident),
        out_shape=(
            jax.ShapeDtypeStruct((slots, width), BF16),
            jax.ShapeDtypeStruct((1,), jnp.int32),
        ),
        in_specs=[SMEM] + [VMEM] * len(ids) + [VMEM if resident else HBM] * 2,
        out_specs=(VMEM, SMEM),
        scratch_shapes=[]
        if resident
        else [pltpu.VMEM((rows, width), BF16)] * 2 + [pltpu.SemaphoreType.DMA((2,))],
        compiler_params=params(16),
        name="lookup",
    )(place, *ids, *tables)


def plan_kernel(place_ref, *refs, size, slots, table_rows):
    *ids_refs, pick_ref = refs
    me, turn = place_ref[0], place_ref[1]
    pair, key, _ = candidates_info(ids_refs, me, size, table_rows)
    count = pair.shape[1]
    key_col = to_column(key)
    pair_col = key_col // count
    before = (key < key_col) & (key >= pair_col * count)
    rank = jnp.sum(before.astype(jnp.int32), axis=1, keepdims=True)
    away = pair_col ^ (me >> 1)
    block = jnp.zeros_like(away)
    for k, b in enumerate(position_bits(size)):
        block = block + jnp.where((away & (b >> 1)) != 0, 1 << k, 0)
    mine = rank - turn * slots
    slot = jnp.where((mine >= 0) & (mine < slots), block * slots + mine, -1)
    pick = slot == lax.broadcasted_iota(jnp.int32, pick_ref.shape, 1)
    pick_ref[...] = pick.astype(F32).astype(BF16)


def plan(place, ids, slots, table_rows, size):
    count = sum(i.shape[1] for i in ids)
    return pl.pallas_call(
        functools.partial(plan_kernel, size=size, slots=slots, table_rows=table_rows),
        out_shape=jax.ShapeDtypeStruct((count, size // 2 * slots), BF16),
        in_specs=[SMEM] + [VMEM] * len(ids),
        out_specs=VMEM,
        compiler_params=params(16),
        name="plan",
    )(place, *ids)


def select_kernel(pick_ref, rows_ref, out_ref):
    out_ref[...] = jnp.dot(pick_ref[...], rows_ref[...], preferred_element_type=F32).astype(BF16)


def select(pick, pieces):
    rows = jnp.concatenate(pieces, axis=0)
    return pl.pallas_call(
        select_kernel,
        out_shape=jax.ShapeDtypeStruct((pick.shape[0], rows.shape[1]), BF16),
        in_specs=[VMEM, VMEM],
        out_specs=VMEM,
        compiler_params=params(32),
        name="select",
    )(pick, rows)


def three_parts(x):
    high = x.astype(BF16)
    rest = x - high.astype(F32)
    middle = rest.astype(BF16)
    return [high, middle, (rest - middle.astype(F32)).astype(BF16)]


def prepare_kernel(
    place_ref, start_ref, times_hbm, time_bias_hbm, pos_bias_hbm, table_hbm, out_ref, table_ref,
    times_ref, time_bias_ref, pos_bias_ref, sems, *, npos, history
):
    pairs = ((times_hbm, times_ref), (time_bias_hbm, time_bias_ref), (pos_bias_hbm, pos_bias_ref), (table_hbm, table_ref))
    copies = [pltpu.make_async_copy(a, b, sems.at[k]) for k, (a, b) in enumerate(pairs)]
    for c in copies:
        c.start()
    events = times_ref.shape[1]
    first = history - start_ref[0] - place_ref[0] * events
    distance = first - lax.broadcasted_iota(jnp.int32, (1, events), 1)
    bucket = jnp.zeros((1, events), jnp.int32)
    for k in range(1, npos):
        bucket = bucket + (distance >= (1 << k)).astype(jnp.int32)
    for c in copies[:3]:
        c.wait()
    columns = []
    for table_ref_, index in ((time_bias_ref, times_ref[...]), (pos_bias_ref, bucket)):
        table = jnp.concatenate(three_parts(table_ref_[...] * 0.5), axis=0)
        kinds = table.shape[1]
        hot = lax.broadcasted_iota(jnp.int32, (kinds, events), 0) == index
        columns.append(jnp.dot(table, hot.astype(F32).astype(BF16), preferred_element_type=F32))
    used = sum(c.shape[0] for c in columns)
    columns.append(jnp.zeros((LANES - used, events), F32))
    out_ref[...] = jnp.concatenate(columns, axis=0).T.astype(BF16)
    copies[3].wait()


def prepare(place, start, times, time_bias, pos_bias, table, history):
    arrays = [times, time_bias, pos_bias, table]
    return pl.pallas_call(
        functools.partial(prepare_kernel, npos=pos_bias.shape[1], history=history),
        out_shape=(
            jax.ShapeDtypeStruct((times.shape[1], LANES), BF16),
            jax.ShapeDtypeStruct(table.shape, BF16),
        ),
        in_specs=[SMEM, SMEM] + [HBM] * 4,
        out_specs=(VMEM, VMEM),
        scratch_shapes=[pltpu.VMEM(a.shape, a.dtype) for a in arrays[:3]] + [pltpu.SemaphoreType.DMA((4,))],
        compiler_params=params(8),
        name="prepare",
    )(place, start, *(pltpu.with_memory_space_constraint(a, pltpu.HBM) for a in arrays))


def silu(x):
    return x / (1.0 + jnp.exp(-x))


def normalise(embedded, gain):
    x = embedded.astype(F32)
    meansq = jnp.mean(x * x, axis=-1, keepdims=True)
    return (x * lax.rsqrt(meansq + 1e-06) * gain).astype(BF16)


def attend_kernel(rounds_ref, pick_ref, *refs, heads, blocks):
    *row_refs, extra_hbm, gain_ref, proj_ref = refs[: -6 - 3 * blocks]
    caches = refs[-6 - 3 * blocks : -6]
    own_ref, keep_ref, send_ref, emb_ref, query_ref, sem = refs[-6:]
    count, width = emb_ref.shape
    rows = jnp.concatenate([r[...] for r in row_refs], axis=0)
    emb_ref[...] = jnp.dot(pick_ref[...], rows, preferred_element_type=F32).astype(BF16)

    @pl.when(rounds_ref[0] > 1)
    def _():
        extra = pltpu.make_async_copy(extra_hbm, query_ref, sem)
        extra.start()
        extra.wait()
        emb_ref[...] = emb_ref[...] + query_ref[...]

    own_ref[...] = emb_ref[: own_ref.shape[0], :]
    head_dim = width // heads
    half = count // 2
    rows = min(ROWS_AT_ONCE, count)
    per = LANES // head_dim
    for first in range(0, count, rows):
        normed = normalise(emb_ref[first : first + rows, :], gain_ref[...])
        projected = jnp.dot(normed, proj_ref[...], preferred_element_type=F32)
        query = silu(projected).astype(BF16)
        query_ref[first : first + rows, :] = query * jnp.asarray(0.5 * head_dim**-0.5, BF16)
        lane = lax.broadcasted_iota(jnp.int32, (rows, LANES), 1)
        for group in range(heads // per):
            at = slice(group * LANES, (group + 1) * LANES)
            part = query_ref[first : first + rows, at]
            zero, one = jnp.zeros_like(part), jnp.ones_like(part)
            stacked = []
            for k in range(per):
                own = jnp.where(lane // head_dim == k, part, zero)
                chosen = jnp.where(lane % heads == group * per + k, one, zero)
                stacked.append(jnp.concatenate([own, chosen], axis=1))
            left = jnp.concatenate(stacked, axis=0)
            total = jnp.zeros((per * rows, LANES), F32)
            for key_ref, value_ref, bias_ref in zip(*(caches[k * blocks : (k + 1) * blocks] for k in range(3))):
                step = min(EVENTS_AT_ONCE, key_ref.shape[0])
                for j in range(0, key_ref.shape[0], step):
                    right = jnp.concatenate([key_ref[j : j + step, at], bias_ref[j : j + step, :]], axis=1)
                    t = lax.dot_general(left, right, NT, preferred_element_type=F32)
                    weights = (t + t * jnp.tanh(t)).astype(BF16)
                    total = total + jnp.dot(weights, value_ref[j : j + step, at], preferred_element_type=F32)
            out = total[:rows]
            for k in range(1, per):
                out = jnp.where(lane // head_dim == k, total[k * rows : (k + 1) * rows], out)
            if first + rows <= half:
                keep_ref[first : first + rows, at] = out
            elif first >= half:
                send_ref[first - half : first - half + rows, at] = out.astype(BF16)
            else:
                keep_ref[first:half, at] = out[: half - first]
                send_ref[: first + rows - half, at] = out[half - first :].astype(BF16)


def attend(rounds, pick, pieces, extra, gain, proj, keys, values, biases, heads, each):
    count, width = extra.shape
    blocks = len(keys)
    return pl.pallas_call(
        functools.partial(attend_kernel, heads=heads, blocks=blocks),
        out_shape=(
            jax.ShapeDtypeStruct((each, width), BF16),
            jax.ShapeDtypeStruct((count // 2, width), F32),
            jax.ShapeDtypeStruct((count // 2, width), BF16),
        ),
        in_specs=[SMEM, VMEM] + [VMEM] * len(pieces) + [HBM] + [VMEM] * (2 + 3 * blocks),
        out_specs=(VMEM, VMEM, VMEM),
        scratch_shapes=[
            pltpu.VMEM((count, width), BF16),
            pltpu.VMEM((count, width), BF16),
            pltpu.SemaphoreType.DMA,
        ],
        compiler_params=params(24),
        cost_estimate=pl.CostEstimate(
            flops=8 * count * width * blocks * keys[0].shape[0],
            transcendentals=count * heads * blocks * keys[0].shape[0],
            bytes_accessed=4 * blocks * keys[0].size,
        ),
        name="attend",
    )(rounds, pick, *pieces, extra, gain, proj, *keys, *values, *biases)


def stage_kernel(*refs, width):
    *refs, sems = refs
    count = len(refs) // 2
    copies = [
        pltpu.make_async_copy(
            a if a.shape[1] == width else a.at[:, pl.ds(0, width)], b, sems.at[k]
        )
        for k, (a, b) in enumerate(zip(refs[:count], refs[count:]))
    ]
    for c in copies:
        c.start()
    for c in copies:
        c.wait()


def stage(width, *arrays):
    return pl.pallas_call(
        functools.partial(stage_kernel, width=width),
        out_shape=tuple(jax.ShapeDtypeStruct((a.shape[0], width), BF16) for a in arrays),
        in_specs=[HBM] * len(arrays),
        out_specs=(VMEM,) * len(arrays),
        scratch_shapes=[pltpu.SemaphoreType.DMA((len(arrays),))],
        compiler_params=params(4),
        name="stage",
    )(*(pltpu.with_memory_space_constraint(a, pltpu.HBM) for a in arrays))


def gates_kernel(emb_ref, gain_ref, proj_ref, out_ref):
    normed = normalise(emb_ref[...], gain_ref[...])
    projected = jnp.dot(normed, proj_ref[...], preferred_element_type=F32)
    out_ref[...] = silu(projected).astype(BF16)


def gates_of(embedded, gain, proj_in):
    return pl.pallas_call(
        gates_kernel,
        out_shape=jax.ShapeDtypeStruct(embedded.shape, BF16),
        grid=(1,),
        in_specs=[VMEM, VMEM, pl.BlockSpec(proj_in.shape[:1] * 2, lambda i: (0, 1))],
        out_specs=VMEM,
        compiler_params=params(16),
        cost_estimate=pl.CostEstimate(flops=1 << 26, transcendentals=1 << 14, bytes_accessed=1 << 22),
        name="gates",
    )(embedded, gain, proj_in)


def finish_kernel(own_ref, *refs):
    *parts, emb_ref, gates_ref, gain_ref, proj_ref, out_ref = refs
    attended = own_ref[...]
    for p in parts:
        attended = attended + p[...].astype(F32)
    centred = attended - jnp.mean(attended, axis=-1, keepdims=True)
    variance = jnp.mean(centred * centred, axis=-1, keepdims=True)
    gated = centred * lax.rsqrt(variance + 1e-05) * gain_ref[...] * gates_ref[...].astype(F32)
    product = jnp.dot(gated.astype(BF16), proj_ref[...], preferred_element_type=F32)
    out_ref[...] = (emb_ref[...].astype(F32) + product).astype(BF16)


def finish(own, parts, embedded, gates, gain, proj_out):
    return pl.pallas_call(
        finish_kernel,
        out_shape=jax.ShapeDtypeStruct(embedded.shape, BF16),
        in_specs=[VMEM] * (len(parts) + 5),
        out_specs=VMEM,
        compiler_params=params(16),
        name="finish",
    )(own, *parts, embedded, gates, gain, proj_out)


def on_device(
    item_ids,
    item_table,
    key_cache,
    value_cache,
    time_buckets,
    window_start,
    norm_gain,
    proj_in,
    time_bias,
    pos_bias,
    out_gain,
    proj_out,
):
    axis = "hist"
    size = lax.axis_size(axis)
    me = lax.axis_index(axis).astype(jnp.int32)
    each = item_ids.shape[0]
    slots = 2 * each
    heads = time_bias.shape[0]
    events, width = key_cache.shape
    table_rows = item_table.shape[0]
    gain = norm_gain[None, :]

    def place(turn):
        return jnp.stack([me, jnp.asarray(turn, jnp.int32)])

    def partners(x):
        return swap(x, PARTNER, axis, size)

    here = place(0)
    other_table = partners(item_table)
    other_keys = partners(key_cache)
    other_values = partners(value_cache)
    bias, own_table = prepare(
        here, window_start, time_buckets[None, :], time_bias, pos_bias, item_table, 2 * events * size
    )
    other_bias = partners(bias)
    ids = gather_relative(item_ids[None, :], 1, axis, size)

    found, rounds = lookup(here, ids, [own_table, other_table], slots, size, True)
    pieces = gather_relative(found, 0, axis, size)
    pick = plan(here, ids, slots, table_rows, size)

    def more(state):
        turn, so_far = state
        picked = plan(place(turn), ids, slots, table_rows, size)
        found, _ = lookup(place(turn), ids, [item_table, other_table], slots, size, False)
        return turn + 1, so_far + select(picked, gather_relative(found, 0, axis, size))

    none = jnp.zeros((each * (size // 2), width), BF16)
    _, extra = lax.while_loop(lambda s: s[0] < rounds[0], more, (jnp.int32(1), none))

    proj, keys, values = stage(width, proj_in, key_cache, value_cache)
    other_keys, other_values = stage(width, other_keys, other_values)
    own, keep, send = attend(
        rounds, pick, pieces, extra, gain, proj, [keys, other_keys], [values, other_values], [bias, other_bias], heads, each
    )
    gates = gates_of(own, gain, proj_in)

    *far, near = stage_masks(size)
    total = keep + swap(send, near[0], axis, size).astype(F32)
    for bits in far[::-1]:
        masks = combos(bits)
        block = total.shape[0] // len(masks)
        parts = [
            swap(total[k * block : (k + 1) * block].astype(BF16), m, axis, size)
            for k, m in enumerate(masks)
            if k
        ]
        if bits is far[0]:
            break
        total = sum([p.astype(F32) for p in parts], total[:block])
    return finish(total[:block], parts, own, gates, out_gain[None, :], proj_out)


def solution(mesh):
    placed = (
        P(("grp", "hist")),
        P("hist", None),
        P(("grp", "hist"), None),
        P(("grp", "hist"), None),
        P(("grp", "hist")),
        P("grp"),
        P(),
        P(),
        P(),
        P(),
        P(),
        P(),
    )

    return jax.shard_map(on_device, mesh=mesh, in_specs=placed, out_specs=P(("grp", "hist"), None), check_vma=False)
```

time: 64.5 us -> 74.7 us (1.16)
  local copies, waits for them, and re-layouts: 6.79 us -> 12.6 us
  starting transfers between devices: 19.6 us -> 22.8 us
  waiting for transfers between devices: 18.1 us -> 19.2 us
  Pallas kernels: 17.3 us -> 18.1 us
    unnamed x22 -> x28, local copies, waits for them, and re-layouts: 5.89 us -> 11.8 us
    ppermute x17 -> x16, starting transfers between devices: 19.6 us -> 22.8 us  [swap(): return lax.ppermute(x, axis, [(i, i ^ mask) for i in range(size)])]
    ppermute x17 -> x16, waiting for transfers between devices: 18.1 us -> 19.2 us  [swap(): return lax.ppermute(x, axis, [(i, i ^ mask) for i in range(size)])]
    pallas_call x4 -> x5, Pallas kernels: 14.6 us -> 15.6 us  [the longest x1 6.23 us: attend(): pl.pallas_call(functools.partial(attend_kernel, heads=heads, blocks=block...]
  transfers between devices with their start and end apart: 17 -> 16, of which waited for: 10 -> 8; matrix products, arithmetic and copies ran while one was open for 1% -> 1% of each run, Pallas kernels for 8% -> 14%
where the time goes in v5:
time: 74.7 us; the launch traced here: 74.4 us
  starting transfers between devices  22.8 us (31%)
  waiting for transfers between devices  19.2 us (26%)
  Pallas kernels  18.1 us (24%)
  local copies, waits for them, and re-layouts  12.6 us (17%)
  between operations  0.81 us (1%)
    ppermute x16, starting transfers between devices, swap(): return lax.ppermute(x, axis, [(i, i ^ mask) for i in range(size)])  22.8 us
    ppermute x16, waiting for transfers between devices, swap(): return lax.ppermute(x, axis, [(i, i ^ mask) for i in range(size)])  19.2 us
    unnamed x28, local copies, waits for them, and re-layouts  11.8 us
    pallas_call x1, Pallas kernels, attend(): pl.pallas_call(functools.partial(attend_kernel, heads=heads, blocks=block...  6.23 us
    pallas_call x2, Pallas kernels, stage(): pl.pallas_call(functools.partial(stage_kernel, width=width), out_shape=tu...  5.12 us
    pallas_call x1, Pallas kernels, prepare(): pl.pallas_call(functools.partial(prepare_kernel, npos=pos_bias.shape[1],...  2.21 us
    pallas_call x1, Pallas kernels, lookup(): pl.pallas_call(functools.partial(lookup_kernel, size=size, resident=resid...  2.02 us
  transfers between devices with their start and end apart: 16, of which 8 were waited for; matrix products, arithmetic and copies ran while one was open for 1% of the time, Pallas kernels for 14%

profile of v5, /device:TPU:0, one launch (start us, length us, event | category | flops | bytes accessed | tf_op | source)
XLA Modules:
  0.0 74.4 jit_solution(11453848723786556627)
XLA Ops:
  0.0 0.0 copy-start.13
  0.0 0.5 collective-permute-start.8
  0.5 0.1 collective-permute-start.13
  0.6 0.4 collective-permute-start.14
  1.7 0.1 pad_add_fusion.1.place_ref
  1.7 2.2 %prepare.1 = (bf16[1024,128]{1,0:T(8,128)(2,1)S(1)}, bf16[1024,1024]{1,0:T(8,128)(2,1)S(1)}) custom-call(s32[2]{0:T(128)S(1)} %pad_add_fusion.1.place_ref, s32[1]{0:T(128)S(6)} %copy.19.start_ref, s32[1,1024]{1,0:T(1,128)} %bitcast.16, f32[16,128]{1,0:T(8,128)} %time_bias_hbm.1, f32[16,18]{1,0:T(8,128)} %pos_bias_hbm.1, bf16[1024,1024]{1,0:T(8,128)(2,1)} %table_hbm.1), custom_call_target="tpu_custom_call" | custom-call | tf_op jit(solution)/shard_map/prepare/pallas_call | solution.py:236
  4.0 0.1 collective-permute-start.15
  4.1 0.0 copy-done.13
  4.1 5.0 %collective-permute-start.6 = (s32[1,16]{1,0:T(1,128)S(1)}, s32[1,16]{1,0:T(1,128)S(1)}, u32[]{:S(2)}, u32[]{:S(2)}) collective-permute-start(s32[1,16]{1,0:T(1,128)S(1)} %bitcast.17), channel_id=1, source_target_pairs={{0,12},{1,13},{2,14},{3,15},{4,8},{5,9},{6,10},{7,11},{8,4},{9,5},... | collective-permute-start | bytes 200 | tf_op jit(solution)/shard_map/ppermute | solution.py:43
  9.1 1.5 %collective-permute-done.6 = s32[1,16]{1,0:T(1,128)S(1)} collective-permute-done((s32[1,16]{1,0:T(1,128)S(1)}, s32[1,16]{1,0:T(1,128)S(1)}, u32[]{:S(2)}, u32[]{:S(2)}) %collective-permute-start.6) | collective-permute-done | bytes 96 | tf_op jit(solution)/shard_map/ppermute | solution.py:43
  10.7 1.0 %collective-permute-start.5 = (s32[1,16]{1,0:T(1,128)S(1)}, s32[1,16]{1,0:T(1,128)S(1)}, u32[]{:S(2)}, u32[]{:S(2)}) collective-permute-start(s32[1,16]{1,0:T(1,128)S(1)} %bitcast.18), channel_id=1, source_target_pairs={{0,8},{1,9},{2,10},{3,11},{4,12},{5,13},{6,14},{7,15},{8,0},{9,1},... | collective-permute-start | bytes 200 | tf_op jit(solution)/shard_map/ppermute | solution.py:43
  11.7 3.5 %collective-permute-done.5 = s32[1,16]{1,0:T(1,128)S(1)} collective-permute-done((s32[1,16]{1,0:T(1,128)S(1)}, s32[1,16]{1,0:T(1,128)S(1)}, u32[]{:S(2)}, u32[]{:S(2)}) %collective-permute-start.5) | collective-permute-done | bytes 96 | tf_op jit(solution)/shard_map/ppermute | solution.py:43
  15.1 1.5 %collective-permute-start.4 = (s32[1,16]{1,0:T(1,128)S(1)}, s32[1,16]{1,0:T(1,128)S(1)}, u32[]{:S(2)}, u32[]{:S(2)}) collective-permute-start(s32[1,16]{1,0:T(1,128)S(1)} %bitcast.19), channel_id=1, source_target_pairs={{0,4},{1,5},{2,6},{3,7},{4,0},{5,1},{6,2},{7,3},{8,12},{9,13},{10,... | collective-permute-start | bytes 200 | tf_op jit(solution)/shard_map/ppermute | solution.py:43
  16.6 2.1 %collective-permute-done.4 = s32[1,16]{1,0:T(1,128)S(1)} collective-permute-done((s32[1,16]{1,0:T(1,128)S(1)}, s32[1,16]{1,0:T(1,128)S(1)}, u32[]{:S(2)}, u32[]{:S(2)}) %collective-permute-start.4) | collective-permute-done | bytes 96 | tf_op jit(solution)/shard_map/ppermute | solution.py:43
  18.7 0.1 pad_add_fusion.2.refs_0_
  18.8 1.7 %collective-permute-start.7 = (s32[1,64]{1,0:T(1,128)S(1)}, s32[1,64]{1,0:T(1,128)S(1)}, u32[]{:S(2)}, u32[]{:S(2)}) collective-permute-start(s32[1,64]{1,0:T(1,128)S(1)} %pad_add_fusion.2.refs_0_), channel_id=1, source_target_pairs={{0,2},{1,3},{2,0},{3,1},{4,6},{5,7},{6,4},{7,5},{8,10},{9,11},{10,... | collective-permute-start | bytes 776 | tf_op jit(solution)/shard_map/ppermute | solution.py:43
  20.5 1.8 %collective-permute-done.7.refs_1_ = s32[1,64]{1,0:T(1,128)S(1)} collective-permute-done((s32[1,64]{1,0:T(1,128)S(1)}, s32[1,64]{1,0:T(1,128)S(1)}, u32[]{:S(2)}, u32[]{:S(2)}) %collective-permute-start.7) | collective-permute-done | bytes 288 | tf_op jit(solution)/shard_map/ppermute | solution.py:43
  22.4 0.0 collective-permute-done.8.refs_3_
  22.4 0.0 copy-start.12
  22.4 2.0 %lookup.2 = (bf16[32,1024]{1,0:T(8,128)(2,1)S(1)}, s32[1]{0:T(128)}) custom-call(s32[2]{0:T(128)S(1)} %pad_add_fusion.1.place_ref, s32[1,64]{1,0:T(1,128)S(1)} %pad_add_fusion.2.refs_0_, s32[1,64]{1,0:T(1,128)S(1)} %collective-permute-done.7.refs_1_, bf16[1024,1024]{1,0:T(8,128)(2,1)S(1)} %get-tuple-element.61.refs_2_, ...), custom_call_target="tpu_custom_call" | custom-call | tf_op jit(solution)/shard_map/lookup/pallas_call | solution.py:136
  24.4 0.0 copy-done.12
  24.4 3.9 %collective-permute-start.11 = (bf16[32,1024]{1,0:T(8,128)(2,1)S(1)}, bf16[32,1024]{1,0:T(8,128)(2,1)S(1)}, u32[]{:S(2)}, u32[]{:S(2)}) collective-permute-start(bf16[32,1024]{1,0:T(8,128)(2,1)S(1)} %get-tuple-element.63.refs_0_), channel_id=1, source_target_pairs={{0,12},{1,13},{2,14},{3,15},{4,8},{5,9},{6,10},{7,11},{8,4},{9,5},... | collective-permute-start | bytes 196616 | tf_op jit(solution)/shard_map/ppermute | solution.py:43
  28.3 0.0 collective-permute-start.10
  28.3 0.0 collective-permute-done.13.refs_0_
  28.3 0.6 collective-permute-start.9
  28.9 2.9 %stage.2 = (bf16[1024,1024]{1,0:T(8,128)(2,1)S(1)}, bf16[1024,1024]{1,0:T(8,128)(2,1)S(1)}, bf16[1024,1024]{1,0:T(8,128)(2,1)S(1)}) custom-call(bf16[1024,2048]{1,0:T(8,128)(2,1)} %proj_ref.1, bf16[1024,1024]{1,0:T(8,128)(2,1)} %refs_1_.1, bf16[1024,1024]{1,0:T(8,128)(2,1)} %refs_2_.1), custom_call_target="tpu_custom_call" | custom-call | tf_op jit(solution)/shard_map/stage/pallas_call | solution.py:359
  31.8 0.0 copy-start.2
  31.8 1.4 %copy-done.2 = bf16[1024,1024]{1,0:T(8,128)(2,1)} copy-done((bf16[1024,1024]{1,0:T(8,128)(2,1)}, bf16[1024,1024]{1,0:T(8,128)(2,1)S(1)}, u32[]{:S(2)}) %copy-start.2) | copy-done | bytes 2097176
  33.2 0.0 copy-start.4
  33.2 1.3 %copy-done.4 = bf16[1024,1024]{1,0:T(8,128)(2,1)} copy-done((bf16[1024,1024]{1,0:T(8,128)(2,1)}, bf16[1024,1024]{1,0:T(8,128)(2,1)S(1)}, u32[]{:S(2)}) %copy-start.4) | copy-done | bytes 2097176
  34.5 0.9 %plan.2.pick_ref = bf16[128,256]{1,0:T(8,128)(2,1)S(1)} custom-call(s32[2]{0:T(128)S(1)} %pad_add_fusion.1.place_ref, s32[1,64]{1,0:T(1,128)S(1)} %pad_add_fusion.2.refs_0_, s32[1,64]{1,0:T(1,128)S(1)} %collective-permute-done.7.refs_1_), custom_call_target="tpu_custom_call" | custom-call | tf_op jit(solution)/shard_map/plan/pallas_call | solution.py:173
  35.4 0.0 collective-permute-done.14.refs_1_
  35.4 2.2 %stage.3 = (bf16[1024,1024]{1,0:T(8,128)(2,1)S(1)}, bf16[1024,1024]{1,0:T(8,128)(2,1)S(1)}) custom-call(bf16[1024,1024]{1,0:T(8,128)(2,1)} %collective-permute-done.13.refs_0_, bf16[1024,1024]{1,0:T(8,128)(2,1)} %collective-permute-done.14.refs_1_), custom_call_target="tpu_custom_call" | custom-call | tf_op jit(solution)/shard_map/stage/pallas_call | solution.py:359
  37.7 0.0 copy-start.6
  37.7 1.4 %copy-done.6 = bf16[1024,1024]{1,0:T(8,128)(2,1)} copy-done((bf16[1024,1024]{1,0:T(8,128)(2,1)}, bf16[1024,1024]{1,0:T(8,128)(2,1)S(1)}, u32[]{:S(2)}) %copy-start.6) | copy-done | bytes 2097176
  39.1 0.0 copy-start.8
  39.1 1.4 %copy-done.8 = bf16[1024,1024]{1,0:T(8,128)(2,1)} copy-done((bf16[1024,1024]{1,0:T(8,128)(2,1)}, bf16[1024,1024]{1,0:T(8,128)(2,1)S(1)}, u32[]{:S(2)}) %copy-start.8) | copy-done | bytes 2097176
  40.4 0.0 collective-permute-done.11.refs_3_
  40.4 0.0 collective-permute-done.10.refs_2_
  40.4 0.0 collective-permute-done.9.refs_1_
  40.5 1.7 %collective-permute-start.12 = (bf16[128,1024]{1,0:T(8,128)(2,1)S(1)}, bf16[128,1024]{1,0:T(8,128)(2,1)S(1)}, u32[]{:S(2)}, u32[]{:S(2)}) collective-permute-start(bf16[128,1024]{1,0:T(8,128)(2,1)S(1)} %join.2.refs_0_), channel_id=1, source_target_pairs={{0,2},{1,3},{2,0},{3,1},{4,6},{5,7},{6,4},{7,5},{8,10},{9,11},{10,... | collective-permute-start | bytes 786440 | tf_op jit(solution)/shard_map/ppermute | solution.py:43
  42.2 0.0 collective-permute-done.15.refs_10_
  42.2 0.8 %broadcast_in_dim.17 = bf16[128,1024]{1,0:T(8,128)(2,1)} broadcast(bf16[]{:T(256)} %constant.4.clone.1), dimensions={} | broadcast | bytes 262146 | tf_op jit(solution)/shard_map/broadcast_in_dim | solution.py:462
  42.9 0.6 while.10
  43.6 3.3 %collective-permute-done.12.refs_1_ = bf16[128,1024]{1,0:T(8,128)(2,1)S(1)} collective-permute-done((bf16[128,1024]{1,0:T(8,128)(2,1)S(1)}, bf16[128,1024]{1,0:T(8,128)(2,1)S(1)}, u32[]{:S(2)}, u32[]{:S(2)}) %collective-permute-start.12) | collective-permute-done | bytes 262176 | tf_op jit(solution)/shard_map/ppermute | solution.py:43
  46.9 0.0 copy-done.10
  46.9 1.6 %copy-done.3 = bf16[1024,1024]{1,0:T(8,128)(2,1)S(1)} copy-done((bf16[1024,1024]{1,0:T(8,128)(2,1)S(1)}, bf16[1024,1024]{1,0:T(8,128)(2,1)}, u32[]{:S(2)}) %copy-start.3) | copy-done | bytes 2097176
  48.5 1.6 %copy-done.5 = bf16[1024,1024]{1,0:T(8,128)(2,1)S(1)} copy-done((bf16[1024,1024]{1,0:T(8,128)(2,1)S(1)}, bf16[1024,1024]{1,0:T(8,128)(2,1)}, u32[]{:S(2)}) %copy-start.5) | copy-done | bytes 2097176
  50.1 1.6 %copy-done.7 = bf16[1024,1024]{1,0:T(8,128)(2,1)S(1)} copy-done((bf16[1024,1024]{1,0:T(8,128)(2,1)S(1)}, bf16[1024,1024]{1,0:T(8,128)(2,1)}, u32[]{:S(2)}) %copy-start.7) | copy-done | bytes 2097176
  51.7 1.6 %copy-done.9 = bf16[1024,1024]{1,0:T(8,128)(2,1)S(1)} copy-done((bf16[1024,1024]{1,0:T(8,128)(2,1)S(1)}, bf16[1024,1024]{1,0:T(8,128)(2,1)}, u32[]{:S(2)}) %copy-start.9) | copy-done | bytes 2097176
  53.3 6.2 %attend.1 = (bf16[16,1024]{1,0:T(8,128)(2,1)S(1)}, f32[64,1024]{1,0:T(8,128)S(1)}, bf16[64,1024]{1,0:T(8,128)(2,1)S(1)}) custom-call(s32[1]{0:T(128)} %get-tuple-element.149.rounds_ref, bf16[128,256]{1,0:T(8,128)(2,1)S(1)} %plan.2.pick_ref, bf16[128,1024]{1,0:T(8,128)(2,1)S(1)} %join.2.refs_0_, bf16[128,1024]{1,0:T(8,128)(2,1)S(1)} %collective-permute-done.12.refs_1_, ...), custom_call_target="tpu_custom_call" | custom-call | flops 2147483648 | bytes 8388608 | tf_op jit(solution)/shard_map/attend/pallas_call | solution.py:319
  59.5 1.7 %collective-permute-start.16 = (bf16[64,1024]{1,0:T(8,128)(2,1)S(1)}, bf16[64,1024]{1,0:T(8,128)(2,1)S(1)}, u32[]{:S(2)}, u32[]{:S(2)}) collective-permute-start(bf16[64,1024]{1,0:T(8,128)(2,1)S(1)} %get-tuple-element.72), channel_id=1, source_target_pairs={{0,2},{1,3},{2,0},{3,1},{4,6},{5,7},{6,4},{7,5},{8,10},{9,11},{10,... | collective-permute-start | bytes 393224 | tf_op jit(solution)/shard_map/ppermute | solution.py:43
  61.2 3.3 %collective-permute-done.16 = bf16[64,1024]{1,0:T(8,128)(2,1)S(1)} collective-permute-done((bf16[64,1024]{1,0:T(8,128)(2,1)S(1)}, bf16[64,1024]{1,0:T(8,128)(2,1)S(1)}, u32[]{:S(2)}, u32[]{:S(2)}) %collective-permute-start.16) | collective-permute-done | bytes 131104 | tf_op jit(solution)/shard_map/ppermute | solution.py:43
  64.6 3.8 %collective-permute-start.19 = (bf16[16,1024]{1,0:T(8,128)(2,1)S(1)}, bf16[16,1024]{1,0:T(8,128)(2,1)S(1)}, u32[]{:S(2)}, u32[]{:S(2)}) collective-permute-start(bf16[16,1024]{1,0:T(8,128)(2,1)S(1)} %get-tuple-element.92), channel_id=1, source_target_pairs={{0,12},{1,13},{2,14},{3,15},{4,8},{5,9},{6,10},{7,11},{8,4},{9,5},... | collective-permute-start | bytes 98312 | tf_op jit(solution)/shard_map/ppermute | solution.py:43
  68.4 0.0 collective-permute-start.18
  68.4 0.6 collective-permute-start.17
  69.0 0.0 copy-done
  69.1 0.5 gates.1.refs_4_
  69.5 0.8 %collective-permute-done.19.refs_2_ = bf16[16,1024]{1,0:T(8,128)(2,1)S(1)} collective-permute-done((bf16[16,1024]{1,0:T(8,128)(2,1)S(1)}, bf16[16,1024]{1,0:T(8,128)(2,1)S(1)}, u32[]{:S(2)}, u32[]{:S(2)}) %collective-permute-start.19) | collective-permute-done | bytes 32800 | tf_op jit(solution)/shard_map/ppermute | solution.py:43
  70.4 2.8 %collective-permute-done.18.refs_1_ = bf16[16,1024]{1,0:T(8,128)(2,1)S(1)} collective-permute-done((bf16[16,1024]{1,0:T(8,128)(2,1)S(1)}, bf16[16,1024]{1,0:T(8,128)(2,1)S(1)}, u32[]{:S(2)}, u32[]{:S(2)}) %collective-permute-start.18) | collective-permute-done | bytes 32800 | tf_op jit(solution)/shard_map/ppermute | solution.py:43
  73.2 0.0 collective-permute-done.17.refs_0_
  73.2 0.0 copy-done.1
  73.2 0.0 copy-done.11
  73.2 1.2 %finish.1 = bf16[16,1024]{1,0:T(8,128)(2,1)} custom-call(f32[16,1024]{1,0:T(8,128)S(1)} %slice.19.own_ref, bf16[16,1024]{1,0:T(8,128)(2,1)S(1)} %collective-permute-done.17.refs_0_, bf16[16,1024]{1,0:T(8,128)(2,1)S(1)} %collective-permute-done.18.refs_1_, bf16[16,1024]{1,0:T(8,128)(2,1)S(1)} %collective-permute-done.19.refs_2_, ...), custom_call_target="tpu_custom_call" | custom-call | tf_op jit(solution)/shard_map/finish/pallas_call | solution.py:402
  (12 shorter events, 0.1 us)
Async XLA Ops:
  0.0 4.1 %copy-start.13 = (s32[16]{0:T(128)S(1)}, s32[16]{0:T(128)}, u32[]{:S(2)}) copy-start(s32[16]{0:T(128)} %param.14) | copy-start | bytes 196
  0.0 22.4 %collective-permute-start.8 = (bf16[1024,1024]{1,0:T(8,128)(2,1)}, bf16[1024,1024]{1,0:T(8,128)(2,1)S(1)}, u32[]{:S(2)}, u32[]{:S(2)}) collective-permute-start(bf16[1024,1024]{1,0:T(8,128)(2,1)} %table_hbm.1), channel_id=1, source_target_pairs={{0,1},{1,0},{2,3},{3,2},{4,5},{5,4},{6,7},{7,6},{8,9},{9,8},{10,11... | collective-permute-start | bytes 6291464 | tf_op jit(solution)/shard_map/ppermute | solution.py:43
  0.5 27.8 %collective-permute-start.13 = (bf16[1024,1024]{1,0:T(8,128)(2,1)}, bf16[1024,1024]{1,0:T(8,128)(2,1)}, u32[]{:S(2)}, u32[]{:S(2)}) collective-permute-start(bf16[1024,1024]{1,0:T(8,128)(2,1)} %refs_1_.1), channel_id=1, source_target_pairs={{0,1},{1,0},{2,3},{3,2},{4,5},{5,4},{6,7},{7,6},{8,9},{9,8},{10,11... | collective-permute-start | bytes 6291464 | tf_op jit(solution)/shard_map/ppermute | solution.py:43
  0.6 34.8 %collective-permute-start.14 = (bf16[1024,1024]{1,0:T(8,128)(2,1)}, bf16[1024,1024]{1,0:T(8,128)(2,1)}, u32[]{:S(2)}, u32[]{:S(2)}) collective-permute-start(bf16[1024,1024]{1,0:T(8,128)(2,1)} %refs_2_.1), channel_id=1, source_target_pairs={{0,1},{1,0},{2,3},{3,2},{4,5},{5,4},{6,7},{7,6},{8,9},{9,8},{10,11... | collective-permute-start | bytes 6291464 | tf_op jit(solution)/shard_map/ppermute | solution.py:43
  4.0 38.2 %collective-permute-start.15 = (bf16[1024,128]{1,0:T(8,128)(2,1)S(1)}, bf16[1024,128]{1,0:T(8,128)(2,1)S(1)}, u32[]{:S(2)}, u32[]{:S(2)}) collective-permute-start(bf16[1024,128]{1,0:T(8,128)(2,1)S(1)} %get-tuple-element.70.refs_9_), channel_id=1, source_target_pairs={{0,1},{1,0},{2,3},{3,2},{4,5},{5,4},{6,7},{7,6},{8,9},{9,8},{10,11... | collective-permute-start | bytes 786440 | tf_op jit(solution)/shard_map/ppermute | solution.py:43
  4.1 6.6 %collective-permute-start.6 = (s32[1,16]{1,0:T(1,128)S(1)}, s32[1,16]{1,0:T(1,128)S(1)}, u32[]{:S(2)}, u32[]{:S(2)}) collective-permute-start(s32[1,16]{1,0:T(1,128)S(1)} %bitcast.17), channel_id=1, source_target_pairs={{0,12},{1,13},{2,14},{3,15},{4,8},{5,9},{6,10},{7,11},{8,4},{9,5},... | collective-permute-start | bytes 200 | tf_op jit(solution)/shard_map/ppermute | solution.py:43
  10.7 4.5 %collective-permute-start.5 = (s32[1,16]{1,0:T(1,128)S(1)}, s32[1,16]{1,0:T(1,128)S(1)}, u32[]{:S(2)}, u32[]{:S(2)}) collective-permute-start(s32[1,16]{1,0:T(1,128)S(1)} %bitcast.18), channel_id=1, source_target_pairs={{0,8},{1,9},{2,10},{3,11},{4,12},{5,13},{6,14},{7,15},{8,0},{9,1},... | collective-permute-start | bytes 200 | tf_op jit(solution)/shard_map/ppermute | solution.py:43
  15.1 3.6 %collective-permute-start.4 = (s32[1,16]{1,0:T(1,128)S(1)}, s32[1,16]{1,0:T(1,128)S(1)}, u32[]{:S(2)}, u32[]{:S(2)}) collective-permute-start(s32[1,16]{1,0:T(1,128)S(1)} %bitcast.19), channel_id=1, source_target_pairs={{0,4},{1,5},{2,6},{3,7},{4,0},{5,1},{6,2},{7,3},{8,12},{9,13},{10,... | collective-permute-start | bytes 200 | tf_op jit(solution)/shard_map/ppermute | solution.py:43
  18.8 3.6 %collective-permute-start.7 = (s32[1,64]{1,0:T(1,128)S(1)}, s32[1,64]{1,0:T(1,128)S(1)}, u32[]{:S(2)}, u32[]{:S(2)}) collective-permute-start(s32[1,64]{1,0:T(1,128)S(1)} %pad_add_fusion.2.refs_0_), channel_id=1, source_target_pairs={{0,2},{1,3},{2,0},{3,1},{4,6},{5,7},{6,4},{7,5},{8,10},{9,11},{10,... | collective-permute-start | bytes 776 | tf_op jit(solution)/shard_map/ppermute | solution.py:43
  22.4 2.0 %copy-start.12 = (bf16[1024,1024]{1,0:T(8,128)(2,1)}, bf16[1024,1024]{1,0:T(8,128)(2,1)S(1)}, u32[]{:S(2)}) copy-start(bf16[1024,1024]{1,0:T(8,128)(2,1)S(1)} %collective-permute-done.8.refs_3_) | copy-start | bytes 6291460
  24.4 16.0 %collective-permute-start.11 = (bf16[32,1024]{1,0:T(8,128)(2,1)S(1)}, bf16[32,1024]{1,0:T(8,128)(2,1)S(1)}, u32[]{:S(2)}, u32[]{:S(2)}) collective-permute-start(bf16[32,1024]{1,0:T(8,128)(2,1)S(1)} %get-tuple-element.63.refs_0_), channel_id=1, source_target_pairs={{0,12},{1,13},{2,14},{3,15},{4,8},{5,9},{6,10},{7,11},{8,4},{9,5},... | collective-permute-start | bytes 196616 | tf_op jit(solution)/shard_map/ppermute | solution.py:43
  28.3 12.1 %collective-permute-start.10 = (bf16[32,1024]{1,0:T(8,128)(2,1)S(1)}, bf16[32,1024]{1,0:T(8,128)(2,1)S(1)}, u32[]{:S(2)}, u32[]{:S(2)}) collective-permute-start(bf16[32,1024]{1,0:T(8,128)(2,1)S(1)} %get-tuple-element.63.refs_0_), channel_id=1, source_target_pairs={{0,8},{1,9},{2,10},{3,11},{4,12},{5,13},{6,14},{7,15},{8,0},{9,1},... | collective-permute-start | bytes 196616 | tf_op jit(solution)/shard_map/ppermute | solution.py:43
  28.3 12.1 %collective-permute-start.9 = (bf16[32,1024]{1,0:T(8,128)(2,1)S(1)}, bf16[32,1024]{1,0:T(8,128)(2,1)S(1)}, u32[]{:S(2)}, u32[]{:S(2)}) collective-permute-start(bf16[32,1024]{1,0:T(8,128)(2,1)S(1)} %get-tuple-element.63.refs_0_), channel_id=1, source_target_pairs={{0,4},{1,5},{2,6},{3,7},{4,0},{5,1},{6,2},{7,3},{8,12},{9,13},{10,... | collective-permute-start | bytes 196616 | tf_op jit(solution)/shard_map/ppermute | solution.py:43
  31.8 1.4 %copy-start.2 = (bf16[1024,1024]{1,0:T(8,128)(2,1)}, bf16[1024,1024]{1,0:T(8,128)(2,1)S(1)}, u32[]{:S(2)}) copy-start(bf16[1024,1024]{1,0:T(8,128)(2,1)S(1)} %get-tuple-element.66.refs_5_) | copy-start | bytes 6291460
  33.2 1.3 %copy-start.4 = (bf16[1024,1024]{1,0:T(8,128)(2,1)}, bf16[1024,1024]{1,0:T(8,128)(2,1)S(1)}, u32[]{:S(2)}) copy-start(bf16[1024,1024]{1,0:T(8,128)(2,1)S(1)} %get-tuple-element.68.refs_7_) | copy-start | bytes 6291460
  37.7 1.4 %copy-start.6 = (bf16[1024,1024]{1,0:T(8,128)(2,1)}, bf16[1024,1024]{1,0:T(8,128)(2,1)S(1)}, u32[]{:S(2)}) copy-start(bf16[1024,1024]{1,0:T(8,128)(2,1)S(1)} %get-tuple-element.67.refs_6_) | copy-start | bytes 6291460
  39.1 1.4 %copy-start.8 = (bf16[1024,1024]{1,0:T(8,128)(2,1)}, bf16[1024,1024]{1,0:T(8,128)(2,1)S(1)}, u32[]{:S(2)}) copy-start(bf16[1024,1024]{1,0:T(8,128)(2,1)S(1)} %get-tuple-element.69.refs_8_) | copy-start | bytes 6291460
  40.5 6.4 %collective-permute-start.12 = (bf16[128,1024]{1,0:T(8,128)(2,1)S(1)}, bf16[128,1024]{1,0:T(8,128)(2,1)S(1)}, u32[]{:S(2)}, u32[]{:S(2)}) collective-permute-start(bf16[128,1024]{1,0:T(8,128)(2,1)S(1)} %join.2.refs_0_), channel_id=1, source_target_pairs={{0,2},{1,3},{2,0},{3,1},{4,6},{5,7},{6,4},{7,5},{8,10},{9,11},{10,... | collective-permute-start | bytes 786440 | tf_op jit(solution)/shard_map/ppermute | solution.py:43
  42.9 4.0 %copy-start.10 = (f32[1024]{0:T(1024)S(1)}, f32[1024]{0:T(1024)}, u32[]{:S(2)}) copy-start(f32[1024]{0:T(1024)} %param.20) | copy-start | bytes 12292
  46.9 1.6 %copy-start.3 = (bf16[1024,1024]{1,0:T(8,128)(2,1)S(1)}, bf16[1024,1024]{1,0:T(8,128)(2,1)}, u32[]{:S(2)}) copy-start(bf16[1024,1024]{1,0:T(8,128)(2,1)} %copy-done.2) | copy-start | bytes 6291460
  48.5 1.6 %copy-start.5 = (bf16[1024,1024]{1,0:T(8,128)(2,1)S(1)}, bf16[1024,1024]{1,0:T(8,128)(2,1)}, u32[]{:S(2)}) copy-start(bf16[1024,1024]{1,0:T(8,128)(2,1)} %copy-done.4) | copy-start | bytes 6291460
  50.1 1.6 %copy-start.7 = (bf16[1024,1024]{1,0:T(8,128)(2,1)S(1)}, bf16[1024,1024]{1,0:T(8,128)(2,1)}, u32[]{:S(2)}) copy-start(bf16[1024,1024]{1,0:T(8,128)(2,1)} %copy-done.6) | copy-start | bytes 6291460
  51.7 1.6 %copy-start.9 = (bf16[1024,1024]{1,0:T(8,128)(2,1)S(1)}, bf16[1024,1024]{1,0:T(8,128)(2,1)}, u32[]{:S(2)}) copy-start(bf16[1024,1024]{1,0:T(8,128)(2,1)} %copy-done.8) | copy-start | bytes 6291460
  53.3 15.8 %copy-start = (bf16[1024,2048]{1,0:T(8,128)(2,1)S(1)}, bf16[1024,2048]{1,0:T(8,128)(2,1)}, u32[]{:S(2)}) copy-start(bf16[1024,2048]{1,0:T(8,128)(2,1)} %proj_ref.1) | copy-start | bytes 12582916
  59.5 5.0 %collective-permute-start.16 = (bf16[64,1024]{1,0:T(8,128)(2,1)S(1)}, bf16[64,1024]{1,0:T(8,128)(2,1)S(1)}, u32[]{:S(2)}, u32[]{:S(2)}) collective-permute-start(bf16[64,1024]{1,0:T(8,128)(2,1)S(1)} %get-tuple-element.72), channel_id=1, source_target_pairs={{0,2},{1,3},{2,0},{3,1},{4,6},{5,7},{6,4},{7,5},{8,10},{9,11},{10,... | collective-permute-start | bytes 393224 | tf_op jit(solution)/shard_map/ppermute | solution.py:43
  64.6 5.8 %collective-permute-start.19 = (bf16[16,1024]{1,0:T(8,128)(2,1)S(1)}, bf16[16,1024]{1,0:T(8,128)(2,1)S(1)}, u32[]{:S(2)}, u32[]{:S(2)}) collective-permute-start(bf16[16,1024]{1,0:T(8,128)(2,1)S(1)} %get-tuple-element.92), channel_id=1, source_target_pairs={{0,12},{1,13},{2,14},{3,15},{4,8},{5,9},{6,10},{7,11},{8,4},{9,5},... | collective-permute-start | bytes 98312 | tf_op jit(solution)/shard_map/ppermute | solution.py:43
  68.4 4.8 %collective-permute-start.18 = (bf16[16,1024]{1,0:T(8,128)(2,1)S(1)}, bf16[16,1024]{1,0:T(8,128)(2,1)S(1)}, u32[]{:S(2)}, u32[]{:S(2)}) collective-permute-start(bf16[16,1024]{1,0:T(8,128)(2,1)S(1)} %get-tuple-element.93), channel_id=1, source_target_pairs={{0,8},{1,9},{2,10},{3,11},{4,12},{5,13},{6,14},{7,15},{8,0},{9,1},... | collective-permute-start | bytes 98312 | tf_op jit(solution)/shard_map/ppermute | solution.py:43
  68.4 4.8 %collective-permute-start.17 = (bf16[16,1024]{1,0:T(8,128)(2,1)S(1)}, bf16[16,1024]{1,0:T(8,128)(2,1)S(1)}, u32[]{:S(2)}, u32[]{:S(2)}) collective-permute-start(bf16[16,1024]{1,0:T(8,128)(2,1)S(1)} %get-tuple-element.94), channel_id=1, source_target_pairs={{0,4},{1,5},{2,6},{3,7},{4,0},{5,1},{6,2},{7,3},{8,12},{9,13},{10,... | collective-permute-start | bytes 98312 | tf_op jit(solution)/shard_map/ppermute | solution.py:43
  69.1 4.2 %copy-start.1 = (bf16[1024,1024]{1,0:T(8,128)(2,1)S(1)}, bf16[1024,1024]{1,0:T(8,128)(2,1)}, u32[]{:S(2)}) copy-start(bf16[1024,1024]{1,0:T(8,128)(2,1)} %refs_6_.1) | copy-start | bytes 6291460
  69.1 4.2 %copy-start.11 = (f32[1024]{0:T(1024)S(1)}, f32[1024]{0:T(1024)}, u32[]{:S(2)}) copy-start(f32[1024]{0:T(1024)} %param.24) | copy-start | bytes 12292

commit v6 on v5

--- a/solution.py
+++ b/solution.py
@@ -69,6 +69,15 @@
     for bits in far:
         x = join([x] + [swap(x, m, axis, size) for m in combos(bits)[1:]], dim)
     return [x, swap(x, near[0], axis, size)]
+
+
+def gather_rows(x, axis, size):
+    *far, near = stage_masks(size)
+    for bits in far[:-1]:
+        x = join([x] + [swap(x, m, axis, size) for m in combos(bits)[1:]], 0)
+    first, *rest = combos(far[-1])[1:]
+    pieces = [x, swap(x, first, axis, size), join([swap(x, m, axis, size) for m in rest], 0)]
+    return pieces + [swap(p, near[0], axis, size) for p in pieces]
 
 
 def position_bits(size):
@@ -258,10 +267,25 @@
 
 
 def attend_kernel(rounds_ref, pick_ref, *refs, heads, blocks):
-    *row_refs, extra_hbm, gain_ref, proj_ref = refs[: -6 - 3 * blocks]
-    caches = refs[-6 - 3 * blocks : -6]
-    own_ref, keep_ref, send_ref, emb_ref, query_ref, sem = refs[-6:]
+    last = 5 * blocks + 7
+    *row_refs, extra_hbm, gain_ref, proj_ref = refs[:-last]
+    refs = refs[-last:]
+    *caches, own_ref, keep_ref, send_ref, emb_ref, query_ref, sem = refs[: -1 - 2 * blocks]
+    chip = refs[-1 - 2 * blocks : -1]
+    sems = refs[-1]
     count, width = emb_ref.shape
+    groups = width // LANES
+    copies = [
+        [
+            pltpu.make_async_copy(a.at[:, pl.ds(g * LANES, LANES)], b.at[:, pl.ds(g * LANES, LANES)], sems.at[g, k])
+            for k, (a, b) in enumerate(zip(caches[: 2 * blocks], chip))
+        ]
+        for g in range(groups)
+    ]
+    for group in copies:
+        for c in group:
+            c.start()
+    key_refs, value_refs, bias_refs = chip[:blocks], chip[blocks:], caches[2 * blocks :]
     rows = jnp.concatenate([r[...] for r in row_refs], axis=0)
     emb_ref[...] = jnp.dot(pick_ref[...], rows, preferred_element_type=F32).astype(BF16)
 
@@ -283,7 +307,10 @@
         query = silu(projected).astype(BF16)
         query_ref[first : first + rows, :] = query * jnp.asarray(0.5 * head_dim**-0.5, BF16)
         lane = lax.broadcasted_iota(jnp.int32, (rows, LANES), 1)
-        for group in range(heads // per):
+        for group in range(groups):
+            if first == 0:
+                for c in copies[group]:
+                    c.wait()
             at = slice(group * LANES, (group + 1) * LANES)
             part = query_ref[first : first + rows, at]
             zero, one = jnp.zeros_like(part), jnp.ones_like(part)
@@ -294,7 +321,7 @@
                 stacked.append(jnp.concatenate([own, chosen], axis=1))
             left = jnp.concatenate(stacked, axis=0)
             total = jnp.zeros((per * rows, LANES), F32)
-            for key_ref, value_ref, bias_ref in zip(*(caches[k * blocks : (k + 1) * blocks] for k in range(3))):
+            for key_ref, value_ref, bias_ref in zip(key_refs, value_refs, bias_refs):
                 step = min(EVENTS_AT_ONCE, key_ref.shape[0])
                 for j in range(0, key_ref.shape[0], step):
                     right = jnp.concatenate([key_ref[j : j + step, at], bias_ref[j : j + step, :]], axis=1)
@@ -316,6 +343,7 @@
 def attend(rounds, pick, pieces, extra, gain, proj, keys, values, biases, heads, each):
     count, width = extra.shape
     blocks = len(keys)
+    caches = [pltpu.with_memory_space_constraint(c, pltpu.HBM) for c in [*keys, *values]]
     return pl.pallas_call(
         functools.partial(attend_kernel, heads=heads, blocks=blocks),
         out_shape=(
@@ -323,21 +351,23 @@
             jax.ShapeDtypeStruct((count // 2, width), F32),
             jax.ShapeDtypeStruct((count // 2, width), BF16),
         ),
-        in_specs=[SMEM, VMEM] + [VMEM] * len(pieces) + [HBM] + [VMEM] * (2 + 3 * blocks),
+        in_specs=[SMEM, VMEM] + [VMEM] * len(pieces) + [HBM, VMEM, VMEM] + [HBM] * 2 * blocks + [VMEM] * blocks,
         out_specs=(VMEM, VMEM, VMEM),
         scratch_shapes=[
             pltpu.VMEM((count, width), BF16),
             pltpu.VMEM((count, width), BF16),
             pltpu.SemaphoreType.DMA,
-        ],
-        compiler_params=params(24),
+        ]
+        + [pltpu.VMEM(c.shape, BF16) for c in caches]
+        + [pltpu.SemaphoreType.DMA((width // LANES, len(caches)))],
+        compiler_params=params(40),
         cost_estimate=pl.CostEstimate(
             flops=8 * count * width * blocks * keys[0].shape[0],
             transcendentals=count * heads * blocks * keys[0].shape[0],
             bytes_accessed=4 * blocks * keys[0].size,
         ),
         name="attend",
-    )(rounds, pick, *pieces, extra, gain, proj, *keys, *values, *biases)
+    )(rounds, pick, *pieces, extra, gain, proj, *caches, *biases)
 
 
 def stage_kernel(*refs, width):
@@ -355,16 +385,16 @@
         c.wait()
 
 
-def stage(width, *arrays):
+def stage(width, *arrays, held=True):
     return pl.pallas_call(
         functools.partial(stage_kernel, width=width),
         out_shape=tuple(jax.ShapeDtypeStruct((a.shape[0], width), BF16) for a in arrays),
-        in_specs=[HBM] * len(arrays),
+        in_specs=[HBM if held else pl.BlockSpec(memory_space=pl.ANY)] * len(arrays),
         out_specs=(VMEM,) * len(arrays),
         scratch_shapes=[pltpu.SemaphoreType.DMA((len(arrays),))],
         compiler_params=params(4),
         name="stage",
-    )(*(pltpu.with_memory_space_constraint(a, pltpu.HBM) for a in arrays))
+    )(*(pltpu.with_memory_space_constraint(a, pltpu.HBM) if held else a for a in arrays))
 
 
 def gates_kernel(emb_ref, gain_ref, proj_ref, out_ref):
@@ -449,23 +479,33 @@
     other_bias = partners(bias)
     ids = gather_relative(item_ids[None, :], 1, axis, size)
 
-    found, rounds = lookup(here, ids, [own_table, other_table], slots, size, True)
-    pieces = gather_relative(found, 0, axis, size)
+    (near_table,) = stage(width, other_table, held=False)
+    found, rounds = lookup(here, ids, [own_table, near_table], slots, size, True)
+    pieces = gather_rows(found, axis, size)
     pick = plan(here, ids, slots, table_rows, size)
 
     def more(state):
         turn, so_far = state
         picked = plan(place(turn), ids, slots, table_rows, size)
         found, _ = lookup(place(turn), ids, [item_table, other_table], slots, size, False)
-        return turn + 1, so_far + select(picked, gather_relative(found, 0, axis, size))
+        return turn + 1, so_far + select(picked, gather_rows(found, axis, size))
 
     none = jnp.zeros((each * (size // 2), width), BF16)
     _, extra = lax.while_loop(lambda s: s[0] < rounds[0], more, (jnp.int32(1), none))
 
-    proj, keys, values = stage(width, proj_in, key_cache, value_cache)
-    other_keys, other_values = stage(width, other_keys, other_values)
+    (proj,) = stage(width, proj_in)
     own, keep, send = attend(
-        rounds, pick, pieces, extra, gain, proj, [keys, other_keys], [values, other_values], [bias, other_bias], heads, each
+        rounds,
+        pick,
+        pieces,
+        extra,
+        gain,
+        proj,
+        [key_cache, other_keys],
+        [value_cache, other_values],
+        [bias, other_bias],
+        heads,
+        each,
     )
     gates = gates_of(own, gain, proj_in)
 

time: 74.7 us -> 58.6 us (0.78)
  local copies, waits for them, and re-layouts: 12.6 us -> 0.8 us
  starting transfers between devices: 22.8 us -> 17.4 us
  waiting for transfers between devices: 19.2 us -> 20.7 us
  Pallas kernels: 18.1 us -> 17.2 us
    unnamed x28 -> x10, local copies, waits for them, and re-layouts: 11.8 us -> 0.76 us
    ppermute x16 -> x18, starting transfers between devices: 22.8 us -> 17.4 us  [swap(): return lax.ppermute(x, axis, [(i, i ^ mask) for i in range(size)])]
    pallas_call x2, Pallas kernels: 5.12 us -> 1.75 us  [stage(): pl.pallas_call(functools.partial(stage_kernel, width=width), out_shape=tu...]
    pallas_call x1, Pallas kernels: 6.23 us -> 8.74 us  [attend(): pl.pallas_call(functools.partial(attend_kernel, heads=heads, blocks=block...]
    ppermute x16 -> x18, waiting for transfers between devices: 19.2 us -> 20.7 us  [swap(): return lax.ppermute(x, axis, [(i, i ^ mask) for i in range(size)])]
  transfers between devices with their start and end apart: 16 -> 18, of which waited for: 8 -> 7; matrix products, arithmetic and copies ran while one was open for 1% -> 1% of each run, Pallas kernels for 14% -> 13%
where the time goes in v6:
time: 58.6 us; the launch traced here: 58.4 us
  waiting for transfers between devices  20.7 us (35%)
  starting transfers between devices  17.4 us (30%)
  Pallas kernels  17.2 us (29%)
  between operations  0.87 us (1%)
  other arithmetic  0.84 us (1%)
  local copies, waits for them, and re-layouts  0.8 us (1%)
  loops' own time  0.64 us (1%)
    ppermute x18, waiting for transfers between devices, swap(): return lax.ppermute(x, axis, [(i, i ^ mask) for i in range(size)])  20.7 us
    ppermute x18, starting transfers between devices, swap(): return lax.ppermute(x, axis, [(i, i ^ mask) for i in range(size)])  17.4 us
    pallas_call x1, Pallas kernels, attend(): pl.pallas_call(functools.partial(attend_kernel, heads=heads, blocks=block...  8.74 us
    pallas_call x1, Pallas kernels, prepare(): pl.pallas_call(functools.partial(prepare_kernel, npos=pos_bias.shape[1],...  2.21 us
    pallas_call x1, Pallas kernels, lookup(): pl.pallas_call(functools.partial(lookup_kernel, size=size, resident=resid...  2.02 us
    pallas_call x2, Pallas kernels, stage(): pl.pallas_call(functools.partial(stage_kernel, width=width), out_shape=tu...  1.75 us
  transfers between devices with their start and end apart: 18, of which 7 were waited for; matrix products, arithmetic and copies ran while one was open for 1% of the time, Pallas kernels for 13%

profile of v6, /device:TPU:0, one launch (start us, length us, event | category | flops | bytes accessed | tf_op | source)
XLA Modules:
  0.0 58.4 jit_solution(14241337309777954449)
XLA Ops:
  0.0 0.5 collective-permute-start.10
  0.5 2.6 %collective-permute-start.6 = (s32[1,16]{1,0:T(1,128)}, s32[1,16]{1,0:T(1,128)S(1)}, u32[]{:S(2)}, u32[]{:S(2)}) collective-permute-start(s32[1,16]{1,0:T(1,128)} %bitcast.17), channel_id=1, source_target_pairs={{0,4},{1,5},{2,6},{3,7},{4,0},{5,1},{6,2},{7,3},{8,12},{9,13},{10,... | collective-permute-start | bytes 200 | tf_op jit(solution)/shard_map/ppermute | solution.py:43
  3.1 2.6 %collective-permute-start.7 = (s32[1,16]{1,0:T(1,128)}, s32[1,16]{1,0:T(1,128)S(1)}, u32[]{:S(2)}, u32[]{:S(2)}) collective-permute-start(s32[1,16]{1,0:T(1,128)} %bitcast.18), channel_id=1, source_target_pairs={{0,8},{1,9},{2,10},{3,11},{4,12},{5,13},{6,14},{7,15},{8,0},{9,1},... | collective-permute-start | bytes 200 | tf_op jit(solution)/shard_map/ppermute | solution.py:43
  5.6 0.0 collective-permute-start.8
  6.3 0.1 pad_add_fusion.1.place_ref
  6.4 0.0 collective-permute-start.17
  6.4 0.0 collective-permute-done.6
  6.4 1.2 %collective-permute-done.7 = s32[1,16]{1,0:T(1,128)S(1)} collective-permute-done((s32[1,16]{1,0:T(1,128)}, s32[1,16]{1,0:T(1,128)S(1)}, u32[]{:S(2)}, u32[]{:S(2)}) %collective-permute-start.7) | collective-permute-done | bytes 96 | tf_op jit(solution)/shard_map/ppermute | solution.py:43
  7.7 3.5 %collective-permute-done.8 = s32[1,16]{1,0:T(1,128)S(1)} collective-permute-done((s32[1,16]{1,0:T(1,128)}, s32[1,16]{1,0:T(1,128)S(1)}, u32[]{:S(2)}, u32[]{:S(2)}) %collective-permute-start.8) | collective-permute-done | bytes 96 | tf_op jit(solution)/shard_map/ppermute | solution.py:43
  11.1 0.7 %pad_add_fusion.2.refs_0_ = s32[1,64]{1,0:T(1,128)S(1)} fusion(s32[1,16]{1,0:T(1,128)S(1)} %collective-permute-done.8, s32[1,16]{1,0:T(1,128)S(1)} %collective-permute-done.7, s32[1,16]{1,0:T(1,128)S(1)} %collective-permute-done.6, s32[1,16]{1,0:T(1,128)} %bitcast.20), kind=kLoop, calls=%fused_computation.9 | loop fusion | flops 192 | bytes 512 | tf_op jit(solution)/shard_map/concatenate | solution.py:55
  11.9 1.5 %collective-permute-start.9 = (s32[1,64]{1,0:T(1,128)S(1)}, s32[1,64]{1,0:T(1,128)S(1)}, u32[]{:S(2)}, u32[]{:S(2)}) collective-permute-start(s32[1,64]{1,0:T(1,128)S(1)} %pad_add_fusion.2.refs_0_), channel_id=1, source_target_pairs={{0,2},{1,3},{2,0},{3,1},{4,6},{5,7},{6,4},{7,5},{8,10},{9,11},{10,... | collective-permute-start | bytes 776 | tf_op jit(solution)/shard_map/ppermute | solution.py:43
  13.4 2.2 %prepare.1 = (bf16[1024,128]{1,0:T(8,128)(2,1)S(1)}, bf16[1024,1024]{1,0:T(8,128)(2,1)S(1)}) custom-call(s32[2]{0:T(128)S(1)} %pad_add_fusion.1.place_ref, s32[1]{0:T(128)S(6)} %copy.24.start_ref, s32[1,1024]{1,0:T(1,128)} %bitcast.16, f32[16,128]{1,0:T(8,128)} %time_bias_hbm.1, f32[16,18]{1,0:T(8,128)} %pos_bias_hbm.1, bf16[1024,1024]{1,0:T(8,128)(2,1)} %table_hbm.1), custom_call_target="tpu_custom_call" | custom-call | tf_op jit(solution)/shard_map/prepare/pallas_call | solution.py:245
  15.6 0.0 collective-permute-done.10.refs_0_
  15.6 0.2 stage.2.refs_3_
  15.8 0.0 collective-permute-done.9.refs_1_
  15.8 2.0 %lookup.2 = (bf16[32,1024]{1,0:T(8,128)(2,1)S(1)}, s32[1]{0:T(128)}) custom-call(s32[2]{0:T(128)S(1)} %pad_add_fusion.1.place_ref, s32[1,64]{1,0:T(1,128)S(1)} %pad_add_fusion.2.refs_0_, s32[1,64]{1,0:T(1,128)S(1)} %collective-permute-done.9.refs_1_, bf16[1024,1024]{1,0:T(8,128)(2,1)S(1)} %get-tuple-element.56.refs_2_, bf16[1024,1024]{1,0:T(8,128)(2,1)S(1)} %stage.2.refs_3_), custom_call_target="tpu_custom_call" | custom-call | tf_op jit(solution)/shard_map/lookup/pallas_call | solution.py:145
  17.9 0.6 %while.10 = (s32[]{:T(128)}, bf16[128,1024]{1,0:T(8,128)(2,1)S(1)}, s32[1]{0:T(128)}, s32[]{:T(128)}, s32[1,64]{1,0:T(1,128)S(1)}, /*index=5*/s32[1,64]{1,0:T(1,...) while((s32[]{:T(128)}, bf16[128,1024]{1,0:T(8,128)(2,1)S(1)}, s32[1]{0:T(128)}, ...), condition=%wide.region_1.0_spmd, body=%wide.region_0.0_spmd.sunk | while | flops 131076 | bytes 20447636 | solution.py:494
  18.5 0.1 collective-permute-start.18
  18.6 0.5 collective-permute-start.19
  19.1 0.0 collective-permute-start.12
  19.1 1.0 %collective-permute-start.13 = (bf16[32,1024]{1,0:T(8,128)(2,1)S(1)}, bf16[32,1024]{1,0:T(8,128)(2,1)S(1)}, u32[]{:S(2)}, u32[]{:S(2)}) collective-permute-start(bf16[32,1024]{1,0:T(8,128)(2,1)S(1)} %get-tuple-element.58.refs_0_), channel_id=1, source_target_pairs={{0,12},{1,13},{2,14},{3,15},{4,8},{5,9},{6,10},{7,11},{8,4},{9,5},... | collective-permute-start | bytes 196616 | tf_op jit(solution)/shard_map/ppermute | solution.py:43
  20.1 6.2 %collective-permute-done.12.refs_0_ = bf16[32,1024]{1,0:T(8,128)(2,1)S(1)} collective-permute-done((bf16[32,1024]{1,0:T(8,128)(2,1)S(1)}, bf16[32,1024]{1,0:T(8,128)(2,1)S(1)}, u32[]{:S(2)}, u32[]{:S(2)}) %collective-permute-start.12) | collective-permute-done | bytes 65568 | tf_op jit(solution)/shard_map/ppermute | solution.py:43
  26.3 0.0 collective-permute-start.11
  26.3 0.0 collective-permute-done.13.refs_1_
  26.3 0.0 copy-start.2
  26.3 1.2 %collective-permute-start.16 = (bf16[64,1024]{1,0:T(8,128)(2,1)S(1)}, bf16[64,1024]{1,0:T(8,128)(2,1)S(1)}, u32[]{:S(2)}, u32[]{:S(2)}) collective-permute-start(bf16[64,1024]{1,0:T(8,128)(2,1)S(1)} %join.2.refs_2_), channel_id=1, source_target_pairs={{0,2},{1,3},{2,0},{3,1},{4,6},{5,7},{6,4},{7,5},{8,10},{9,11},{10,... | collective-permute-start | bytes 393224 | tf_op jit(solution)/shard_map/ppermute | solution.py:43
  27.5 0.0 collective-permute-done.19.refs_14_
  27.5 0.9 %collective-permute-start.14 = (bf16[32,1024]{1,0:T(8,128)(2,1)S(1)}, bf16[32,1024]{1,0:T(8,128)(2,1)S(1)}, u32[]{:S(2)}, u32[]{:S(2)}) collective-permute-start(bf16[32,1024]{1,0:T(8,128)(2,1)S(1)} %get-tuple-element.58.refs_0_), channel_id=1, source_target_pairs={{0,2},{1,3},{2,0},{3,1},{4,6},{5,7},{6,4},{7,5},{8,10},{9,11},{10,... | collective-permute-start | bytes 196616 | tf_op jit(solution)/shard_map/ppermute | solution.py:43
  28.4 2.1 %collective-permute-done.11.refs_1_ = bf16[32,1024]{1,0:T(8,128)(2,1)S(1)} collective-permute-done((bf16[32,1024]{1,0:T(8,128)(2,1)S(1)}, bf16[32,1024]{1,0:T(8,128)(2,1)S(1)}, u32[]{:S(2)}, u32[]{:S(2)}) %collective-permute-start.11) | collective-permute-done | bytes 65568 | tf_op jit(solution)/shard_map/ppermute | solution.py:43
  30.5 1.2 %collective-permute-start.15 = (bf16[32,1024]{1,0:T(8,128)(2,1)S(1)}, bf16[32,1024]{1,0:T(8,128)(2,1)S(1)}, u32[]{:S(2)}, u32[]{:S(2)}) collective-permute-start(bf16[32,1024]{1,0:T(8,128)(2,1)S(1)} %collective-permute-done.11.refs_1_), channel_id=1, source_target_pairs={{0,2},{1,3},{2,0},{3,1},{4,6},{5,7},{6,4},{7,5},{8,10},{9,11},{10,... | collective-permute-start | bytes 196616 | tf_op jit(solution)/shard_map/ppermute | solution.py:43
  31.7 1.6 %stage.3.refs_8_ = bf16[1024,1024]{1,0:T(8,128)(2,1)S(1)} custom-call(bf16[1024,2048]{1,0:T(8,128)(2,1)} %proj_ref.1), custom_call_target="tpu_custom_call" | custom-call | tf_op jit(solution)/shard_map/stage/pallas_call | solution.py:389
  33.3 0.9 %plan.2.pick_ref = bf16[128,256]{1,0:T(8,128)(2,1)S(1)} custom-call(s32[2]{0:T(128)S(1)} %pad_add_fusion.1.place_ref, s32[1,64]{1,0:T(1,128)S(1)} %get-tuple-element.201, s32[1,64]{1,0:T(1,128)S(1)} %get-tuple-element.203), custom_call_target="tpu_custom_call" | custom-call | tf_op jit(solution)/shard_map/plan/pallas_call | solution.py:182
  34.2 0.0 collective-permute-done.17.refs_10_
  34.2 0.0 collective-permute-done.18.refs_12_
  34.2 0.0 copy-start.6
  34.2 0.0 collective-permute-done.14.refs_3_
  34.2 0.6 collective-permute-done.15.refs_4_
  34.8 0.0 collective-permute-done.16.refs_5_
  34.8 0.7 %copy-done.6 = bf16[1024,1024]{1,0:T(8,128)(2,1)} copy-done((bf16[1024,1024]{1,0:T(8,128)(2,1)}, bf16[1024,1024]{1,0:T(8,128)(2,1)S(1)}, u32[]{:S(2)}) %copy-start.6) | copy-done | bytes 2097176
  35.5 0.0 copy-done.2
  35.5 0.0 copy-start
  35.6 8.7 %attend.1 = (bf16[16,1024]{1,0:T(8,128)(2,1)S(1)}, f32[64,1024]{1,0:T(8,128)S(1)}, bf16[64,1024]{1,0:T(8,128)(2,1)S(1)}) custom-call(s32[1]{0:T(128)} %get-tuple-element.139.rounds_ref, bf16[128,256]{1,0:T(8,128)(2,1)S(1)} %plan.2.pick_ref, bf16[32,1024]{1,0:T(8,128)(2,1)S(1)} %get-tuple-element.58.refs_0_, ...), custom_call_target="tpu_custom_call" | custom-call | flops 2147483648 | bytes 8388608 | tf_op jit(solution)/shard_map/attend/pallas_call | solution.py:347
  44.3 0.9 %collective-permute-start.20 = (bf16[64,1024]{1,0:T(8,128)(2,1)S(1)}, bf16[64,1024]{1,0:T(8,128)(2,1)S(1)}, u32[]{:S(2)}, u32[]{:S(2)}) collective-permute-start(bf16[64,1024]{1,0:T(8,128)(2,1)S(1)} %get-tuple-element.62), channel_id=1, source_target_pairs={{0,2},{1,3},{2,0},{3,1},{4,6},{5,7},{6,4},{7,5},{8,10},{9,11},{10,... | collective-permute-start | bytes 393224 | tf_op jit(solution)/shard_map/ppermute | solution.py:43
  45.2 4.1 %collective-permute-done.20 = bf16[64,1024]{1,0:T(8,128)(2,1)S(1)} collective-permute-done((bf16[64,1024]{1,0:T(8,128)(2,1)S(1)}, bf16[64,1024]{1,0:T(8,128)(2,1)S(1)}, u32[]{:S(2)}, u32[]{:S(2)}) %collective-permute-start.20) | collective-permute-done | bytes 131104 | tf_op jit(solution)/shard_map/ppermute | solution.py:43
  49.4 0.1 collective-permute-start.21
  49.5 2.1 %collective-permute-start.22 = (bf16[16,1024]{1,0:T(8,128)(2,1)S(1)}, bf16[16,1024]{1,0:T(8,128)(2,1)S(1)}, u32[]{:S(2)}, u32[]{:S(2)}) collective-permute-start(bf16[16,1024]{1,0:T(8,128)(2,1)S(1)} %get-tuple-element.83), channel_id=1, source_target_pairs={{0,8},{1,9},{2,10},{3,11},{4,12},{5,13},{6,14},{7,15},{8,0},{9,1},... | collective-permute-start | bytes 98312 | tf_op jit(solution)/shard_map/ppermute | solution.py:43
  51.6 2.3 %collective-permute-start.23 = (bf16[16,1024]{1,0:T(8,128)(2,1)S(1)}, bf16[16,1024]{1,0:T(8,128)(2,1)S(1)}, u32[]{:S(2)}, u32[]{:S(2)}) collective-permute-start(bf16[16,1024]{1,0:T(8,128)(2,1)S(1)} %get-tuple-element.82), channel_id=1, source_target_pairs={{0,12},{1,13},{2,14},{3,15},{4,8},{5,9},{6,10},{7,11},{8,4},{9,5},... | collective-permute-start | bytes 98312 | tf_op jit(solution)/shard_map/ppermute | solution.py:43
  53.8 0.0 copy-done
  53.8 0.0 copy-start.1
  53.8 0.0 copy-start.3
  53.8 0.5 gates.1.refs_4_
  54.3 0.0 collective-permute-done.21.refs_0_
  54.3 0.0 collective-permute-done.22.refs_1_
  54.4 2.9 %collective-permute-done.23.refs_2_ = bf16[16,1024]{1,0:T(8,128)(2,1)S(1)} collective-permute-done((bf16[16,1024]{1,0:T(8,128)(2,1)S(1)}, bf16[16,1024]{1,0:T(8,128)(2,1)S(1)}, u32[]{:S(2)}, u32[]{:S(2)}) %collective-permute-start.23) | collective-permute-done | bytes 32800 | tf_op jit(solution)/shard_map/ppermute | solution.py:43
  57.3 0.0 copy-done.1
  57.3 0.0 copy-done.3
  57.3 1.2 %finish.1 = bf16[16,1024]{1,0:T(8,128)(2,1)} custom-call(f32[16,1024]{1,0:T(8,128)S(1)} %slice.19.own_ref, bf16[16,1024]{1,0:T(8,128)(2,1)S(1)} %collective-permute-done.21.refs_0_, bf16[16,1024]{1,0:T(8,128)(2,1)S(1)} %collective-permute-done.22.refs_1_, bf16[16,1024]{1,0:T(8,128)(2,1)S(1)} %collective-permute-done.23.refs_2_, ...), custom_call_target="tpu_custom_call" | custom-call | tf_op jit(solution)/shard_map/finish/pallas_call | solution.py:432
  (5 shorter events, 0.1 us)
Async XLA Ops:
  0.0 15.6 %collective-permute-start.10 = (bf16[1024,1024]{1,0:T(8,128)(2,1)}, bf16[1024,1024]{1,0:T(8,128)(2,1)S(1)}, u32[]{:S(2)}, u32[]{:S(2)}) collective-permute-start(bf16[1024,1024]{1,0:T(8,128)(2,1)} %table_hbm.1), channel_id=1, source_target_pairs={{0,1},{1,0},{2,3},{3,2},{4,5},{5,4},{6,7},{7,6},{8,9},{9,8},{10,11... | collective-permute-start | bytes 6291464 | tf_op jit(solution)/shard_map/ppermute | solution.py:43
  0.5 5.9 %collective-permute-start.6 = (s32[1,16]{1,0:T(1,128)}, s32[1,16]{1,0:T(1,128)S(1)}, u32[]{:S(2)}, u32[]{:S(2)}) collective-permute-start(s32[1,16]{1,0:T(1,128)} %bitcast.17), channel_id=1, source_target_pairs={{0,4},{1,5},{2,6},{3,7},{4,0},{5,1},{6,2},{7,3},{8,12},{9,13},{10,... | collective-permute-start | bytes 200 | tf_op jit(solution)/shard_map/ppermute | solution.py:43
  3.1 4.6 %collective-permute-start.7 = (s32[1,16]{1,0:T(1,128)}, s32[1,16]{1,0:T(1,128)S(1)}, u32[]{:S(2)}, u32[]{:S(2)}) collective-permute-start(s32[1,16]{1,0:T(1,128)} %bitcast.18), channel_id=1, source_target_pairs={{0,8},{1,9},{2,10},{3,11},{4,12},{5,13},{6,14},{7,15},{8,0},{9,1},... | collective-permute-start | bytes 200 | tf_op jit(solution)/shard_map/ppermute | solution.py:43
  5.6 5.5 %collective-permute-start.8 = (s32[1,16]{1,0:T(1,128)}, s32[1,16]{1,0:T(1,128)S(1)}, u32[]{:S(2)}, u32[]{:S(2)}) collective-permute-start(s32[1,16]{1,0:T(1,128)} %bitcast.19), channel_id=1, source_target_pairs={{0,12},{1,13},{2,14},{3,15},{4,8},{5,9},{6,10},{7,11},{8,4},{9,5},... | collective-permute-start | bytes 200 | tf_op jit(solution)/shard_map/ppermute | solution.py:43
  6.4 27.8 %collective-permute-start.17 = (bf16[1024,1024]{1,0:T(8,128)(2,1)}, bf16[1024,1024]{1,0:T(8,128)(2,1)}, u32[]{:S(2)}, u32[]{:S(2)}) collective-permute-start(bf16[1024,1024]{1,0:T(8,128)(2,1)} %refs_9_.1), channel_id=1, source_target_pairs={{0,1},{1,0},{2,3},{3,2},{4,5},{5,4},{6,7},{7,6},{8,9},{9,8},{10,11... | collective-permute-start | bytes 6291464 | tf_op jit(solution)/shard_map/ppermute | solution.py:43
  11.9 3.9 %collective-permute-start.9 = (s32[1,64]{1,0:T(1,128)S(1)}, s32[1,64]{1,0:T(1,128)S(1)}, u32[]{:S(2)}, u32[]{:S(2)}) collective-permute-start(s32[1,64]{1,0:T(1,128)S(1)} %pad_add_fusion.2.refs_0_), channel_id=1, source_target_pairs={{0,2},{1,3},{2,0},{3,1},{4,6},{5,7},{6,4},{7,5},{8,10},{9,11},{10,... | collective-permute-start | bytes 776 | tf_op jit(solution)/shard_map/ppermute | solution.py:43
  18.5 15.7 %collective-permute-start.18 = (bf16[1024,1024]{1,0:T(8,128)(2,1)}, bf16[1024,1024]{1,0:T(8,128)(2,1)S(1)}, u32[]{:S(2)}, u32[]{:S(2)}) collective-permute-start(bf16[1024,1024]{1,0:T(8,128)(2,1)} %refs_11_.1), channel_id=1, source_target_pairs={{0,1},{1,0},{2,3},{3,2},{4,5},{5,4},{6,7},{7,6},{8,9},{9,8},{10,11... | collective-permute-start | bytes 6291464 | tf_op jit(solution)/shard_map/ppermute | solution.py:43
  18.6 8.9 %collective-permute-start.19 = (bf16[1024,128]{1,0:T(8,128)(2,1)S(1)}, bf16[1024,128]{1,0:T(8,128)(2,1)S(1)}, u32[]{:S(2)}, u32[]{:S(2)}) collective-permute-start(bf16[1024,128]{1,0:T(8,128)(2,1)S(1)} %get-tuple-element.60.refs_13_), channel_id=1, source_target_pairs={{0,1},{1,0},{2,3},{3,2},{4,5},{5,4},{6,7},{7,6},{8,9},{9,8},{10,11... | collective-permute-start | bytes 786440 | tf_op jit(solution)/shard_map/ppermute | solution.py:43
  19.1 7.2 %collective-permute-start.12 = (bf16[32,1024]{1,0:T(8,128)(2,1)S(1)}, bf16[32,1024]{1,0:T(8,128)(2,1)S(1)}, u32[]{:S(2)}, u32[]{:S(2)}) collective-permute-start(bf16[32,1024]{1,0:T(8,128)(2,1)S(1)} %get-tuple-element.58.refs_0_), channel_id=1, source_target_pairs={{0,8},{1,9},{2,10},{3,11},{4,12},{5,13},{6,14},{7,15},{8,0},{9,1},... | collective-permute-start | bytes 196616 | tf_op jit(solution)/shard_map/ppermute | solution.py:43
  19.1 7.2 %collective-permute-start.13 = (bf16[32,1024]{1,0:T(8,128)(2,1)S(1)}, bf16[32,1024]{1,0:T(8,128)(2,1)S(1)}, u32[]{:S(2)}, u32[]{:S(2)}) collective-permute-start(bf16[32,1024]{1,0:T(8,128)(2,1)S(1)} %get-tuple-element.58.refs_0_), channel_id=1, source_target_pairs={{0,12},{1,13},{2,14},{3,15},{4,8},{5,9},{6,10},{7,11},{8,4},{9,5},... | collective-permute-start | bytes 196616 | tf_op jit(solution)/shard_map/ppermute | solution.py:43
  26.3 4.3 %collective-permute-start.11 = (bf16[32,1024]{1,0:T(8,128)(2,1)S(1)}, bf16[32,1024]{1,0:T(8,128)(2,1)S(1)}, u32[]{:S(2)}, u32[]{:S(2)}) collective-permute-start(bf16[32,1024]{1,0:T(8,128)(2,1)S(1)} %get-tuple-element.58.refs_0_), channel_id=1, source_target_pairs={{0,4},{1,5},{2,6},{3,7},{4,0},{5,1},{6,2},{7,3},{8,12},{9,13},{10,... | collective-permute-start | bytes 196616 | tf_op jit(solution)/shard_map/ppermute | solution.py:43
  26.3 9.3 %copy-start.2 = (f32[1024]{0:T(1024)S(1)}, f32[1024]{0:T(1024)}, u32[]{:S(2)}) copy-start(f32[1024]{0:T(1024)} %param.20) | copy-start | bytes 12292
  26.3 8.5 %collective-permute-start.16 = (bf16[64,1024]{1,0:T(8,128)(2,1)S(1)}, bf16[64,1024]{1,0:T(8,128)(2,1)S(1)}, u32[]{:S(2)}, u32[]{:S(2)}) collective-permute-start(bf16[64,1024]{1,0:T(8,128)(2,1)S(1)} %join.2.refs_2_), channel_id=1, source_target_pairs={{0,2},{1,3},{2,0},{3,1},{4,6},{5,7},{6,4},{7,5},{8,10},{9,11},{10,... | collective-permute-start | bytes 393224 | tf_op jit(solution)/shard_map/ppermute | solution.py:43
  27.5 6.7 %collective-permute-start.14 = (bf16[32,1024]{1,0:T(8,128)(2,1)S(1)}, bf16[32,1024]{1,0:T(8,128)(2,1)S(1)}, u32[]{:S(2)}, u32[]{:S(2)}) collective-permute-start(bf16[32,1024]{1,0:T(8,128)(2,1)S(1)} %get-tuple-element.58.refs_0_), channel_id=1, source_target_pairs={{0,2},{1,3},{2,0},{3,1},{4,6},{5,7},{6,4},{7,5},{8,10},{9,11},{10,... | collective-permute-start | bytes 196616 | tf_op jit(solution)/shard_map/ppermute | solution.py:43
  30.5 4.3 %collective-permute-start.15 = (bf16[32,1024]{1,0:T(8,128)(2,1)S(1)}, bf16[32,1024]{1,0:T(8,128)(2,1)S(1)}, u32[]{:S(2)}, u32[]{:S(2)}) collective-permute-start(bf16[32,1024]{1,0:T(8,128)(2,1)S(1)} %collective-permute-done.11.refs_1_), channel_id=1, source_target_pairs={{0,2},{1,3},{2,0},{3,1},{4,6},{5,7},{6,4},{7,5},{8,10},{9,11},{10,... | collective-permute-start | bytes 196616 | tf_op jit(solution)/shard_map/ppermute | solution.py:43
  34.2 1.3 %copy-start.6 = (bf16[1024,1024]{1,0:T(8,128)(2,1)}, bf16[1024,1024]{1,0:T(8,128)(2,1)S(1)}, u32[]{:S(2)}) copy-start(bf16[1024,1024]{1,0:T(8,128)(2,1)S(1)} %collective-permute-done.18.refs_12_) | copy-start | bytes 6291460
  35.5 18.3 %copy-start = (bf16[1024,2048]{1,0:T(8,128)(2,1)S(1)}, bf16[1024,2048]{1,0:T(8,128)(2,1)}, u32[]{:S(2)}) copy-start(bf16[1024,2048]{1,0:T(8,128)(2,1)} %proj_ref.1) | copy-start | bytes 12582916
  44.3 5.0 %collective-permute-start.20 = (bf16[64,1024]{1,0:T(8,128)(2,1)S(1)}, bf16[64,1024]{1,0:T(8,128)(2,1)S(1)}, u32[]{:S(2)}, u32[]{:S(2)}) collective-permute-start(bf16[64,1024]{1,0:T(8,128)(2,1)S(1)} %get-tuple-element.62), channel_id=1, source_target_pairs={{0,2},{1,3},{2,0},{3,1},{4,6},{5,7},{6,4},{7,5},{8,10},{9,11},{10,... | collective-permute-start | bytes 393224 | tf_op jit(solution)/shard_map/ppermute | solution.py:43
  49.4 5.0 %collective-permute-start.21 = (bf16[16,1024]{1,0:T(8,128)(2,1)S(1)}, bf16[16,1024]{1,0:T(8,128)(2,1)S(1)}, u32[]{:S(2)}, u32[]{:S(2)}) collective-permute-start(bf16[16,1024]{1,0:T(8,128)(2,1)S(1)} %get-tuple-element.84), channel_id=1, source_target_pairs={{0,4},{1,5},{2,6},{3,7},{4,0},{5,1},{6,2},{7,3},{8,12},{9,13},{10,... | collective-permute-start | bytes 98312 | tf_op jit(solution)/shard_map/ppermute | solution.py:43
  49.5 4.9 %collective-permute-start.22 = (bf16[16,1024]{1,0:T(8,128)(2,1)S(1)}, bf16[16,1024]{1,0:T(8,128)(2,1)S(1)}, u32[]{:S(2)}, u32[]{:S(2)}) collective-permute-start(bf16[16,1024]{1,0:T(8,128)(2,1)S(1)} %get-tuple-element.83), channel_id=1, source_target_pairs={{0,8},{1,9},{2,10},{3,11},{4,12},{5,13},{6,14},{7,15},{8,0},{9,1},... | collective-permute-start | bytes 98312 | tf_op jit(solution)/shard_map/ppermute | solution.py:43
  51.6 5.7 %collective-permute-start.23 = (bf16[16,1024]{1,0:T(8,128)(2,1)S(1)}, bf16[16,1024]{1,0:T(8,128)(2,1)S(1)}, u32[]{:S(2)}, u32[]{:S(2)}) collective-permute-start(bf16[16,1024]{1,0:T(8,128)(2,1)S(1)} %get-tuple-element.82), channel_id=1, source_target_pairs={{0,12},{1,13},{2,14},{3,15},{4,8},{5,9},{6,10},{7,11},{8,4},{9,5},... | collective-permute-start | bytes 98312 | tf_op jit(solution)/shard_map/ppermute | solution.py:43
  53.8 3.4 %copy-start.1 = (bf16[1024,1024]{1,0:T(8,128)(2,1)S(1)}, bf16[1024,1024]{1,0:T(8,128)(2,1)}, u32[]{:S(2)}) copy-start(bf16[1024,1024]{1,0:T(8,128)(2,1)} %refs_6_.1) | copy-start | bytes 6291460
  53.8 3.4 %copy-start.3 = (f32[1024]{0:T(1024)S(1)}, f32[1024]{0:T(1024)}, u32[]{:S(2)}) copy-start(f32[1024]{0:T(1024)} %param.24) | copy-start | bytes 12292

commit v7 on v5

--- a/solution.py
+++ b/solution.py
@@ -69,6 +69,14 @@
     for bits in far:
         x = join([x] + [swap(x, m, axis, size) for m in combos(bits)[1:]], dim)
     return [x, swap(x, near[0], axis, size)]
+
+
+def gather_rows(x, axis, size):
+    *far, near = stage_masks(size)
+    for bits in far[:-1]:
+        x = join([x] + [swap(x, m, axis, size) for m in combos(bits)[1:]], 0)
+    pieces = [x, join([swap(x, m, axis, size) for m in combos(far[-1])[1:]], 0)]
+    return pieces + [swap(p, near[0], axis, size) for p in pieces]
 
 
 def position_bits(size):
@@ -191,7 +199,7 @@
         out_shape=jax.ShapeDtypeStruct((pick.shape[0], rows.shape[1]), BF16),
         in_specs=[VMEM, VMEM],
         out_specs=VMEM,
-        compiler_params=params(32),
+        compiler_params=params(12),
         name="select",
     )(pick, rows)
 
@@ -283,7 +291,7 @@
         query = silu(projected).astype(BF16)
         query_ref[first : first + rows, :] = query * jnp.asarray(0.5 * head_dim**-0.5, BF16)
         lane = lax.broadcasted_iota(jnp.int32, (rows, LANES), 1)
-        for group in range(heads // per):
+        for group in range(width // LANES):
             at = slice(group * LANES, (group + 1) * LANES)
             part = query_ref[first : first + rows, at]
             zero, one = jnp.zeros_like(part), jnp.ones_like(part)
@@ -330,7 +338,7 @@
             pltpu.VMEM((count, width), BF16),
             pltpu.SemaphoreType.DMA,
         ],
-        compiler_params=params(24),
+        compiler_params=params(20),
         cost_estimate=pl.CostEstimate(
             flops=8 * count * width * blocks * keys[0].shape[0],
             transcendentals=count * heads * blocks * keys[0].shape[0],
@@ -355,16 +363,16 @@
         c.wait()
 
 
-def stage(width, *arrays):
+def stage(width, *arrays, held=True):
     return pl.pallas_call(
         functools.partial(stage_kernel, width=width),
         out_shape=tuple(jax.ShapeDtypeStruct((a.shape[0], width), BF16) for a in arrays),
-        in_specs=[HBM] * len(arrays),
+        in_specs=[HBM if held else pl.BlockSpec(memory_space=pl.ANY)] * len(arrays),
         out_specs=(VMEM,) * len(arrays),
         scratch_shapes=[pltpu.SemaphoreType.DMA((len(arrays),))],
         compiler_params=params(4),
         name="stage",
-    )(*(pltpu.with_memory_space_constraint(a, pltpu.HBM) for a in arrays))
+    )(*(pltpu.with_memory_space_constraint(a, pltpu.HBM) if held else a for a in arrays))
 
 
 def gates_kernel(emb_ref, gain_ref, proj_ref, out_ref):
@@ -449,23 +457,34 @@
     other_bias = partners(bias)
     ids = gather_relative(item_ids[None, :], 1, axis, size)
 
-    found, rounds = lookup(here, ids, [own_table, other_table], slots, size, True)
-    pieces = gather_relative(found, 0, axis, size)
+    (near_table,) = stage(width, other_table, held=False)
+    found, rounds = lookup(here, ids, [own_table, near_table], slots, size, True)
+    pieces = gather_rows(found, axis, size)
     pick = plan(here, ids, slots, table_rows, size)
 
     def more(state):
         turn, so_far = state
         picked = plan(place(turn), ids, slots, table_rows, size)
         found, _ = lookup(place(turn), ids, [item_table, other_table], slots, size, False)
-        return turn + 1, so_far + select(picked, gather_relative(found, 0, axis, size))
+        return turn + 1, so_far + select(picked, gather_rows(found, axis, size))
 
     none = jnp.zeros((each * (size // 2), width), BF16)
     _, extra = lax.while_loop(lambda s: s[0] < rounds[0], more, (jnp.int32(1), none))
 
-    proj, keys, values = stage(width, proj_in, key_cache, value_cache)
-    other_keys, other_values = stage(width, other_keys, other_values)
+    keys, values = stage(width, key_cache, value_cache)
+    proj, other_keys, other_values = stage(width, proj_in, other_keys, other_values)
     own, keep, send = attend(
-        rounds, pick, pieces, extra, gain, proj, [keys, other_keys], [values, other_values], [bias, other_bias], heads, each
+        rounds,
+        pick,
+        pieces,
+        extra,
+        gain,
+        proj,
+        [keys, other_keys],
+        [values, other_values],
+        [bias, other_bias],
+        heads,
+        each,
     )
     gates = gates_of(own, gain, proj_in)
 

time: 74.7 us -> 77 us (1.031)
  starting transfers between devices: 22.8 us -> 24.5 us
    ppermute x16 -> x17, starting transfers between devices: 22.8 us -> 24.5 us  [swap(): return lax.ppermute(x, axis, [(i, i ^ mask) for i in range(size)])]
    ppermute x16 -> x17, waiting for transfers between devices: 19.2 us -> 19.7 us  [swap(): return lax.ppermute(x, axis, [(i, i ^ mask) for i in range(size)])]
    pallas_call x2 -> x3, Pallas kernels: 5.12 us -> 5.28 us  [stage(): pl.pallas_call(functools.partial(stage_kernel, width=width), out_shape=tu...]
  transfers between devices with their start and end apart: 16 -> 17, of which waited for: 8 -> 9; matrix products, arithmetic and copies ran while one was open for 1% -> 1% of each run, Pallas kernels for 14% -> 14%
where the time goes in v7:
time: 77 us; the launch traced here: 76.7 us
  starting transfers between devices  24.5 us (32%)
  waiting for transfers between devices  19.7 us (26%)
  Pallas kernels  18.3 us (24%)
  local copies, waits for them, and re-layouts  12.6 us (16%)
  between operations  0.83 us (1%)
    ppermute x17, starting transfers between devices, swap(): return lax.ppermute(x, axis, [(i, i ^ mask) for i in range(size)])  24.5 us
    ppermute x17, waiting for transfers between devices, swap(): return lax.ppermute(x, axis, [(i, i ^ mask) for i in range(size)])  19.7 us
    unnamed x28, local copies, waits for them, and re-layouts  11.8 us
    pallas_call x1, Pallas kernels, attend(): pl.pallas_call(functools.partial(attend_kernel, heads=heads, blocks=block...  6.23 us
    pallas_call x3, Pallas kernels, stage(): pl.pallas_call(functools.partial(stage_kernel, width=width), out_shape=tu...  5.28 us
    pallas_call x1, Pallas kernels, prepare(): pl.pallas_call(functools.partial(prepare_kernel, npos=pos_bias.shape[1],...  2.21 us
    pallas_call x1, Pallas kernels, lookup(): pl.pallas_call(functools.partial(lookup_kernel, size=size, resident=resid...  2.02 us
  transfers between devices with their start and end apart: 17, of which 9 were waited for; matrix products, arithmetic and copies ran while one was open for 1% of the time, Pallas kernels for 14%

profile of v7, /device:TPU:0, one launch (start us, length us, event | category | flops | bytes accessed | tf_op | source)
XLA Modules:
  0.0 76.7 jit_solution(11853842851248171037)
XLA Ops:
  0.0 0.0 copy-start.13
  0.0 0.5 collective-permute-start.9
  0.5 0.1 collective-permute-start.15
  0.6 0.4 collective-permute-start.16
  1.7 0.1 pad_add_fusion.1.place_ref
  1.7 2.2 %prepare.1 = (bf16[1024,128]{1,0:T(8,128)(2,1)S(1)}, bf16[1024,1024]{1,0:T(8,128)(2,1)S(1)}) custom-call(s32[2]{0:T(128)S(1)} %pad_add_fusion.1.place_ref, s32[1]{0:T(128)S(6)} %copy.19.start_ref, s32[1,1024]{1,0:T(1,128)} %bitcast.16, f32[16,128]{1,0:T(8,128)} %time_bias_hbm.1, f32[16,18]{1,0:T(8,128)} %pos_bias_hbm.1, bf16[1024,1024]{1,0:T(8,128)(2,1)} %table_hbm.1), custom_call_target="tpu_custom_call" | custom-call | tf_op jit(solution)/shard_map/prepare/pallas_call | solution.py:244
  4.0 0.1 collective-permute-start.17
  4.1 0.0 copy-done.13
  4.1 3.0 %collective-permute-start.5 = (s32[1,16]{1,0:T(1,128)S(1)}, s32[1,16]{1,0:T(1,128)S(1)}, u32[]{:S(2)}, u32[]{:S(2)}) collective-permute-start(s32[1,16]{1,0:T(1,128)S(1)} %bitcast.17), channel_id=1, source_target_pairs={{0,4},{1,5},{2,6},{3,7},{4,0},{5,1},{6,2},{7,3},{8,12},{9,13},{10,... | collective-permute-start | bytes 200 | tf_op jit(solution)/shard_map/ppermute | solution.py:43
  7.1 1.5 %collective-permute-done.5 = s32[1,16]{1,0:T(1,128)S(1)} collective-permute-done((s32[1,16]{1,0:T(1,128)S(1)}, s32[1,16]{1,0:T(1,128)S(1)}, u32[]{:S(2)}, u32[]{:S(2)}) %collective-permute-start.5) | collective-permute-done | bytes 96 | tf_op jit(solution)/shard_map/ppermute | solution.py:43
  8.6 3.0 %collective-permute-start.6 = (s32[1,16]{1,0:T(1,128)S(1)}, s32[1,16]{1,0:T(1,128)S(1)}, u32[]{:S(2)}, u32[]{:S(2)}) collective-permute-start(s32[1,16]{1,0:T(1,128)S(1)} %bitcast.18), channel_id=1, source_target_pairs={{0,8},{1,9},{2,10},{3,11},{4,12},{5,13},{6,14},{7,15},{8,0},{9,1},... | collective-permute-start | bytes 200 | tf_op jit(solution)/shard_map/ppermute | solution.py:43
  11.7 1.5 %collective-permute-done.6 = s32[1,16]{1,0:T(1,128)S(1)} collective-permute-done((s32[1,16]{1,0:T(1,128)S(1)}, s32[1,16]{1,0:T(1,128)S(1)}, u32[]{:S(2)}, u32[]{:S(2)}) %collective-permute-start.6) | collective-permute-done | bytes 96 | tf_op jit(solution)/shard_map/ppermute | solution.py:43
  13.2 3.9 %collective-permute-start.7 = (s32[1,16]{1,0:T(1,128)S(1)}, s32[1,16]{1,0:T(1,128)S(1)}, u32[]{:S(2)}, u32[]{:S(2)}) collective-permute-start(s32[1,16]{1,0:T(1,128)S(1)} %bitcast.19), channel_id=1, source_target_pairs={{0,12},{1,13},{2,14},{3,15},{4,8},{5,9},{6,10},{7,11},{8,4},{9,5},... | collective-permute-start | bytes 200 | tf_op jit(solution)/shard_map/ppermute | solution.py:43
  17.2 1.5 %collective-permute-done.7 = s32[1,16]{1,0:T(1,128)S(1)} collective-permute-done((s32[1,16]{1,0:T(1,128)S(1)}, s32[1,16]{1,0:T(1,128)S(1)}, u32[]{:S(2)}, u32[]{:S(2)}) %collective-permute-start.7) | collective-permute-done | bytes 96 | tf_op jit(solution)/shard_map/ppermute | solution.py:43
  18.7 0.1 pad_add_fusion.2.refs_0_
  18.8 1.7 %collective-permute-start.8 = (s32[1,64]{1,0:T(1,128)S(1)}, s32[1,64]{1,0:T(1,128)S(1)}, u32[]{:S(2)}, u32[]{:S(2)}) collective-permute-start(s32[1,64]{1,0:T(1,128)S(1)} %pad_add_fusion.2.refs_0_), channel_id=1, source_target_pairs={{0,2},{1,3},{2,0},{3,1},{4,6},{5,7},{6,4},{7,5},{8,10},{9,11},{10,... | collective-permute-start | bytes 776 | tf_op jit(solution)/shard_map/ppermute | solution.py:43
  20.5 0.0 collective-permute-done.9.refs_0_
  20.5 0.2 stage.3.refs_3_
  20.7 1.7 %collective-permute-done.8.refs_1_ = s32[1,64]{1,0:T(1,128)S(1)} collective-permute-done((s32[1,64]{1,0:T(1,128)S(1)}, s32[1,64]{1,0:T(1,128)S(1)}, u32[]{:S(2)}, u32[]{:S(2)}) %collective-permute-start.8) | collective-permute-done | bytes 288 | tf_op jit(solution)/shard_map/ppermute | solution.py:43
  22.4 0.0 copy-done.12
  22.4 2.0 %lookup.2 = (bf16[32,1024]{1,0:T(8,128)(2,1)S(1)}, s32[1]{0:T(128)}) custom-call(s32[2]{0:T(128)S(1)} %pad_add_fusion.1.place_ref, s32[1,64]{1,0:T(1,128)S(1)} %pad_add_fusion.2.refs_0_, s32[1,64]{1,0:T(1,128)S(1)} %collective-permute-done.8.refs_1_, bf16[1024,1024]{1,0:T(8,128)(2,1)S(1)} %get-tuple-element.61.refs_2_, bf16[1024,1024]{1,0:T(8,128)(2,1)S(1)} %stage.3.refs_3_), custom_call_target="tpu_custom_call" | custom-call | tf_op jit(solution)/shard_map/lookup/pallas_call | solution.py:144
  24.4 0.1 collective-permute-start.10
  24.5 4.4 %collective-permute-start.11 = (bf16[32,1024]{1,0:T(8,128)(2,1)S(1)}, bf16[32,1024]{1,0:T(8,128)(2,1)S(1)}, u32[]{:S(2)}, u32[]{:S(2)}) collective-permute-start(bf16[32,1024]{1,0:T(8,128)(2,1)S(1)} %get-tuple-element.63.refs_0_), channel_id=1, source_target_pairs={{0,8},{1,9},{2,10},{3,11},{4,12},{5,13},{6,14},{7,15},{8,0},{9,1},... | collective-permute-start | bytes 196616 | tf_op jit(solution)/shard_map/ppermute | solution.py:43
  28.8 0.0 collective-permute-done.15.refs_1_
  28.8 0.0 collective-permute-start.12
  28.8 2.2 %stage.5 = (bf16[1024,1024]{1,0:T(8,128)(2,1)S(1)}, bf16[1024,1024]{1,0:T(8,128)(2,1)S(1)}) custom-call(bf16[1024,1024]{1,0:T(8,128)(2,1)} %refs_0_.3, bf16[1024,1024]{1,0:T(8,128)(2,1)} %refs_1_.1), custom_call_target="tpu_custom_call" | custom-call | tf_op jit(solution)/shard_map/stage/pallas_call | solution.py:367
  31.1 0.0 copy-start.2
  31.1 1.3 %copy-done.2 = bf16[1024,1024]{1,0:T(8,128)(2,1)} copy-done((bf16[1024,1024]{1,0:T(8,128)(2,1)}, bf16[1024,1024]{1,0:T(8,128)(2,1)S(1)}, u32[]{:S(2)}) %copy-start.2) | copy-done | bytes 2097176
  32.4 0.9 %plan.2.pick_ref = bf16[128,256]{1,0:T(8,128)(2,1)S(1)} custom-call(s32[2]{0:T(128)S(1)} %pad_add_fusion.1.place_ref, s32[1,64]{1,0:T(1,128)S(1)} %pad_add_fusion.2.refs_0_, s32[1,64]{1,0:T(1,128)S(1)} %collective-permute-done.8.refs_1_), custom_call_target="tpu_custom_call" | custom-call | tf_op jit(solution)/shard_map/plan/pallas_call | solution.py:181
  33.3 0.0 collective-permute-done.16.refs_2_
  33.3 2.9 %stage.4 = (bf16[1024,1024]{1,0:T(8,128)(2,1)S(1)}, bf16[1024,1024]{1,0:T(8,128)(2,1)S(1)}, bf16[1024,1024]{1,0:T(8,128)(2,1)S(1)}) custom-call(bf16[1024,2048]{1,0:T(8,128)(2,1)} %proj_ref.1, bf16[1024,1024]{1,0:T(8,128)(2,1)} %collective-permute-done.15.refs_1_, bf16[1024,1024]{1,0:T(8,128)(2,1)} %collective-permute-done.16.refs_2_), custom_call_target="tpu_custom_call" | custom-call | tf_op jit(solution)/shard_map/stage/pallas_call | solution.py:367
  36.2 0.0 copy-start.4
  36.2 1.4 %copy-done.4 = bf16[1024,1024]{1,0:T(8,128)(2,1)} copy-done((bf16[1024,1024]{1,0:T(8,128)(2,1)}, bf16[1024,1024]{1,0:T(8,128)(2,1)S(1)}, u32[]{:S(2)}) %copy-start.4) | copy-done | bytes 2097176
  37.6 1.4 %copy-done.6 = bf16[1024,1024]{1,0:T(8,128)(2,1)} copy-done((bf16[1024,1024]{1,0:T(8,128)(2,1)}, bf16[1024,1024]{1,0:T(8,128)(2,1)S(1)}, u32[]{:S(2)}) %copy-start.6) | copy-done | bytes 2097176
  39.0 1.3 %copy-done.8 = bf16[1024,1024]{1,0:T(8,128)(2,1)} copy-done((bf16[1024,1024]{1,0:T(8,128)(2,1)}, bf16[1024,1024]{1,0:T(8,128)(2,1)S(1)}, u32[]{:S(2)}) %copy-start.8) | copy-done | bytes 2097176
  40.3 1.7 %collective-permute-start.13 = (bf16[32,1024]{1,0:T(8,128)(2,1)S(1)}, bf16[32,1024]{1,0:T(8,128)(2,1)S(1)}, u32[]{:S(2)}, u32[]{:S(2)}) collective-permute-start(bf16[32,1024]{1,0:T(8,128)(2,1)S(1)} %get-tuple-element.63.refs_0_), channel_id=1, source_target_pairs={{0,2},{1,3},{2,0},{3,1},{4,6},{5,7},{6,4},{7,5},{8,10},{9,11},{10,... | collective-permute-start | bytes 196616 | tf_op jit(solution)/shard_map/ppermute | solution.py:43
  42.1 0.0 collective-permute-done.10.refs_0_
  42.1 0.0 collective-permute-done.11.refs_1_
  42.1 0.0 collective-permute-done.12.refs_2_
  42.1 0.4 collective-permute-start.14
  42.5 0.0 collective-permute-done.17.refs_12_
  42.5 0.7 broadcast_in_dim.17
  43.2 0.6 while.10
  43.9 0.8 collective-permute-done.13.refs_2_
  44.6 3.2 %collective-permute-done.14.refs_3_ = bf16[96,1024]{1,0:T(8,128)(2,1)S(1)} collective-permute-done((bf16[96,1024]{1,0:T(8,128)(2,1)S(1)}, bf16[96,1024]{1,0:T(8,128)(2,1)S(1)}, u32[]{:S(2)}, u32[]{:S(2)}) %collective-permute-start.14) | collective-permute-done | bytes 196640 | tf_op jit(solution)/shard_map/ppermute | solution.py:43
  47.9 0.0 copy-done.10
  47.9 1.6 %copy-done.3 = bf16[1024,1024]{1,0:T(8,128)(2,1)S(1)} copy-done((bf16[1024,1024]{1,0:T(8,128)(2,1)S(1)}, bf16[1024,1024]{1,0:T(8,128)(2,1)}, u32[]{:S(2)}) %copy-start.3) | copy-done | bytes 2097176
  49.5 1.6 %copy-done.5 = bf16[1024,1024]{1,0:T(8,128)(2,1)S(1)} copy-done((bf16[1024,1024]{1,0:T(8,128)(2,1)S(1)}, bf16[1024,1024]{1,0:T(8,128)(2,1)}, u32[]{:S(2)}) %copy-start.5) | copy-done | bytes 2097176
  51.0 1.6 %copy-done.7 = bf16[1024,1024]{1,0:T(8,128)(2,1)S(1)} copy-done((bf16[1024,1024]{1,0:T(8,128)(2,1)S(1)}, bf16[1024,1024]{1,0:T(8,128)(2,1)}, u32[]{:S(2)}) %copy-start.7) | copy-done | bytes 2097176
  52.6 1.6 %copy-done.9 = bf16[1024,1024]{1,0:T(8,128)(2,1)S(1)} copy-done((bf16[1024,1024]{1,0:T(8,128)(2,1)S(1)}, bf16[1024,1024]{1,0:T(8,128)(2,1)}, u32[]{:S(2)}) %copy-start.9) | copy-done | bytes 2097176
  54.2 6.2 %attend.1 = (bf16[16,1024]{1,0:T(8,128)(2,1)S(1)}, f32[64,1024]{1,0:T(8,128)S(1)}, bf16[64,1024]{1,0:T(8,128)(2,1)S(1)}) custom-call(s32[1]{0:T(128)} %get-tuple-element.149.rounds_ref, bf16[128,256]{1,0:T(8,128)(2,1)S(1)} %plan.2.pick_ref, bf16[32,1024]{1,0:T(8,128)(2,1)S(1)} %get-tuple-element.63.refs_0_, bf16[96,1024]{1,0:T(8,128)(2,1)S(1)} %join.2.refs_1_, ...), custom_call_target="tpu_custom_call" | custom-call | flops 2147483648 | bytes 8388608 | tf_op jit(solution)/shard_map/attend/pallas_call | solution.py:327
  60.5 0.7 collective-permute-start.18
  61.1 4.4 %collective-permute-done.18 = bf16[64,1024]{1,0:T(8,128)(2,1)S(1)} collective-permute-done((bf16[64,1024]{1,0:T(8,128)(2,1)S(1)}, bf16[64,1024]{1,0:T(8,128)(2,1)S(1)}, u32[]{:S(2)}, u32[]{:S(2)}) %collective-permute-start.18) | collective-permute-done | bytes 131104 | tf_op jit(solution)/shard_map/ppermute | solution.py:43
  65.6 0.4 collective-permute-start.19
  66.0 3.8 %collective-permute-start.20 = (bf16[16,1024]{1,0:T(8,128)(2,1)S(1)}, bf16[16,1024]{1,0:T(8,128)(2,1)S(1)}, u32[]{:S(2)}, u32[]{:S(2)}) collective-permute-start(bf16[16,1024]{1,0:T(8,128)(2,1)S(1)} %get-tuple-element.93), channel_id=1, source_target_pairs={{0,8},{1,9},{2,10},{3,11},{4,12},{5,13},{6,14},{7,15},{8,0},{9,1},... | collective-permute-start | bytes 98312 | tf_op jit(solution)/shard_map/ppermute | solution.py:43
  69.8 0.2 collective-permute-start.21
  70.0 0.0 copy-done
  70.0 0.5 gates.1.refs_4_
  70.5 0.0 collective-permute-done.19.refs_0_
  70.5 1.5 %collective-permute-done.20.refs_1_ = bf16[16,1024]{1,0:T(8,128)(2,1)S(1)} collective-permute-done((bf16[16,1024]{1,0:T(8,128)(2,1)S(1)}, bf16[16,1024]{1,0:T(8,128)(2,1)S(1)}, u32[]{:S(2)}, u32[]{:S(2)}) %collective-permute-start.20) | collective-permute-done | bytes 32800 | tf_op jit(solution)/shard_map/ppermute | solution.py:43
  72.0 3.5 %collective-permute-done.21.refs_2_ = bf16[16,1024]{1,0:T(8,128)(2,1)S(1)} collective-permute-done((bf16[16,1024]{1,0:T(8,128)(2,1)S(1)}, bf16[16,1024]{1,0:T(8,128)(2,1)S(1)}, u32[]{:S(2)}, u32[]{:S(2)}) %collective-permute-start.21) | collective-permute-done | bytes 32800 | tf_op jit(solution)/shard_map/ppermute | solution.py:43
  75.5 0.0 copy-done.1
  75.5 0.0 copy-done.11
  75.5 1.2 %finish.1 = bf16[16,1024]{1,0:T(8,128)(2,1)} custom-call(f32[16,1024]{1,0:T(8,128)S(1)} %slice.19.own_ref, bf16[16,1024]{1,0:T(8,128)(2,1)S(1)} %collective-permute-done.19.refs_0_, bf16[16,1024]{1,0:T(8,128)(2,1)S(1)} %collective-permute-done.20.refs_1_, bf16[16,1024]{1,0:T(8,128)(2,1)S(1)} %collective-permute-done.21.refs_2_, ...), custom_call_target="tpu_custom_call" | custom-call | tf_op jit(solution)/shard_map/finish/pallas_call | solution.py:410
  (15 shorter events, 0.1 us)
Async XLA Ops:
  0.0 4.1 %copy-start.13 = (s32[16]{0:T(128)S(1)}, s32[16]{0:T(128)}, u32[]{:S(2)}) copy-start(s32[16]{0:T(128)} %param.14) | copy-start | bytes 196
  0.0 20.5 %collective-permute-start.9 = (bf16[1024,1024]{1,0:T(8,128)(2,1)}, bf16[1024,1024]{1,0:T(8,128)(2,1)S(1)}, u32[]{:S(2)}, u32[]{:S(2)}) collective-permute-start(bf16[1024,1024]{1,0:T(8,128)(2,1)} %table_hbm.1), channel_id=1, source_target_pairs={{0,1},{1,0},{2,3},{3,2},{4,5},{5,4},{6,7},{7,6},{8,9},{9,8},{10,11... | collective-permute-start | bytes 6291464 | tf_op jit(solution)/shard_map/ppermute | solution.py:43
  0.5 28.3 %collective-permute-start.15 = (bf16[1024,1024]{1,0:T(8,128)(2,1)}, bf16[1024,1024]{1,0:T(8,128)(2,1)}, u32[]{:S(2)}, u32[]{:S(2)}) collective-permute-start(bf16[1024,1024]{1,0:T(8,128)(2,1)} %refs_0_.3), channel_id=1, source_target_pairs={{0,1},{1,0},{2,3},{3,2},{4,5},{5,4},{6,7},{7,6},{8,9},{9,8},{10,11... | collective-permute-start | bytes 6291464 | tf_op jit(solution)/shard_map/ppermute | solution.py:43
  0.6 32.8 %collective-permute-start.16 = (bf16[1024,1024]{1,0:T(8,128)(2,1)}, bf16[1024,1024]{1,0:T(8,128)(2,1)}, u32[]{:S(2)}, u32[]{:S(2)}) collective-permute-start(bf16[1024,1024]{1,0:T(8,128)(2,1)} %refs_1_.1), channel_id=1, source_target_pairs={{0,1},{1,0},{2,3},{3,2},{4,5},{5,4},{6,7},{7,6},{8,9},{9,8},{10,11... | collective-permute-start | bytes 6291464 | tf_op jit(solution)/shard_map/ppermute | solution.py:43
  4.0 38.5 %collective-permute-start.17 = (bf16[1024,128]{1,0:T(8,128)(2,1)S(1)}, bf16[1024,128]{1,0:T(8,128)(2,1)S(1)}, u32[]{:S(2)}, u32[]{:S(2)}) collective-permute-start(bf16[1024,128]{1,0:T(8,128)(2,1)S(1)} %get-tuple-element.70.refs_11_), channel_id=1, source_target_pairs={{0,1},{1,0},{2,3},{3,2},{4,5},{5,4},{6,7},{7,6},{8,9},{9,8},{10,11... | collective-permute-start | bytes 786440 | tf_op jit(solution)/shard_map/ppermute | solution.py:43
  4.1 4.6 %collective-permute-start.5 = (s32[1,16]{1,0:T(1,128)S(1)}, s32[1,16]{1,0:T(1,128)S(1)}, u32[]{:S(2)}, u32[]{:S(2)}) collective-permute-start(s32[1,16]{1,0:T(1,128)S(1)} %bitcast.17), channel_id=1, source_target_pairs={{0,4},{1,5},{2,6},{3,7},{4,0},{5,1},{6,2},{7,3},{8,12},{9,13},{10,... | collective-permute-start | bytes 200 | tf_op jit(solution)/shard_map/ppermute | solution.py:43
  8.6 4.6 %collective-permute-start.6 = (s32[1,16]{1,0:T(1,128)S(1)}, s32[1,16]{1,0:T(1,128)S(1)}, u32[]{:S(2)}, u32[]{:S(2)}) collective-permute-start(s32[1,16]{1,0:T(1,128)S(1)} %bitcast.18), channel_id=1, source_target_pairs={{0,8},{1,9},{2,10},{3,11},{4,12},{5,13},{6,14},{7,15},{8,0},{9,1},... | collective-permute-start | bytes 200 | tf_op jit(solution)/shard_map/ppermute | solution.py:43
  13.2 5.5 %collective-permute-start.7 = (s32[1,16]{1,0:T(1,128)S(1)}, s32[1,16]{1,0:T(1,128)S(1)}, u32[]{:S(2)}, u32[]{:S(2)}) collective-permute-start(s32[1,16]{1,0:T(1,128)S(1)} %bitcast.19), channel_id=1, source_target_pairs={{0,12},{1,13},{2,14},{3,15},{4,8},{5,9},{6,10},{7,11},{8,4},{9,5},... | collective-permute-start | bytes 200 | tf_op jit(solution)/shard_map/ppermute | solution.py:43
  18.8 3.6 %collective-permute-start.8 = (s32[1,64]{1,0:T(1,128)S(1)}, s32[1,64]{1,0:T(1,128)S(1)}, u32[]{:S(2)}, u32[]{:S(2)}) collective-permute-start(s32[1,64]{1,0:T(1,128)S(1)} %pad_add_fusion.2.refs_0_), channel_id=1, source_target_pairs={{0,2},{1,3},{2,0},{3,1},{4,6},{5,7},{6,4},{7,5},{8,10},{9,11},{10,... | collective-permute-start | bytes 776 | tf_op jit(solution)/shard_map/ppermute | solution.py:43
  20.5 1.8 %copy-start.12 = (bf16[1024,1024]{1,0:T(8,128)(2,1)}, bf16[1024,1024]{1,0:T(8,128)(2,1)S(1)}, u32[]{:S(2)}) copy-start(bf16[1024,1024]{1,0:T(8,128)(2,1)S(1)} %collective-permute-done.9.refs_0_) | copy-start | bytes 6291460
  24.4 17.7 %collective-permute-start.10 = (bf16[32,1024]{1,0:T(8,128)(2,1)S(1)}, bf16[32,1024]{1,0:T(8,128)(2,1)S(1)}, u32[]{:S(2)}, u32[]{:S(2)}) collective-permute-start(bf16[32,1024]{1,0:T(8,128)(2,1)S(1)} %get-tuple-element.63.refs_0_), channel_id=1, source_target_pairs={{0,4},{1,5},{2,6},{3,7},{4,0},{5,1},{6,2},{7,3},{8,12},{9,13},{10,... | collective-permute-start | bytes 196616 | tf_op jit(solution)/shard_map/ppermute | solution.py:43
  24.5 17.6 %collective-permute-start.11 = (bf16[32,1024]{1,0:T(8,128)(2,1)S(1)}, bf16[32,1024]{1,0:T(8,128)(2,1)S(1)}, u32[]{:S(2)}, u32[]{:S(2)}) collective-permute-start(bf16[32,1024]{1,0:T(8,128)(2,1)S(1)} %get-tuple-element.63.refs_0_), channel_id=1, source_target_pairs={{0,8},{1,9},{2,10},{3,11},{4,12},{5,13},{6,14},{7,15},{8,0},{9,1},... | collective-permute-start | bytes 196616 | tf_op jit(solution)/shard_map/ppermute | solution.py:43
  28.8 13.3 %collective-permute-start.12 = (bf16[32,1024]{1,0:T(8,128)(2,1)S(1)}, bf16[32,1024]{1,0:T(8,128)(2,1)S(1)}, u32[]{:S(2)}, u32[]{:S(2)}) collective-permute-start(bf16[32,1024]{1,0:T(8,128)(2,1)S(1)} %get-tuple-element.63.refs_0_), channel_id=1, source_target_pairs={{0,12},{1,13},{2,14},{3,15},{4,8},{5,9},{6,10},{7,11},{8,4},{9,5},... | collective-permute-start | bytes 196616 | tf_op jit(solution)/shard_map/ppermute | solution.py:43
  31.1 1.4 %copy-start.2 = (bf16[1024,1024]{1,0:T(8,128)(2,1)}, bf16[1024,1024]{1,0:T(8,128)(2,1)S(1)}, u32[]{:S(2)}) copy-start(bf16[1024,1024]{1,0:T(8,128)(2,1)S(1)} %get-tuple-element.68.refs_9_) | copy-start | bytes 6291460
  36.2 1.4 %copy-start.4 = (bf16[1024,1024]{1,0:T(8,128)(2,1)}, bf16[1024,1024]{1,0:T(8,128)(2,1)S(1)}, u32[]{:S(2)}) copy-start(bf16[1024,1024]{1,0:T(8,128)(2,1)S(1)} %get-tuple-element.65.refs_6_) | copy-start | bytes 6291460
  37.6 1.4 %copy-start.6 = (bf16[1024,1024]{1,0:T(8,128)(2,1)}, bf16[1024,1024]{1,0:T(8,128)(2,1)S(1)}, u32[]{:S(2)}) copy-start(bf16[1024,1024]{1,0:T(8,128)(2,1)S(1)} %get-tuple-element.67.refs_8_) | copy-start | bytes 6291460
  39.0 1.3 %copy-start.8 = (bf16[1024,1024]{1,0:T(8,128)(2,1)}, bf16[1024,1024]{1,0:T(8,128)(2,1)S(1)}, u32[]{:S(2)}) copy-start(bf16[1024,1024]{1,0:T(8,128)(2,1)S(1)} %get-tuple-element.69.refs_10_) | copy-start | bytes 6291460
  40.3 4.3 %collective-permute-start.13 = (bf16[32,1024]{1,0:T(8,128)(2,1)S(1)}, bf16[32,1024]{1,0:T(8,128)(2,1)S(1)}, u32[]{:S(2)}, u32[]{:S(2)}) collective-permute-start(bf16[32,1024]{1,0:T(8,128)(2,1)S(1)} %get-tuple-element.63.refs_0_), channel_id=1, source_target_pairs={{0,2},{1,3},{2,0},{3,1},{4,6},{5,7},{6,4},{7,5},{8,10},{9,11},{10,... | collective-permute-start | bytes 196616 | tf_op jit(solution)/shard_map/ppermute | solution.py:43
  42.1 5.7 %collective-permute-start.14 = (bf16[96,1024]{1,0:T(8,128)(2,1)S(1)}, bf16[96,1024]{1,0:T(8,128)(2,1)S(1)}, u32[]{:S(2)}, u32[]{:S(2)}) collective-permute-start(bf16[96,1024]{1,0:T(8,128)(2,1)S(1)} %join.2.refs_1_), channel_id=1, source_target_pairs={{0,2},{1,3},{2,0},{3,1},{4,6},{5,7},{6,4},{7,5},{8,10},{9,11},{10,... | collective-permute-start | bytes 589832 | tf_op jit(solution)/shard_map/ppermute | solution.py:43
  43.2 4.6 %copy-start.10 = (f32[1024]{0:T(1024)S(1)}, f32[1024]{0:T(1024)}, u32[]{:S(2)}) copy-start(f32[1024]{0:T(1024)} %param.20) | copy-start | bytes 12292
  47.9 1.6 %copy-start.3 = (bf16[1024,1024]{1,0:T(8,128)(2,1)S(1)}, bf16[1024,1024]{1,0:T(8,128)(2,1)}, u32[]{:S(2)}) copy-start(bf16[1024,1024]{1,0:T(8,128)(2,1)} %copy-done.2) | copy-start | bytes 6291460
  49.5 1.6 %copy-start.5 = (bf16[1024,1024]{1,0:T(8,128)(2,1)S(1)}, bf16[1024,1024]{1,0:T(8,128)(2,1)}, u32[]{:S(2)}) copy-start(bf16[1024,1024]{1,0:T(8,128)(2,1)} %copy-done.4) | copy-start | bytes 6291460
  51.0 1.6 %copy-start.7 = (bf16[1024,1024]{1,0:T(8,128)(2,1)S(1)}, bf16[1024,1024]{1,0:T(8,128)(2,1)}, u32[]{:S(2)}) copy-start(bf16[1024,1024]{1,0:T(8,128)(2,1)} %copy-done.6) | copy-start | bytes 6291460
  52.6 1.6 %copy-start.9 = (bf16[1024,1024]{1,0:T(8,128)(2,1)S(1)}, bf16[1024,1024]{1,0:T(8,128)(2,1)}, u32[]{:S(2)}) copy-start(bf16[1024,1024]{1,0:T(8,128)(2,1)} %copy-done.8) | copy-start | bytes 6291460
  54.2 15.8 %copy-start = (bf16[1024,2048]{1,0:T(8,128)(2,1)S(1)}, bf16[1024,2048]{1,0:T(8,128)(2,1)}, u32[]{:S(2)}) copy-start(bf16[1024,2048]{1,0:T(8,128)(2,1)} %proj_ref.1) | copy-start | bytes 12582916
  60.5 5.0 %collective-permute-start.18 = (bf16[64,1024]{1,0:T(8,128)(2,1)S(1)}, bf16[64,1024]{1,0:T(8,128)(2,1)S(1)}, u32[]{:S(2)}, u32[]{:S(2)}) collective-permute-start(bf16[64,1024]{1,0:T(8,128)(2,1)S(1)} %get-tuple-element.72), channel_id=1, source_target_pairs={{0,2},{1,3},{2,0},{3,1},{4,6},{5,7},{6,4},{7,5},{8,10},{9,11},{10,... | collective-permute-start | bytes 393224 | tf_op jit(solution)/shard_map/ppermute | solution.py:43
  65.6 5.0 %collective-permute-start.19 = (bf16[16,1024]{1,0:T(8,128)(2,1)S(1)}, bf16[16,1024]{1,0:T(8,128)(2,1)S(1)}, u32[]{:S(2)}, u32[]{:S(2)}) collective-permute-start(bf16[16,1024]{1,0:T(8,128)(2,1)S(1)} %get-tuple-element.94), channel_id=1, source_target_pairs={{0,4},{1,5},{2,6},{3,7},{4,0},{5,1},{6,2},{7,3},{8,12},{9,13},{10,... | collective-permute-start | bytes 98312 | tf_op jit(solution)/shard_map/ppermute | solution.py:43
  66.0 6.1 %collective-permute-start.20 = (bf16[16,1024]{1,0:T(8,128)(2,1)S(1)}, bf16[16,1024]{1,0:T(8,128)(2,1)S(1)}, u32[]{:S(2)}, u32[]{:S(2)}) collective-permute-start(bf16[16,1024]{1,0:T(8,128)(2,1)S(1)} %get-tuple-element.93), channel_id=1, source_target_pairs={{0,8},{1,9},{2,10},{3,11},{4,12},{5,13},{6,14},{7,15},{8,0},{9,1},... | collective-permute-start | bytes 98312 | tf_op jit(solution)/shard_map/ppermute | solution.py:43
  69.8 5.7 %collective-permute-start.21 = (bf16[16,1024]{1,0:T(8,128)(2,1)S(1)}, bf16[16,1024]{1,0:T(8,128)(2,1)S(1)}, u32[]{:S(2)}, u32[]{:S(2)}) collective-permute-start(bf16[16,1024]{1,0:T(8,128)(2,1)S(1)} %get-tuple-element.92), channel_id=1, source_target_pairs={{0,12},{1,13},{2,14},{3,15},{4,8},{5,9},{6,10},{7,11},{8,4},{9,5},... | collective-permute-start | bytes 98312 | tf_op jit(solution)/shard_map/ppermute | solution.py:43
  70.0 5.5 %copy-start.1 = (bf16[1024,1024]{1,0:T(8,128)(2,1)S(1)}, bf16[1024,1024]{1,0:T(8,128)(2,1)}, u32[]{:S(2)}) copy-start(bf16[1024,1024]{1,0:T(8,128)(2,1)} %refs_6_.1) | copy-start | bytes 6291460
  70.0 5.5 %copy-start.11 = (f32[1024]{0:T(1024)S(1)}, f32[1024]{0:T(1024)}, u32[]{:S(2)}) copy-start(f32[1024]{0:T(1024)} %param.24) | copy-start | bytes 12292

commit v8 on v7

--- a/solution.py
+++ b/solution.py
@@ -11,8 +11,11 @@
 BF16 = jnp.bfloat16
 F32 = jnp.float32
 LANES = 128
-ROWS_AT_ONCE = 256
-EVENTS_AT_ONCE = 1024
+ROWS_AT_ONCE = 128
+EVENTS_AT_ONCE = 512
+STEPS_AHEAD = 2
+BLOCK = 16
+TN = (((0,), (0,)), ((), ()))
 NT = (((1,), (1,)), ((), ()))
 VMEM = pl.BlockSpec(memory_space=pltpu.VMEM)
 SMEM = pl.BlockSpec(memory_space=pltpu.SMEM)
@@ -107,10 +110,10 @@
 
 def lookup_kernel(place_ref, *refs, size, resident):
     if resident:
-        *ids_refs, own_ref, other_ref, out_ref, rounds_ref = refs
+        *ids_refs, own_ref, other_ref, out_ref, rounds_ref, blocks_ref = refs
         copies = []
     else:
-        *ids_refs, own_hbm, other_hbm, out_ref, rounds_ref, own_ref, other_ref, sems = refs
+        *ids_refs, own_hbm, other_hbm, out_ref, rounds_ref, blocks_ref, own_ref, other_ref, sems = refs
         copies = [
             pltpu.make_async_copy(own_hbm, own_ref, sems.at[0]),
             pltpu.make_async_copy(other_hbm, other_ref, sems.at[1]),
@@ -128,13 +131,21 @@
     slot = lax.broadcasted_iota(jnp.int32, (slots, count), 0) + turn * slots
     hit = (pair == (me >> 1)) & (rank == slot)
     want = jnp.sum(jnp.where(hit, offset + 1, 0), axis=1, keepdims=True) - 1
-    row = lax.broadcasted_iota(jnp.int32, (slots, rows), 1)
     rounds_ref[0] = jnp.max(rank) // slots + 1
     for c in copies:
         c.wait()
-    found = jnp.dot((want == row).astype(F32).astype(BF16), own_ref[...], preferred_element_type=F32)
-    other = (want == row + rows).astype(F32).astype(BF16)
-    out_ref[...] = (found + jnp.dot(other, other_ref[...], preferred_element_type=F32)).astype(BF16)
+    near = jnp.where(want < 0, 0, want // BLOCK)
+    for k in range(slots):
+        block = near[k, 0]
+        in_own = block < rows // BLOCK
+        at = pl.multiple_of((block - jnp.where(in_own, 0, rows // BLOCK)) * BLOCK, BLOCK)
+        own, other = own_ref[pl.ds(at, BLOCK), :], other_ref[pl.ds(at, BLOCK), :]
+        blocks_ref[k * BLOCK : (k + 1) * BLOCK, :] = jnp.where(in_own, own, other)
+    column = lax.broadcasted_iota(jnp.int32, (slots, slots * BLOCK), 1)
+    line = lax.broadcasted_iota(jnp.int32, (slots, slots * BLOCK), 0)
+    pick = (want >= 0) & (column == line * BLOCK + (want - near * BLOCK))
+    found = jnp.dot(pick.astype(F32).astype(BF16), blocks_ref[...], preferred_element_type=F32)
+    out_ref[...] = found.astype(BF16)
 
 
 def lookup(place, ids, tables, slots, size, resident):
@@ -149,9 +160,8 @@
         ),
         in_specs=[SMEM] + [VMEM] * len(ids) + [VMEM if resident else HBM] * 2,
         out_specs=(VMEM, SMEM),
-        scratch_shapes=[]
-        if resident
-        else [pltpu.VMEM((rows, width), BF16)] * 2 + [pltpu.SemaphoreType.DMA((2,))],
+        scratch_shapes=[pltpu.VMEM((slots * BLOCK, width), BF16)]
+        + ([] if resident else [pltpu.VMEM((rows, width), BF16)] * 2 + [pltpu.SemaphoreType.DMA((2,))]),
         compiler_params=params(16),
         name="lookup",
     )(place, *ids, *tables)
@@ -291,27 +301,57 @@
         query = silu(projected).astype(BF16)
         query_ref[first : first + rows, :] = query * jnp.asarray(0.5 * head_dim**-0.5, BF16)
         lane = lax.broadcasted_iota(jnp.int32, (rows, LANES), 1)
-        for group in range(width // LANES):
+        stacks = {}
+
+        def stack(group):
+            if group not in stacks:
+                part = query_ref[first : first + rows, group * LANES : (group + 1) * LANES]
+                zero, one = jnp.zeros_like(part), jnp.ones_like(part)
+                blocks_of = []
+                for k in range(per):
+                    own = jnp.where(lane // head_dim == k, part, zero)
+                    chosen = jnp.where(lane % heads == group * per + k, one, zero)
+                    blocks_of.append(jnp.concatenate([own, chosen], axis=1))
+                stacks[group] = jnp.concatenate(blocks_of, axis=0)
+            return stacks[group]
+
+        def halves(group, block, j):
             at = slice(group * LANES, (group + 1) * LANES)
-            part = query_ref[first : first + rows, at]
-            zero, one = jnp.zeros_like(part), jnp.ones_like(part)
-            stacked = []
-            for k in range(per):
-                own = jnp.where(lane // head_dim == k, part, zero)
-                chosen = jnp.where(lane % heads == group * per + k, one, zero)
-                stacked.append(jnp.concatenate([own, chosen], axis=1))
-            left = jnp.concatenate(stacked, axis=0)
-            total = jnp.zeros((per * rows, LANES), F32)
-            for key_ref, value_ref, bias_ref in zip(*(caches[k * blocks : (k + 1) * blocks] for k in range(3))):
-                step = min(EVENTS_AT_ONCE, key_ref.shape[0])
-                for j in range(0, key_ref.shape[0], step):
-                    right = jnp.concatenate([key_ref[j : j + step, at], bias_ref[j : j + step, :]], axis=1)
-                    t = lax.dot_general(left, right, NT, preferred_element_type=F32)
-                    weights = (t + t * jnp.tanh(t)).astype(BF16)
-                    total = total + jnp.dot(weights, value_ref[j : j + step, at], preferred_element_type=F32)
-            out = total[:rows]
-            for k in range(1, per):
-                out = jnp.where(lane // head_dim == k, total[k * rows : (k + 1) * rows], out)
+            keys = jnp.concatenate(
+                [caches[block][j : j + step, at], caches[2 * blocks + block][j : j + step, :]], axis=1
+            )
+            return lax.dot_general(keys, stack(group), NT, preferred_element_type=F32)
+
+        events = caches[0].shape[0]
+        step = min(EVENTS_AT_ONCE, events)
+        steps = [
+            (group, block, j)
+            for group in range(width // LANES)
+            for block in range(blocks)
+            for j in range(0, events, step)
+        ]
+        ahead = [halves(*s) for s in steps[:STEPS_AHEAD]]
+        total = None
+        for n, (group, block, j) in enumerate(steps):
+            if n + STEPS_AHEAD < len(steps):
+                ahead.append(halves(*steps[n + STEPS_AHEAD]))
+            t = ahead.pop(0)
+            weights = (t + t * jnp.tanh(t)).astype(BF16)
+            at = slice(group * LANES, (group + 1) * LANES)
+            term = lax.dot_general(
+                caches[blocks + block][j : j + step, at], weights, TN, preferred_element_type=F32
+            )
+            total = term if total is None else total + term
+            if n + 1 < len(steps) and steps[n + 1][0] == group:
+                continue
+            out = jnp.concatenate(
+                [
+                    total[k * head_dim : (k + 1) * head_dim, k * rows : (k + 1) * rows]
+                    for k in range(per)
+                ],
+                axis=0,
+            ).T
+            total = None
             if first + rows <= half:
                 keep_ref[first : first + rows, at] = out
             elif first >= half:

time: 77 us -> 76 us (0.987)
  Pallas kernels: 18.3 us -> 17.3 us
where the time goes in v8:
time: 76 us; the launch traced here: 75.7 us
  starting transfers between devices  24.5 us (32%)
  waiting for transfers between devices  19.7 us (26%)
  Pallas kernels  17.3 us (23%)
  local copies, waits for them, and re-layouts  12.6 us (17%)
  between operations  0.83 us (1%)
    ppermute x17, starting transfers between devices, swap(): return lax.ppermute(x, axis, [(i, i ^ mask) for i in range(size)])  24.5 us
    ppermute x17, waiting for transfers between devices, swap(): return lax.ppermute(x, axis, [(i, i ^ mask) for i in range(size)])  19.7 us
    unnamed x28, local copies, waits for them, and re-layouts  11.8 us
    pallas_call x1, Pallas kernels, attend(): pl.pallas_call(functools.partial(attend_kernel, heads=heads, blocks=block...  5.71 us
    pallas_call x3, Pallas kernels, stage(): pl.pallas_call(functools.partial(stage_kernel, width=width), out_shape=tu...  5.28 us
    pallas_call x1, Pallas kernels, prepare(): pl.pallas_call(functools.partial(prepare_kernel, npos=pos_bias.shape[1],...  2.21 us
    pallas_call x1, Pallas kernels, lookup(): pl.pallas_call(functools.partial(lookup_kernel, size=size, resident=resid...  1.6 us
  transfers between devices with their start and end apart: 17, of which 9 were waited for; matrix products, arithmetic and copies ran while one was open for 1% of the time, Pallas kernels for 14%

profile of v8, /device:TPU:0, one launch (start us, length us, event | category | flops | bytes accessed | tf_op | source)
XLA Modules:
  0.0 75.7 jit_solution(8919599052949216275)
XLA Ops:
  0.0 0.0 copy-start.13
  0.0 0.5 collective-permute-start.9
  0.5 0.1 collective-permute-start.15
  0.6 0.4 collective-permute-start.16
  1.7 0.1 pad_add_fusion.1.place_ref
  1.7 2.2 %prepare.1 = (bf16[1024,128]{1,0:T(8,128)(2,1)S(1)}, bf16[1024,1024]{1,0:T(8,128)(2,1)S(1)}) custom-call(s32[2]{0:T(128)S(1)} %pad_add_fusion.1.place_ref, s32[1]{0:T(128)S(6)} %copy.19.start_ref, s32[1,1024]{1,0:T(1,128)} %bitcast.16, f32[16,128]{1,0:T(8,128)} %time_bias_hbm.1, f32[16,18]{1,0:T(8,128)} %pos_bias_hbm.1, bf16[1024,1024]{1,0:T(8,128)(2,1)} %table_hbm.1), custom_call_target="tpu_custom_call" | custom-call | tf_op jit(solution)/shard_map/prepare/pallas_call | solution.py:254
  4.0 0.1 collective-permute-start.17
  4.1 0.0 copy-done.13
  4.1 3.0 %collective-permute-start.5 = (s32[1,16]{1,0:T(1,128)S(1)}, s32[1,16]{1,0:T(1,128)S(1)}, u32[]{:S(2)}, u32[]{:S(2)}) collective-permute-start(s32[1,16]{1,0:T(1,128)S(1)} %bitcast.17), channel_id=1, source_target_pairs={{0,4},{1,5},{2,6},{3,7},{4,0},{5,1},{6,2},{7,3},{8,12},{9,13},{10,... | collective-permute-start | bytes 200 | tf_op jit(solution)/shard_map/ppermute | solution.py:46
  7.1 1.5 %collective-permute-done.5 = s32[1,16]{1,0:T(1,128)S(1)} collective-permute-done((s32[1,16]{1,0:T(1,128)S(1)}, s32[1,16]{1,0:T(1,128)S(1)}, u32[]{:S(2)}, u32[]{:S(2)}) %collective-permute-start.5) | collective-permute-done | bytes 96 | tf_op jit(solution)/shard_map/ppermute | solution.py:46
  8.6 3.0 %collective-permute-start.6 = (s32[1,16]{1,0:T(1,128)S(1)}, s32[1,16]{1,0:T(1,128)S(1)}, u32[]{:S(2)}, u32[]{:S(2)}) collective-permute-start(s32[1,16]{1,0:T(1,128)S(1)} %bitcast.18), channel_id=1, source_target_pairs={{0,8},{1,9},{2,10},{3,11},{4,12},{5,13},{6,14},{7,15},{8,0},{9,1},... | collective-permute-start | bytes 200 | tf_op jit(solution)/shard_map/ppermute | solution.py:46
  11.7 1.5 %collective-permute-done.6 = s32[1,16]{1,0:T(1,128)S(1)} collective-permute-done((s32[1,16]{1,0:T(1,128)S(1)}, s32[1,16]{1,0:T(1,128)S(1)}, u32[]{:S(2)}, u32[]{:S(2)}) %collective-permute-start.6) | collective-permute-done | bytes 96 | tf_op jit(solution)/shard_map/ppermute | solution.py:46
  13.2 3.9 %collective-permute-start.7 = (s32[1,16]{1,0:T(1,128)S(1)}, s32[1,16]{1,0:T(1,128)S(1)}, u32[]{:S(2)}, u32[]{:S(2)}) collective-permute-start(s32[1,16]{1,0:T(1,128)S(1)} %bitcast.19), channel_id=1, source_target_pairs={{0,12},{1,13},{2,14},{3,15},{4,8},{5,9},{6,10},{7,11},{8,4},{9,5},... | collective-permute-start | bytes 200 | tf_op jit(solution)/shard_map/ppermute | solution.py:46
  17.2 1.5 %collective-permute-done.7 = s32[1,16]{1,0:T(1,128)S(1)} collective-permute-done((s32[1,16]{1,0:T(1,128)S(1)}, s32[1,16]{1,0:T(1,128)S(1)}, u32[]{:S(2)}, u32[]{:S(2)}) %collective-permute-start.7) | collective-permute-done | bytes 96 | tf_op jit(solution)/shard_map/ppermute | solution.py:46
  18.7 0.1 pad_add_fusion.2.refs_0_
  18.8 1.7 %collective-permute-start.8 = (s32[1,64]{1,0:T(1,128)S(1)}, s32[1,64]{1,0:T(1,128)S(1)}, u32[]{:S(2)}, u32[]{:S(2)}) collective-permute-start(s32[1,64]{1,0:T(1,128)S(1)} %pad_add_fusion.2.refs_0_), channel_id=1, source_target_pairs={{0,2},{1,3},{2,0},{3,1},{4,6},{5,7},{6,4},{7,5},{8,10},{9,11},{10,... | collective-permute-start | bytes 776 | tf_op jit(solution)/shard_map/ppermute | solution.py:46
  20.5 0.0 collective-permute-done.9.refs_0_
  20.5 0.2 stage.3.refs_3_
  20.7 1.7 %collective-permute-done.8.refs_1_ = s32[1,64]{1,0:T(1,128)S(1)} collective-permute-done((s32[1,64]{1,0:T(1,128)S(1)}, s32[1,64]{1,0:T(1,128)S(1)}, u32[]{:S(2)}, u32[]{:S(2)}) %collective-permute-start.8) | collective-permute-done | bytes 288 | tf_op jit(solution)/shard_map/ppermute | solution.py:46
  22.4 0.0 copy-done.12
  22.4 1.6 %lookup.2 = (bf16[32,1024]{1,0:T(8,128)(2,1)S(1)}, s32[1]{0:T(128)}) custom-call(s32[2]{0:T(128)S(1)} %pad_add_fusion.1.place_ref, s32[1,64]{1,0:T(1,128)S(1)} %pad_add_fusion.2.refs_0_, s32[1,64]{1,0:T(1,128)S(1)} %collective-permute-done.8.refs_1_, bf16[1024,1024]{1,0:T(8,128)(2,1)S(1)} %get-tuple-element.61.refs_2_, bf16[1024,1024]{1,0:T(8,128)(2,1)S(1)} %stage.3.refs_3_), custom_call_target="tpu_custom_call" | custom-call | tf_op jit(solution)/shard_map/lookup/pallas_call | solution.py:155
  24.0 0.1 collective-permute-start.10
  24.0 4.4 %collective-permute-start.11 = (bf16[32,1024]{1,0:T(8,128)(2,1)S(1)}, bf16[32,1024]{1,0:T(8,128)(2,1)S(1)}, u32[]{:S(2)}, u32[]{:S(2)}) collective-permute-start(bf16[32,1024]{1,0:T(8,128)(2,1)S(1)} %get-tuple-element.63.refs_0_), channel_id=1, source_target_pairs={{0,8},{1,9},{2,10},{3,11},{4,12},{5,13},{6,14},{7,15},{8,0},{9,1},... | collective-permute-start | bytes 196616 | tf_op jit(solution)/shard_map/ppermute | solution.py:46
  28.4 0.0 collective-permute-done.15.refs_1_
  28.4 0.0 collective-permute-start.12
  28.4 2.2 %stage.5 = (bf16[1024,1024]{1,0:T(8,128)(2,1)S(1)}, bf16[1024,1024]{1,0:T(8,128)(2,1)S(1)}) custom-call(bf16[1024,1024]{1,0:T(8,128)(2,1)} %refs_0_.3, bf16[1024,1024]{1,0:T(8,128)(2,1)} %refs_1_.1), custom_call_target="tpu_custom_call" | custom-call | tf_op jit(solution)/shard_map/stage/pallas_call | solution.py:407
  30.7 0.0 copy-start.2
  30.7 1.3 %copy-done.2 = bf16[1024,1024]{1,0:T(8,128)(2,1)} copy-done((bf16[1024,1024]{1,0:T(8,128)(2,1)}, bf16[1024,1024]{1,0:T(8,128)(2,1)S(1)}, u32[]{:S(2)}) %copy-start.2) | copy-done | bytes 2097176
  32.0 0.9 %plan.2.pick_ref = bf16[128,256]{1,0:T(8,128)(2,1)S(1)} custom-call(s32[2]{0:T(128)S(1)} %pad_add_fusion.1.place_ref, s32[1,64]{1,0:T(1,128)S(1)} %pad_add_fusion.2.refs_0_, s32[1,64]{1,0:T(1,128)S(1)} %collective-permute-done.8.refs_1_), custom_call_target="tpu_custom_call" | custom-call | tf_op jit(solution)/shard_map/plan/pallas_call | solution.py:191
  32.9 0.0 collective-permute-done.16.refs_2_
  32.9 2.9 %stage.4 = (bf16[1024,1024]{1,0:T(8,128)(2,1)S(1)}, bf16[1024,1024]{1,0:T(8,128)(2,1)S(1)}, bf16[1024,1024]{1,0:T(8,128)(2,1)S(1)}) custom-call(bf16[1024,2048]{1,0:T(8,128)(2,1)} %proj_ref.1, bf16[1024,1024]{1,0:T(8,128)(2,1)} %collective-permute-done.15.refs_1_, bf16[1024,1024]{1,0:T(8,128)(2,1)} %collective-permute-done.16.refs_2_), custom_call_target="tpu_custom_call" | custom-call | tf_op jit(solution)/shard_map/stage/pallas_call | solution.py:407
  35.8 0.0 copy-start.4
  35.8 1.4 %copy-done.4 = bf16[1024,1024]{1,0:T(8,128)(2,1)} copy-done((bf16[1024,1024]{1,0:T(8,128)(2,1)}, bf16[1024,1024]{1,0:T(8,128)(2,1)S(1)}, u32[]{:S(2)}) %copy-start.4) | copy-done | bytes 2097176
  37.2 1.4 %copy-done.6 = bf16[1024,1024]{1,0:T(8,128)(2,1)} copy-done((bf16[1024,1024]{1,0:T(8,128)(2,1)}, bf16[1024,1024]{1,0:T(8,128)(2,1)S(1)}, u32[]{:S(2)}) %copy-start.6) | copy-done | bytes 2097176
  38.6 1.3 %copy-done.8 = bf16[1024,1024]{1,0:T(8,128)(2,1)} copy-done((bf16[1024,1024]{1,0:T(8,128)(2,1)}, bf16[1024,1024]{1,0:T(8,128)(2,1)S(1)}, u32[]{:S(2)}) %copy-start.8) | copy-done | bytes 2097176
  39.9 1.7 %collective-permute-start.13 = (bf16[32,1024]{1,0:T(8,128)(2,1)S(1)}, bf16[32,1024]{1,0:T(8,128)(2,1)S(1)}, u32[]{:S(2)}, u32[]{:S(2)}) collective-permute-start(bf16[32,1024]{1,0:T(8,128)(2,1)S(1)} %get-tuple-element.63.refs_0_), channel_id=1, source_target_pairs={{0,2},{1,3},{2,0},{3,1},{4,6},{5,7},{6,4},{7,5},{8,10},{9,11},{10,... | collective-permute-start | bytes 196616 | tf_op jit(solution)/shard_map/ppermute | solution.py:46
  41.7 0.0 collective-permute-done.10.refs_0_
  41.7 0.0 collective-permute-done.11.refs_1_
  41.7 0.0 collective-permute-done.12.refs_2_
  41.7 0.4 collective-permute-start.14
  42.1 0.0 collective-permute-done.17.refs_12_
  42.1 0.7 broadcast_in_dim.17
  42.8 0.6 while.10
  43.4 0.8 collective-permute-done.13.refs_2_
  44.2 3.2 %collective-permute-done.14.refs_3_ = bf16[96,1024]{1,0:T(8,128)(2,1)S(1)} collective-permute-done((bf16[96,1024]{1,0:T(8,128)(2,1)S(1)}, bf16[96,1024]{1,0:T(8,128)(2,1)S(1)}, u32[]{:S(2)}, u32[]{:S(2)}) %collective-permute-start.14) | collective-permute-done | bytes 196640 | tf_op jit(solution)/shard_map/ppermute | solution.py:46
  47.4 0.0 copy-done.10
  47.4 1.6 %copy-done.3 = bf16[1024,1024]{1,0:T(8,128)(2,1)S(1)} copy-done((bf16[1024,1024]{1,0:T(8,128)(2,1)S(1)}, bf16[1024,1024]{1,0:T(8,128)(2,1)}, u32[]{:S(2)}) %copy-start.3) | copy-done | bytes 2097176
  49.0 1.6 %copy-done.5 = bf16[1024,1024]{1,0:T(8,128)(2,1)S(1)} copy-done((bf16[1024,1024]{1,0:T(8,128)(2,1)S(1)}, bf16[1024,1024]{1,0:T(8,128)(2,1)}, u32[]{:S(2)}) %copy-start.5) | copy-done | bytes 2097176
  50.6 1.6 %copy-done.7 = bf16[1024,1024]{1,0:T(8,128)(2,1)S(1)} copy-done((bf16[1024,1024]{1,0:T(8,128)(2,1)S(1)}, bf16[1024,1024]{1,0:T(8,128)(2,1)}, u32[]{:S(2)}) %copy-start.7) | copy-done | bytes 2097176
  52.2 1.6 %copy-done.9 = bf16[1024,1024]{1,0:T(8,128)(2,1)S(1)} copy-done((bf16[1024,1024]{1,0:T(8,128)(2,1)S(1)}, bf16[1024,1024]{1,0:T(8,128)(2,1)}, u32[]{:S(2)}) %copy-start.9) | copy-done | bytes 2097176
  53.8 5.7 %attend.1 = (bf16[16,1024]{1,0:T(8,128)(2,1)S(1)}, f32[64,1024]{1,0:T(8,128)S(1)}, bf16[64,1024]{1,0:T(8,128)(2,1)S(1)}) custom-call(s32[1]{0:T(128)} %get-tuple-element.149.rounds_ref, bf16[128,256]{1,0:T(8,128)(2,1)S(1)} %plan.2.pick_ref, bf16[32,1024]{1,0:T(8,128)(2,1)S(1)} %get-tuple-element.63.refs_0_, bf16[96,1024]{1,0:T(8,128)(2,1)S(1)} %join.2.refs_1_, ...), custom_call_target="tpu_custom_call" | custom-call | flops 2147483648 | bytes 8388608 | tf_op jit(solution)/shard_map/attend/pallas_call | solution.py:367
  59.5 0.7 collective-permute-start.18
  60.2 4.4 %collective-permute-done.18 = bf16[64,1024]{1,0:T(8,128)(2,1)S(1)} collective-permute-done((bf16[64,1024]{1,0:T(8,128)(2,1)S(1)}, bf16[64,1024]{1,0:T(8,128)(2,1)S(1)}, u32[]{:S(2)}, u32[]{:S(2)}) %collective-permute-start.18) | collective-permute-done | bytes 131104 | tf_op jit(solution)/shard_map/ppermute | solution.py:46
  64.6 0.4 collective-permute-start.19
  65.0 3.8 %collective-permute-start.20 = (bf16[16,1024]{1,0:T(8,128)(2,1)S(1)}, bf16[16,1024]{1,0:T(8,128)(2,1)S(1)}, u32[]{:S(2)}, u32[]{:S(2)}) collective-permute-start(bf16[16,1024]{1,0:T(8,128)(2,1)S(1)} %get-tuple-element.93), channel_id=1, source_target_pairs={{0,8},{1,9},{2,10},{3,11},{4,12},{5,13},{6,14},{7,15},{8,0},{9,1},... | collective-permute-start | bytes 98312 | tf_op jit(solution)/shard_map/ppermute | solution.py:46
  68.9 0.2 collective-permute-start.21
  69.1 0.0 copy-done
  69.1 0.5 gates.1.refs_4_
  69.6 0.0 collective-permute-done.19.refs_0_
  69.6 1.5 %collective-permute-done.20.refs_1_ = bf16[16,1024]{1,0:T(8,128)(2,1)S(1)} collective-permute-done((bf16[16,1024]{1,0:T(8,128)(2,1)S(1)}, bf16[16,1024]{1,0:T(8,128)(2,1)S(1)}, u32[]{:S(2)}, u32[]{:S(2)}) %collective-permute-start.20) | collective-permute-done | bytes 32800 | tf_op jit(solution)/shard_map/ppermute | solution.py:46
  71.1 3.5 %collective-permute-done.21.refs_2_ = bf16[16,1024]{1,0:T(8,128)(2,1)S(1)} collective-permute-done((bf16[16,1024]{1,0:T(8,128)(2,1)S(1)}, bf16[16,1024]{1,0:T(8,128)(2,1)S(1)}, u32[]{:S(2)}, u32[]{:S(2)}) %collective-permute-start.21) | collective-permute-done | bytes 32800 | tf_op jit(solution)/shard_map/ppermute | solution.py:46
  74.6 0.0 copy-done.1
  74.6 0.0 copy-done.11
  74.6 1.2 %finish.1 = bf16[16,1024]{1,0:T(8,128)(2,1)} custom-call(f32[16,1024]{1,0:T(8,128)S(1)} %slice.19.own_ref, bf16[16,1024]{1,0:T(8,128)(2,1)S(1)} %collective-permute-done.19.refs_0_, bf16[16,1024]{1,0:T(8,128)(2,1)S(1)} %collective-permute-done.20.refs_1_, bf16[16,1024]{1,0:T(8,128)(2,1)S(1)} %collective-permute-done.21.refs_2_, ...), custom_call_target="tpu_custom_call" | custom-call | tf_op jit(solution)/shard_map/finish/pallas_call | solution.py:450
  (15 shorter events, 0.1 us)
Async XLA Ops:
  0.0 4.1 %copy-start.13 = (s32[16]{0:T(128)S(1)}, s32[16]{0:T(128)}, u32[]{:S(2)}) copy-start(s32[16]{0:T(128)} %param.14) | copy-start | bytes 196
  0.0 20.5 %collective-permute-start.9 = (bf16[1024,1024]{1,0:T(8,128)(2,1)}, bf16[1024,1024]{1,0:T(8,128)(2,1)S(1)}, u32[]{:S(2)}, u32[]{:S(2)}) collective-permute-start(bf16[1024,1024]{1,0:T(8,128)(2,1)} %table_hbm.1), channel_id=1, source_target_pairs={{0,1},{1,0},{2,3},{3,2},{4,5},{5,4},{6,7},{7,6},{8,9},{9,8},{10,11... | collective-permute-start | bytes 6291464 | tf_op jit(solution)/shard_map/ppermute | solution.py:46
  0.5 27.9 %collective-permute-start.15 = (bf16[1024,1024]{1,0:T(8,128)(2,1)}, bf16[1024,1024]{1,0:T(8,128)(2,1)}, u32[]{:S(2)}, u32[]{:S(2)}) collective-permute-start(bf16[1024,1024]{1,0:T(8,128)(2,1)} %refs_0_.3), channel_id=1, source_target_pairs={{0,1},{1,0},{2,3},{3,2},{4,5},{5,4},{6,7},{7,6},{8,9},{9,8},{10,11... | collective-permute-start | bytes 6291464 | tf_op jit(solution)/shard_map/ppermute | solution.py:46
  0.6 32.3 %collective-permute-start.16 = (bf16[1024,1024]{1,0:T(8,128)(2,1)}, bf16[1024,1024]{1,0:T(8,128)(2,1)}, u32[]{:S(2)}, u32[]{:S(2)}) collective-permute-start(bf16[1024,1024]{1,0:T(8,128)(2,1)} %refs_1_.1), channel_id=1, source_target_pairs={{0,1},{1,0},{2,3},{3,2},{4,5},{5,4},{6,7},{7,6},{8,9},{9,8},{10,11... | collective-permute-start | bytes 6291464 | tf_op jit(solution)/shard_map/ppermute | solution.py:46
  4.0 38.1 %collective-permute-start.17 = (bf16[1024,128]{1,0:T(8,128)(2,1)S(1)}, bf16[1024,128]{1,0:T(8,128)(2,1)S(1)}, u32[]{:S(2)}, u32[]{:S(2)}) collective-permute-start(bf16[1024,128]{1,0:T(8,128)(2,1)S(1)} %get-tuple-element.70.refs_11_), channel_id=1, source_target_pairs={{0,1},{1,0},{2,3},{3,2},{4,5},{5,4},{6,7},{7,6},{8,9},{9,8},{10,11... | collective-permute-start | bytes 786440 | tf_op jit(solution)/shard_map/ppermute | solution.py:46
  4.1 4.6 %collective-permute-start.5 = (s32[1,16]{1,0:T(1,128)S(1)}, s32[1,16]{1,0:T(1,128)S(1)}, u32[]{:S(2)}, u32[]{:S(2)}) collective-permute-start(s32[1,16]{1,0:T(1,128)S(1)} %bitcast.17), channel_id=1, source_target_pairs={{0,4},{1,5},{2,6},{3,7},{4,0},{5,1},{6,2},{7,3},{8,12},{9,13},{10,... | collective-permute-start | bytes 200 | tf_op jit(solution)/shard_map/ppermute | solution.py:46
  8.6 4.6 %collective-permute-start.6 = (s32[1,16]{1,0:T(1,128)S(1)}, s32[1,16]{1,0:T(1,128)S(1)}, u32[]{:S(2)}, u32[]{:S(2)}) collective-permute-start(s32[1,16]{1,0:T(1,128)S(1)} %bitcast.18), channel_id=1, source_target_pairs={{0,8},{1,9},{2,10},{3,11},{4,12},{5,13},{6,14},{7,15},{8,0},{9,1},... | collective-permute-start | bytes 200 | tf_op jit(solution)/shard_map/ppermute | solution.py:46
  13.2 5.5 %collective-permute-start.7 = (s32[1,16]{1,0:T(1,128)S(1)}, s32[1,16]{1,0:T(1,128)S(1)}, u32[]{:S(2)}, u32[]{:S(2)}) collective-permute-start(s32[1,16]{1,0:T(1,128)S(1)} %bitcast.19), channel_id=1, source_target_pairs={{0,12},{1,13},{2,14},{3,15},{4,8},{5,9},{6,10},{7,11},{8,4},{9,5},... | collective-permute-start | bytes 200 | tf_op jit(solution)/shard_map/ppermute | solution.py:46
  18.8 3.6 %collective-permute-start.8 = (s32[1,64]{1,0:T(1,128)S(1)}, s32[1,64]{1,0:T(1,128)S(1)}, u32[]{:S(2)}, u32[]{:S(2)}) collective-permute-start(s32[1,64]{1,0:T(1,128)S(1)} %pad_add_fusion.2.refs_0_), channel_id=1, source_target_pairs={{0,2},{1,3},{2,0},{3,1},{4,6},{5,7},{6,4},{7,5},{8,10},{9,11},{10,... | collective-permute-start | bytes 776 | tf_op jit(solution)/shard_map/ppermute | solution.py:46
  20.5 1.8 %copy-start.12 = (bf16[1024,1024]{1,0:T(8,128)(2,1)}, bf16[1024,1024]{1,0:T(8,128)(2,1)S(1)}, u32[]{:S(2)}) copy-start(bf16[1024,1024]{1,0:T(8,128)(2,1)S(1)} %collective-permute-done.9.refs_0_) | copy-start | bytes 6291460
  24.0 17.7 %collective-permute-start.10 = (bf16[32,1024]{1,0:T(8,128)(2,1)S(1)}, bf16[32,1024]{1,0:T(8,128)(2,1)S(1)}, u32[]{:S(2)}, u32[]{:S(2)}) collective-permute-start(bf16[32,1024]{1,0:T(8,128)(2,1)S(1)} %get-tuple-element.63.refs_0_), channel_id=1, source_target_pairs={{0,4},{1,5},{2,6},{3,7},{4,0},{5,1},{6,2},{7,3},{8,12},{9,13},{10,... | collective-permute-start | bytes 196616 | tf_op jit(solution)/shard_map/ppermute | solution.py:46
  24.0 17.6 %collective-permute-start.11 = (bf16[32,1024]{1,0:T(8,128)(2,1)S(1)}, bf16[32,1024]{1,0:T(8,128)(2,1)S(1)}, u32[]{:S(2)}, u32[]{:S(2)}) collective-permute-start(bf16[32,1024]{1,0:T(8,128)(2,1)S(1)} %get-tuple-element.63.refs_0_), channel_id=1, source_target_pairs={{0,8},{1,9},{2,10},{3,11},{4,12},{5,13},{6,14},{7,15},{8,0},{9,1},... | collective-permute-start | bytes 196616 | tf_op jit(solution)/shard_map/ppermute | solution.py:46
  28.4 13.3 %collective-permute-start.12 = (bf16[32,1024]{1,0:T(8,128)(2,1)S(1)}, bf16[32,1024]{1,0:T(8,128)(2,1)S(1)}, u32[]{:S(2)}, u32[]{:S(2)}) collective-permute-start(bf16[32,1024]{1,0:T(8,128)(2,1)S(1)} %get-tuple-element.63.refs_0_), channel_id=1, source_target_pairs={{0,12},{1,13},{2,14},{3,15},{4,8},{5,9},{6,10},{7,11},{8,4},{9,5},... | collective-permute-start | bytes 196616 | tf_op jit(solution)/shard_map/ppermute | solution.py:46
  30.7 1.4 %copy-start.2 = (bf16[1024,1024]{1,0:T(8,128)(2,1)}, bf16[1024,1024]{1,0:T(8,128)(2,1)S(1)}, u32[]{:S(2)}) copy-start(bf16[1024,1024]{1,0:T(8,128)(2,1)S(1)} %get-tuple-element.68.refs_9_) | copy-start | bytes 6291460
  35.8 1.4 %copy-start.4 = (bf16[1024,1024]{1,0:T(8,128)(2,1)}, bf16[1024,1024]{1,0:T(8,128)(2,1)S(1)}, u32[]{:S(2)}) copy-start(bf16[1024,1024]{1,0:T(8,128)(2,1)S(1)} %get-tuple-element.65.refs_6_) | copy-start | bytes 6291460
  37.2 1.4 %copy-start.6 = (bf16[1024,1024]{1,0:T(8,128)(2,1)}, bf16[1024,1024]{1,0:T(8,128)(2,1)S(1)}, u32[]{:S(2)}) copy-start(bf16[1024,1024]{1,0:T(8,128)(2,1)S(1)} %get-tuple-element.67.refs_8_) | copy-start | bytes 6291460
  38.6 1.3 %copy-start.8 = (bf16[1024,1024]{1,0:T(8,128)(2,1)}, bf16[1024,1024]{1,0:T(8,128)(2,1)S(1)}, u32[]{:S(2)}) copy-start(bf16[1024,1024]{1,0:T(8,128)(2,1)S(1)} %get-tuple-element.69.refs_10_) | copy-start | bytes 6291460
  39.9 4.3 %collective-permute-start.13 = (bf16[32,1024]{1,0:T(8,128)(2,1)S(1)}, bf16[32,1024]{1,0:T(8,128)(2,1)S(1)}, u32[]{:S(2)}, u32[]{:S(2)}) collective-permute-start(bf16[32,1024]{1,0:T(8,128)(2,1)S(1)} %get-tuple-element.63.refs_0_), channel_id=1, source_target_pairs={{0,2},{1,3},{2,0},{3,1},{4,6},{5,7},{6,4},{7,5},{8,10},{9,11},{10,... | collective-permute-start | bytes 196616 | tf_op jit(solution)/shard_map/ppermute | solution.py:46
  41.7 5.7 %collective-permute-start.14 = (bf16[96,1024]{1,0:T(8,128)(2,1)S(1)}, bf16[96,1024]{1,0:T(8,128)(2,1)S(1)}, u32[]{:S(2)}, u32[]{:S(2)}) collective-permute-start(bf16[96,1024]{1,0:T(8,128)(2,1)S(1)} %join.2.refs_1_), channel_id=1, source_target_pairs={{0,2},{1,3},{2,0},{3,1},{4,6},{5,7},{6,4},{7,5},{8,10},{9,11},{10,... | collective-permute-start | bytes 589832 | tf_op jit(solution)/shard_map/ppermute | solution.py:46
  42.8 4.6 %copy-start.10 = (f32[1024]{0:T(1024)S(1)}, f32[1024]{0:T(1024)}, u32[]{:S(2)}) copy-start(f32[1024]{0:T(1024)} %param.20) | copy-start | bytes 12292
  47.4 1.6 %copy-start.3 = (bf16[1024,1024]{1,0:T(8,128)(2,1)S(1)}, bf16[1024,1024]{1,0:T(8,128)(2,1)}, u32[]{:S(2)}) copy-start(bf16[1024,1024]{1,0:T(8,128)(2,1)} %copy-done.2) | copy-start | bytes 6291460
  49.0 1.6 %copy-start.5 = (bf16[1024,1024]{1,0:T(8,128)(2,1)S(1)}, bf16[1024,1024]{1,0:T(8,128)(2,1)}, u32[]{:S(2)}) copy-start(bf16[1024,1024]{1,0:T(8,128)(2,1)} %copy-done.4) | copy-start | bytes 6291460
  50.6 1.6 %copy-start.7 = (bf16[1024,1024]{1,0:T(8,128)(2,1)S(1)}, bf16[1024,1024]{1,0:T(8,128)(2,1)}, u32[]{:S(2)}) copy-start(bf16[1024,1024]{1,0:T(8,128)(2,1)} %copy-done.6) | copy-start | bytes 6291460
  52.2 1.6 %copy-start.9 = (bf16[1024,1024]{1,0:T(8,128)(2,1)S(1)}, bf16[1024,1024]{1,0:T(8,128)(2,1)}, u32[]{:S(2)}) copy-start(bf16[1024,1024]{1,0:T(8,128)(2,1)} %copy-done.8) | copy-start | bytes 6291460
  53.8 15.3 %copy-start = (bf16[1024,2048]{1,0:T(8,128)(2,1)S(1)}, bf16[1024,2048]{1,0:T(8,128)(2,1)}, u32[]{:S(2)}) copy-start(bf16[1024,2048]{1,0:T(8,128)(2,1)} %proj_ref.1) | copy-start | bytes 12582916
  59.5 5.0 %collective-permute-start.18 = (bf16[64,1024]{1,0:T(8,128)(2,1)S(1)}, bf16[64,1024]{1,0:T(8,128)(2,1)S(1)}, u32[]{:S(2)}, u32[]{:S(2)}) collective-permute-start(bf16[64,1024]{1,0:T(8,128)(2,1)S(1)} %get-tuple-element.72), channel_id=1, source_target_pairs={{0,2},{1,3},{2,0},{3,1},{4,6},{5,7},{6,4},{7,5},{8,10},{9,11},{10,... | collective-permute-start | bytes 393224 | tf_op jit(solution)/shard_map/ppermute | solution.py:46
  64.6 5.0 %collective-permute-start.19 = (bf16[16,1024]{1,0:T(8,128)(2,1)S(1)}, bf16[16,1024]{1,0:T(8,128)(2,1)S(1)}, u32[]{:S(2)}, u32[]{:S(2)}) collective-permute-start(bf16[16,1024]{1,0:T(8,128)(2,1)S(1)} %get-tuple-element.94), channel_id=1, source_target_pairs={{0,4},{1,5},{2,6},{3,7},{4,0},{5,1},{6,2},{7,3},{8,12},{9,13},{10,... | collective-permute-start | bytes 98312 | tf_op jit(solution)/shard_map/ppermute | solution.py:46
  65.0 6.1 %collective-permute-start.20 = (bf16[16,1024]{1,0:T(8,128)(2,1)S(1)}, bf16[16,1024]{1,0:T(8,128)(2,1)S(1)}, u32[]{:S(2)}, u32[]{:S(2)}) collective-permute-start(bf16[16,1024]{1,0:T(8,128)(2,1)S(1)} %get-tuple-element.93), channel_id=1, source_target_pairs={{0,8},{1,9},{2,10},{3,11},{4,12},{5,13},{6,14},{7,15},{8,0},{9,1},... | collective-permute-start | bytes 98312 | tf_op jit(solution)/shard_map/ppermute | solution.py:46
  68.9 5.7 %collective-permute-start.21 = (bf16[16,1024]{1,0:T(8,128)(2,1)S(1)}, bf16[16,1024]{1,0:T(8,128)(2,1)S(1)}, u32[]{:S(2)}, u32[]{:S(2)}) collective-permute-start(bf16[16,1024]{1,0:T(8,128)(2,1)S(1)} %get-tuple-element.92), channel_id=1, source_target_pairs={{0,12},{1,13},{2,14},{3,15},{4,8},{5,9},{6,10},{7,11},{8,4},{9,5},... | collective-permute-start | bytes 98312 | tf_op jit(solution)/shard_map/ppermute | solution.py:46
  69.1 5.5 %copy-start.1 = (bf16[1024,1024]{1,0:T(8,128)(2,1)S(1)}, bf16[1024,1024]{1,0:T(8,128)(2,1)}, u32[]{:S(2)}) copy-start(bf16[1024,1024]{1,0:T(8,128)(2,1)} %refs_6_.1) | copy-start | bytes 6291460
  69.1 5.5 %copy-start.11 = (f32[1024]{0:T(1024)S(1)}, f32[1024]{0:T(1024)}, u32[]{:S(2)}) copy-start(f32[1024]{0:T(1024)} %param.24) | copy-start | bytes 12292
